TPU v7x, 32 devices: a whole 2x2x4 slice. The times are simulated.
32 devices in a mesh: gx: 8 (over z, x), gy: 2 (over core), gz: 2 (over y).
Axes of the slice: x: 2, y: 2, z: 4, core: 2. Of those that a mesh axis runs over, the one named last changes fastest.
Arguments:
- feats: bfloat16 [8, 2, 2, 128, 256], P('gx', 'gy', 'gz'), may hold values from -6 to 6
- positions: float32 [8, 2, 2, 3, 128], P('gx', 'gy', 'gz'), may hold values from 0 to 1
- species: int32 [8, 2, 2, 128], P('gx', 'gy', 'gz'), may hold values from 0 to 5
- cell_counts: int32 [8, 2, 2], P('gx', 'gy', 'gz'), may hold values from 16 to 128, as said below
- pair_list: int32 [8, 2, 2, 27], P('gx', 'gy', 'gz'), may hold values 0 or 1
- w_env: bfloat16 [256, 64], replicated, may hold values from -0.375 to 0.375
- radial: float32 [4, 64], replicated, may hold values from -3 to 3
- pair_scale: float32 [6, 6], replicated, may hold values from 0.5 to 2
- w_hidden: bfloat16 [256, 256], replicated, may hold values from -0.375 to 0.375
- w_zero: bfloat16 [64, 256], replicated, may hold values from -0.75 to 0.75
- w_one: bfloat16 [64, 256], replicated, may hold values from -0.25 to 0.25
- w_out: float32 [256], replicated, may hold values from -0.375 to 0.375
Outputs:
- atom_energy: float32 [8, 2, 2, 128], P('gx', 'gy', 'gz')
- forces: float32 [8, 2, 2, 3, 128], P('gx', 'gy', 'gz')
- feat_grad: bfloat16 [8, 2, 2, 128, 256], P('gx', 'gy', 'gz')
Inputs may be any that keep to these rules, and one draw needn't show every extreme that they name: `cell_counts`: slots at or beyond a cell's count are empty and carry no atom.
All inputs are finite; a program needn't handle non-finite values. No bound on the sum of `pair_list` on one device may be relied on, other than what follows from the above.
Results may differ from a plain program's by a relative error of at most 0.0066.
Values may be sent and summed in bfloat16 or wider, within the bound.
No kernel may reach another device: no remote copies, remote signals or barrier semaphores. Data moves between devices by JAX's collectives and lax.ppermute only.
A program may use at most 64 MiB of HBM per device.

v0:
```python
import jax
import jax.numpy as jnp
from jax import lax
from jax.sharding import PartitionSpec as P

D = 256
CHANNELS = 64
NBASIS = 4
NSPEC = 6
SLOTS = 128


CUTOFF = 0.55


def passed_along(value, axis, steps):
    count = lax.axis_size(axis)
    pairs = [(source, (source + steps) % count) for source in range(count)]
    return lax.ppermute(value, axis, pairs)


def extended(block, sides, width):
    for axis, dim in sides:
        count = lax.axis_size(axis)
        forward = [(i, i + 1) for i in range(count - 1)]
        forward.append((count - 1, 0))
        backward = [(target, source) for source, target in forward]
        low = lax.ppermute(
            lax.slice_in_dim(block, block.shape[dim] - width, None, axis=dim), axis, forward
        )
        high = lax.ppermute(lax.slice_in_dim(block, 0, width, axis=dim), axis, backward)
        block = jnp.concatenate([low, block, high], axis=dim)
    return block


def pair_terms(pos_i, pos_j, offset_index):
    offset = jnp.stack(
        [offset_index // 9 - 1, offset_index // 3 % 3 - 1, offset_index % 3 - 1]
    ).astype(jnp.float32)
    relative = offset[:, None, None] + pos_j[:, None, :] - pos_i[:, :, None]
    scaled = jnp.sum(relative * relative, axis=0) / (CUTOFF * CUTOFF)
    inside = jnp.maximum(1.0 - scaled, 0.0)
    envelope = inside * inside
    centers = (jnp.arange(NBASIS, dtype=jnp.float32) + 0.5) / NBASIS
    spread = (scaled[None] - centers[:, None, None]) * NBASIS
    radial_basis = jnp.exp(-spread * spread)
    harmonic = jnp.concatenate([jnp.ones_like(scaled)[None], relative / CUTOFF], axis=0)
    return (relative, scaled, inside, envelope, spread, radial_basis, harmonic)


def build_tile(weight, envelope, radial_basis, harmonic):
    full = (weight * envelope)[None, None] * radial_basis[:, None] * harmonic[None, :]
    return full.astype(jnp.bfloat16).reshape(4 * NBASIS * SLOTS, SLOTS)


def pair_grad(tile_grad, terms, weight):
    relative, scaled, inside, envelope, spread, radial_basis, harmonic = terms
    through_basis = jnp.sum(tile_grad * harmonic[None], axis=1)
    value_part = jnp.sum(through_basis * radial_basis, axis=0)
    slope_part = jnp.sum(through_basis * radial_basis * spread, axis=0) * (-2.0 * NBASIS)
    vector_part = jnp.sum(tile_grad[:, 1:] * radial_basis[:, None], axis=0)
    grad_scaled = weight * (-2.0 * inside * value_part + envelope * slope_part)
    return (
        grad_scaled[None] * (2.0 / (CUTOFF * CUTOFF)) * relative
        + (weight * envelope)[None] * vector_part / CUTOFF
    )


def fold_back(packed):
    for shift_by in (1, -1):
        outer_layer = packed[-1] if shift_by == 1 else packed[0]
        arrived = passed_along(outer_layer.astype(jnp.bfloat16), "gx", shift_by).astype(
            outer_layer.dtype
        )
        target = 1 if shift_by == 1 else packed.shape[0] - 2
        packed = packed.at[target].add(arrived)
    packed = packed[1:-1]
    for shift_by in (1, -1):
        outer_layer = packed[:, -1] if shift_by == 1 else packed[:, 0]
        arrived = passed_along(outer_layer.astype(jnp.bfloat16), "gy", shift_by).astype(
            outer_layer.dtype
        )
        packed = packed.at[:, 1].add(arrived)
    packed = packed[:, 1:-1]
    for shift_by in (1, -1):
        outer_layer = packed[:, :, -1] if shift_by == 1 else packed[:, :, 0]
        arrived = passed_along(outer_layer.astype(jnp.bfloat16), "gz", shift_by).astype(
            outer_layer.dtype
        )
        packed = packed.at[:, :, 1].add(arrived)
    packed = packed[:, :, 1:-1]
    return packed.reshape(packed.shape[0], packed.shape[-1])


def local(
    feats,
    positions,
    species,
    cell_counts,
    pair_list,
    w_env,
    radial,
    pair_scale,
    w_hidden,
    w_zero,
    w_one,
    w_out,
):
    own_cells = feats.shape[0]
    quad_rows = 4 * NBASIS * SLOTS
    own_feat = feats.reshape(own_cells * SLOTS, D)
    own_pos = positions.reshape(own_cells, 3, SLOTS)
    slot_ids = jnp.arange(SLOTS, dtype=jnp.int32)
    occupied = (slot_ids[None, :] < cell_counts.reshape(own_cells, 1)).astype(jnp.float32)
    onehot = (
        species.reshape(own_cells, 1, SLOTS) == jnp.arange(NSPEC, dtype=jnp.int32)[None, :, None]
    ).astype(jnp.float32)
    species_coef = (
        jnp.einsum("st,ctj->csj", pair_scale, onehot, precision=lax.Precision.HIGHEST)
        * occupied[:, None, :]
    )
    geometry = jnp.concatenate([own_pos, species_coef], axis=1).reshape(
        own_cells, 1, 1, (3 + NSPEC) * SLOTS
    )
    geo_ext = extended(geometry, (("gx", 0), ("gy", 1), ("gz", 2)), 1).reshape(
        own_cells + 2, 3, 3, 3 + NSPEC, SLOTS
    )
    feat_ext = extended(
        feats.reshape(own_cells, 1, 1, SLOTS * D), (("gx", 0), ("gy", 1), ("gz", 2)), 1
    )
    chan_ext = jnp.dot(
        feat_ext.reshape((own_cells + 2) * 9 * SLOTS, D), w_env, preferred_element_type=jnp.float32
    ).astype(jnp.bfloat16)
    chan_ext = chan_ext.reshape(own_cells + 2, 3, 3, SLOTS, CHANNELS)
    tile_flags = pair_list.reshape(own_cells * 27)
    tile_order = jnp.arange(own_cells * 27, dtype=jnp.int32)
    live_tiles = own_cells * 27
    listed_all = tile_flags.astype(jnp.float32)

    def tile_setup(step_index):
        tile_index = tile_order[step_index]
        own_cell = tile_index // 27
        offset_index = tile_index % 27
        ext_x = own_cell + offset_index // 9
        ext_y = offset_index // 3 % 3
        ext_z = offset_index % 3
        neighbour_geo = geo_ext[ext_x, ext_y, ext_z]
        species_pair = jnp.dot(
            onehot[own_cell].T,
            neighbour_geo[3:],
            precision=lax.Precision.HIGHEST,
            preferred_element_type=jnp.float32,
        )
        self_tile = (offset_index == 13).astype(jnp.float32)
        not_self = 1.0 - self_tile * jnp.eye(SLOTS, dtype=jnp.float32)
        weight = species_pair * not_self * occupied[own_cell][:, None] * listed_all[tile_index]
        terms = pair_terms(own_pos[own_cell], neighbour_geo[:3], offset_index)
        pair_tile = build_tile(weight, terms[3], terms[5], terms[6])
        return (
            own_cell,
            (ext_x, ext_y, ext_z),
            chan_ext[ext_x, ext_y, ext_z],
            weight,
            terms,
            pair_tile,
        )

    def forward_tile(step_index, moments):
        own_cell, ext_place, neighbour_chans, weight, terms, pair_tile = tile_setup(step_index)
        return moments.at[own_cell].add(
            jnp.dot(pair_tile, neighbour_chans, preferred_element_type=jnp.float32)
        )

    moments = lax.fori_loop(
        0, live_tiles, forward_tile, jnp.zeros((own_cells, quad_rows, CHANNELS), jnp.float32)
    )
    vectors = jnp.einsum(
        "kc,akmic->amic",
        radial,
        moments.reshape(own_cells, NBASIS, 4, SLOTS, CHANNELS),
        precision=lax.Precision.HIGHEST,
    )
    scalar_zero = vectors[:, 0].reshape(own_cells * SLOTS, CHANNELS).astype(jnp.bfloat16)
    scalar_one = (
        jnp.sum(vectors[:, 1:] * vectors[:, 1:], axis=1)
        .reshape(own_cells * SLOTS, CHANNELS)
        .astype(jnp.bfloat16)
    )
    pre = jnp.dot(own_feat, w_hidden, preferred_element_type=jnp.float32)
    pre = pre + jnp.dot(scalar_zero, w_zero, preferred_element_type=jnp.float32)
    pre = pre + jnp.dot(scalar_one, w_one, preferred_element_type=jnp.float32)
    gate = jax.nn.sigmoid(pre)
    occupied_rows = occupied.reshape(own_cells * SLOTS, 1)
    atom_energy = occupied.reshape(own_cells * SLOTS) * jnp.dot(
        pre * gate, w_out, precision=lax.Precision.HIGHEST
    )
    pre_grad = (occupied_rows * w_out[None, :] * gate * (1.0 + pre * (1.0 - gate))).astype(
        jnp.bfloat16
    )
    direct_grad = jnp.dot(pre_grad, w_hidden.T, preferred_element_type=jnp.float32)
    zero_grad = jnp.dot(pre_grad, w_zero.T, preferred_element_type=jnp.float32).reshape(
        own_cells, SLOTS, CHANNELS
    )
    one_grad = jnp.dot(pre_grad, w_one.T, preferred_element_type=jnp.float32).reshape(
        own_cells, SLOTS, CHANNELS
    )
    vector_grad = jnp.concatenate(
        [zero_grad[:, None], 2.0 * vectors[:, 1:] * one_grad[:, None]], axis=1
    )
    moment_grad = (
        (radial[None, :, None, None, :] * vector_grad[:, None])
        .astype(jnp.bfloat16)
        .reshape(own_cells, quad_rows, CHANNELS)
    )

    def backward_tile(step_index, partial_sums):
        chan_grad, pos_grad = partial_sums
        own_cell, ext_place, neighbour_chans, weight, terms, pair_tile = tile_setup(step_index)
        cell_grad = moment_grad[own_cell]
        to_chans = lax.dot_general(
            pair_tile, cell_grad, (((0,), (0,)), ((), ())), preferred_element_type=jnp.float32
        )
        tile_grad = jnp.dot(
            cell_grad, neighbour_chans.T, preferred_element_type=jnp.float32
        ).reshape(NBASIS, 4, SLOTS, SLOTS)
        rel_grad = pair_grad(tile_grad, terms, weight)
        chan_grad = chan_grad.at[ext_place].add(to_chans)
        pos_grad = pos_grad.at[ext_place].add(jnp.sum(rel_grad, axis=1))
        pos_grad = pos_grad.at[own_cell + 1, 1, 1].add(-jnp.sum(rel_grad, axis=2))
        return (chan_grad, pos_grad)

    initial = (
        jnp.zeros((own_cells + 2, 3, 3, SLOTS, CHANNELS), jnp.float32),
        jnp.zeros((own_cells + 2, 3, 3, 3, SLOTS), jnp.float32),
    )
    chan_grad_ext, pos_grad_ext = lax.fori_loop(0, live_tiles, backward_tile, initial)
    pos_part = pos_grad_ext.reshape(own_cells + 2, 3, 3, 3 * SLOTS)
    feat_part = jnp.dot(
        chan_grad_ext.reshape((own_cells + 2) * 9 * SLOTS, CHANNELS),
        w_env.astype(jnp.float32).T,
        precision=lax.Precision.HIGHEST,
    )
    folded = fold_back(
        jnp.concatenate([feat_part.reshape(own_cells + 2, 3, 3, SLOTS * D), pos_part], axis=-1)
    )
    chan_total = folded[:, : SLOTS * D].reshape(own_cells * SLOTS, D)
    pos_total = folded[:, SLOTS * D :]
    feat_grad = (direct_grad + chan_total).astype(jnp.bfloat16)
    return (
        atom_energy.reshape(own_cells, 1, 1, SLOTS),
        (-pos_total).reshape(own_cells, 1, 1, 3, SLOTS),
        feat_grad.reshape(own_cells, 1, 1, SLOTS, D),
    )


def solution(mesh):
    in_specs = (
        P("gx", "gy", "gz", None, None),
        P("gx", "gy", "gz", None, None),
        P("gx", "gy", "gz", None),
        P("gx", "gy", "gz"),
        P("gx", "gy", "gz", None),
        P(),
        P(),
        P(),
        P(),
        P(),
        P(),
        P(),
    )
    out_specs = (
        P("gx", "gy", "gz", None),
        P("gx", "gy", "gz", None, None),
        P("gx", "gy", "gz", None, None),
    )
    return jax.shard_map(local, mesh=mesh, in_specs=in_specs, out_specs=out_specs, check_vma=False)
```

profile of v0, /device:TPU:0, one launch (start us, length us, event | category | flops | bytes accessed | tf_op | source)
XLA Modules:
  0.0 1172.5 jit_solution(7135989356032380869)
XLA Ops:
  2.9 3.0 collective-permute-start
  5.9 3.1 collective-permute-start.1
  9.9 2.0 collective-permute-start.7
  12.0 7.6 collective-permute-done.6
  22.4 2.2 pad_maximum_fusion.1
  29.4 33.2 %collective-permute-done.5 = f32[3,3,1,1152]{3,2,1,0:T(1,128)S(1)} collective-permute-done((f32[3,3,1,1152]{3,2,1,0:T(1,128)S(1)}, f32[3,3,1,1152]{3,2,1,0:T(1,128)S(1)}, u32[]{:S(2)}, u32[]{:S(2)}) %collective-permute-start.5) | collective-permute-done | bytes 41504 | tf_op jit(solution)/shard_map/ppermute | solution.py:31
  63.9 3.3 pad_maximum_fusion
  67.3 1.8 copy.80
  69.1 3.3 reshape.1060
  72.4 2.2 convolution_convert_fusion
  75.0 318.0 %while.47 = (s32[]{:T(128)}, f32[1,2048,64]{1,2,0:T(8,128)S(1)}, s32[27]{0:T(128)S(1)}, f32[3,3,3,9,128]{4,3,2,1,0:T(8,128)}, f32[27]{0:T(128)}, /*index=5*/f32[...) while((s32[]{:T(128)}, f32[1,2048,64]{1,2,0:T(8,128)S(1)}, ...), condition=%wide.region_3.4_spmd.clone, body=%wide.region_0.3_spmd.clone.sunk | while | flops 36358368 | bytes 4436906 | solution.py:174
  398.2 708.2 %while.46 = (s32[]{:T(128)}, f32[3,3,3,128,64]{3,2,1,0,4:T(4,128)}, f32[3,3,3,3,128]{3,4,2,1,0:T(8,128)S(1)}, s32[27]{0:T(128)S(1)}, f32[3,3,3,9,128]{4,3,2,1,0:...) while((s32[]{:T(128)}, f32[3,3,3,128,64]{3,2,1,0,4:T(4,128)}, ...), condition=%wide.region_15.16_spmd.clone, body=%wide.region_5.15_spmd.clone.sunk | while | flops 71601512 | bytes 15402979 | solution.py:236
  409.8 2.3 broadcast_multiply_fusion.6
  436.1 2.2 broadcast_multiply_fusion.6
  462.3 2.3 broadcast_multiply_fusion.6
  488.5 2.3 broadcast_multiply_fusion.6
  514.8 2.3 broadcast_multiply_fusion.6
  541.0 2.2 broadcast_multiply_fusion.6
  567.2 2.3 broadcast_multiply_fusion.6
  579.7 1.7 scatter-add.39
  593.4 2.3 broadcast_multiply_fusion.6
  619.7 2.3 broadcast_multiply_fusion.6
  645.9 2.2 broadcast_multiply_fusion.6
  672.1 2.3 broadcast_multiply_fusion.6
  698.3 2.3 broadcast_multiply_fusion.6
  724.6 2.3 broadcast_multiply_fusion.6
  750.8 2.3 broadcast_multiply_fusion.6
  777.0 2.3 broadcast_multiply_fusion.6
  803.2 2.3 broadcast_multiply_fusion.6
  829.4 2.3 broadcast_multiply_fusion.6
  855.7 2.3 broadcast_multiply_fusion.6
  881.9 2.3 broadcast_multiply_fusion.6
  908.1 2.3 broadcast_multiply_fusion.6
  934.3 2.3 broadcast_multiply_fusion.6
  960.6 2.3 broadcast_multiply_fusion.6
  986.8 2.2 broadcast_multiply_fusion.6
  1013.0 2.3 broadcast_multiply_fusion.6
  1039.2 2.3 broadcast_multiply_fusion.6
  1065.4 2.2 broadcast_multiply_fusion.6
  1091.7 2.3 broadcast_multiply_fusion.6
  1108.2 3.4 fusion.74
  1111.6 6.1 reshape.1065
  1117.7 3.1 constant_dynamic-update-slice_fusion.8
  1122.3 4.7 collective-permute-start.13
  1127.0 28.6 %collective-permute-done.12 = bf16[3,3,33152]{2,1,0:T(4,128)(2,1)S(1)} collective-permute-done((bf16[3,3,33152]{2,1,0:T(4,128)(2,1)S(1)}, bf16[3,3,33152]{2,1,0:T(4,128)(2,1)S(1)}, u32[]{:S(2)}, u32[]{:S(2)}) %collective-permute-start.12) | collective-permute-done | bytes 596768 | tf_op jit(solution)/shard_map/ppermute | solution.py:19
  1155.6 2.9 collective-permute-done.13
  1164.8 3.6 collective-permute-done.16
  1168.4 2.0 collective-permute-done.17
  (2247 shorter events, 761.8 us)
Async XLA Ops:
  0.6 394.6 %copy-start = (bf16[256,256]{1,0:T(8,128)(2,1)S(1)}, bf16[256,256]{1,0:T(8,128)(2,1)}, u32[]{:S(2)}) copy-start(bf16[256,256]{1,0:T(8,128)(2,1)} %param.44) | copy-start | bytes 393220
  0.6 28.1 %copy-start.30 = (s32[1,1,1,27]{3,2,1,0:T(1,128)S(1)}, s32[1,1,1,27]{3,2,1,0:T(1,128)}, u32[]{:S(2)}) copy-start(s32[1,1,1,27]{3,2,1,0:T(1,128)} %param.40) | copy-start | bytes 328
  0.7 28.7 %copy-start.21 = (f32[4,64]{1,0:T(4,128)S(1)}, f32[4,64]{1,0:T(4,128)}, u32[]{:S(2)}) copy-start(f32[4,64]{1,0:T(4,128)} %param.42) | copy-start | bytes 3076
  2.9 9.1 collective-permute-start
  5.9 14.7 %collective-permute-start.1 = (f32[1,1,1,1152]{3,2,1,0:T(1,128)S(1)}, f32[1,1,1,1152]{3,2,1,0:T(1,128)S(1)}, u32[]{:S(2)}, u32[]{:S(2)}) collective-permute-start(f32[1,1,1,1152]{3,2,1,0:T(1,128)S(1)} %reshape.1057), channel_id=1, source_target_pairs={{4,0},{8,4},{12,8},{16,12},{20,16},{24,20},{28,24},{0,28},{5,1},{9... | collective-permute-start | bytes 13832 | tf_op jit(solution)/shard_map/ppermute | solution.py:31
  9.9 10.0 collective-permute-start.7
  11.9 7.7 collective-permute-start.6
  20.0 1.8 collective-permute-start.9
  20.1 2.3 collective-permute-start.8
  20.6 6.0 collective-permute-start.3
  20.7 5.9 collective-permute-start.2
  24.6 39.3 %collective-permute-start.11 = (bf16[3,3,1,32768]{3,1,2,0:T(4,128)(2,1)}, bf16[3,3,1,32768]{3,1,2,0:T(4,128)(2,1)S(1)}, u32[]{:S(2)}, u32[]{:S(2)}) collective-permute-start(bf16[3,3,1,32768]{3,1,2,0:T(4,128)(2,1)} %pad_maximum_fusion.1), channel_id=1, source_target_pairs={{1,0},{0,1},{3,2},{2,3},{5,4},{4,5},{7,6},{6,7},{9,8},{8,9},{11,10... | collective-permute-start | bytes 1769480 | tf_op jit(solution)/shard_map/ppermute | solution.py:31
  26.1 37.8 %collective-permute-start.10 = (bf16[3,3,1,32768]{3,1,2,0:T(4,128)(2,1)}, bf16[3,3,1,32768]{3,1,2,0:T(4,128)(2,1)}, u32[]{:S(2)}, u32[]{:S(2)}) collective-permute-start(bf16[3,3,1,32768]{3,1,2,0:T(4,128)(2,1)} %pad_maximum_fusion.1), channel_id=1, source_target_pairs={{0,1},{1,0},{2,3},{3,2},{4,5},{5,4},{6,7},{7,6},{8,9},{9,8},{10,11... | collective-permute-start | bytes 1769480 | tf_op jit(solution)/shard_map/ppermute | solution.py:28
  26.7 35.9 %collective-permute-start.5 = (f32[3,3,1,1152]{3,2,1,0:T(1,128)S(1)}, f32[3,3,1,1152]{3,2,1,0:T(1,128)S(1)}, u32[]{:S(2)}, u32[]{:S(2)}) collective-permute-start(f32[3,3,1,1152]{3,2,1,0:T(1,128)S(1)} %pad_maximum_fusion.3), channel_id=1, source_target_pairs={{1,0},{0,1},{3,2},{2,3},{5,4},{4,5},{7,6},{6,7},{9,8},{8,9},{11,10... | collective-permute-start | bytes 124424 | tf_op jit(solution)/shard_map/ppermute | solution.py:31
  28.3 34.8 %collective-permute-start.4 = (f32[3,3,1,1152]{3,2,1,0:T(1,128)S(1)}, f32[3,3,1,1152]{3,2,1,0:T(1,128)S(1)}, u32[]{:S(2)}, u32[]{:S(2)}) collective-permute-start(f32[3,3,1,1152]{3,2,1,0:T(1,128)S(1)} %pad_maximum_fusion.3), channel_id=1, source_target_pairs={{0,1},{1,0},{2,3},{3,2},{4,5},{5,4},{6,7},{7,6},{8,9},{9,8},{10,11... | collective-permute-start | bytes 124424 | tf_op jit(solution)/shard_map/ppermute | solution.py:28
  398.4 15.4 %copy-start.9 = (f32[4,128,64]{2,1,0:T(8,128)}, f32[4,128,64]{2,1,0:T(8,128)S(1)}, u32[]{:S(2)}) copy-start(f32[4,128,64]{2,1,0:T(8,128)S(1)} %get-tuple-element.1317) | copy-start | bytes 393220 | tf_op jit(solution)/shard_map/while
  424.7 15.4 %copy-start.9 = (f32[4,128,64]{2,1,0:T(8,128)}, f32[4,128,64]{2,1,0:T(8,128)S(1)}, u32[]{:S(2)}) copy-start(f32[4,128,64]{2,1,0:T(8,128)S(1)} %get-tuple-element.1317) | copy-start | bytes 393220 | tf_op jit(solution)/shard_map/while
  450.9 15.4 %copy-start.9 = (f32[4,128,64]{2,1,0:T(8,128)}, f32[4,128,64]{2,1,0:T(8,128)S(1)}, u32[]{:S(2)}) copy-start(f32[4,128,64]{2,1,0:T(8,128)S(1)} %get-tuple-element.1317) | copy-start | bytes 393220 | tf_op jit(solution)/shard_map/while
  477.1 15.4 %copy-start.9 = (f32[4,128,64]{2,1,0:T(8,128)}, f32[4,128,64]{2,1,0:T(8,128)S(1)}, u32[]{:S(2)}) copy-start(f32[4,128,64]{2,1,0:T(8,128)S(1)} %get-tuple-element.1317) | copy-start | bytes 393220 | tf_op jit(solution)/shard_map/while
  503.4 15.4 %copy-start.9 = (f32[4,128,64]{2,1,0:T(8,128)}, f32[4,128,64]{2,1,0:T(8,128)S(1)}, u32[]{:S(2)}) copy-start(f32[4,128,64]{2,1,0:T(8,128)S(1)} %get-tuple-element.1317) | copy-start | bytes 393220 | tf_op jit(solution)/shard_map/while
  529.6 15.4 %copy-start.9 = (f32[4,128,64]{2,1,0:T(8,128)}, f32[4,128,64]{2,1,0:T(8,128)S(1)}, u32[]{:S(2)}) copy-start(f32[4,128,64]{2,1,0:T(8,128)S(1)} %get-tuple-element.1317) | copy-start | bytes 393220 | tf_op jit(solution)/shard_map/while
  555.8 15.4 %copy-start.9 = (f32[4,128,64]{2,1,0:T(8,128)}, f32[4,128,64]{2,1,0:T(8,128)S(1)}, u32[]{:S(2)}) copy-start(f32[4,128,64]{2,1,0:T(8,128)S(1)} %get-tuple-element.1317) | copy-start | bytes 393220 | tf_op jit(solution)/shard_map/while
  582.0 15.4 %copy-start.9 = (f32[4,128,64]{2,1,0:T(8,128)}, f32[4,128,64]{2,1,0:T(8,128)S(1)}, u32[]{:S(2)}) copy-start(f32[4,128,64]{2,1,0:T(8,128)S(1)} %get-tuple-element.1317) | copy-start | bytes 393220 | tf_op jit(solution)/shard_map/while
  608.3 15.4 %copy-start.9 = (f32[4,128,64]{2,1,0:T(8,128)}, f32[4,128,64]{2,1,0:T(8,128)S(1)}, u32[]{:S(2)}) copy-start(f32[4,128,64]{2,1,0:T(8,128)S(1)} %get-tuple-element.1317) | copy-start | bytes 393220 | tf_op jit(solution)/shard_map/while
  634.5 15.4 %copy-start.9 = (f32[4,128,64]{2,1,0:T(8,128)}, f32[4,128,64]{2,1,0:T(8,128)S(1)}, u32[]{:S(2)}) copy-start(f32[4,128,64]{2,1,0:T(8,128)S(1)} %get-tuple-element.1317) | copy-start | bytes 393220 | tf_op jit(solution)/shard_map/while
  660.7 15.4 %copy-start.9 = (f32[4,128,64]{2,1,0:T(8,128)}, f32[4,128,64]{2,1,0:T(8,128)S(1)}, u32[]{:S(2)}) copy-start(f32[4,128,64]{2,1,0:T(8,128)S(1)} %get-tuple-element.1317) | copy-start | bytes 393220 | tf_op jit(solution)/shard_map/while
  686.9 15.4 %copy-start.9 = (f32[4,128,64]{2,1,0:T(8,128)}, f32[4,128,64]{2,1,0:T(8,128)S(1)}, u32[]{:S(2)}) copy-start(f32[4,128,64]{2,1,0:T(8,128)S(1)} %get-tuple-element.1317) | copy-start | bytes 393220 | tf_op jit(solution)/shard_map/while
  713.1 15.4 %copy-start.9 = (f32[4,128,64]{2,1,0:T(8,128)}, f32[4,128,64]{2,1,0:T(8,128)S(1)}, u32[]{:S(2)}) copy-start(f32[4,128,64]{2,1,0:T(8,128)S(1)} %get-tuple-element.1317) | copy-start | bytes 393220 | tf_op jit(solution)/shard_map/while
  739.4 15.4 %copy-start.9 = (f32[4,128,64]{2,1,0:T(8,128)}, f32[4,128,64]{2,1,0:T(8,128)S(1)}, u32[]{:S(2)}) copy-start(f32[4,128,64]{2,1,0:T(8,128)S(1)} %get-tuple-element.1317) | copy-start | bytes 393220 | tf_op jit(solution)/shard_map/while
  765.6 15.4 %copy-start.9 = (f32[4,128,64]{2,1,0:T(8,128)}, f32[4,128,64]{2,1,0:T(8,128)S(1)}, u32[]{:S(2)}) copy-start(f32[4,128,64]{2,1,0:T(8,128)S(1)} %get-tuple-element.1317) | copy-start | bytes 393220 | tf_op jit(solution)/shard_map/while
  791.8 15.4 %copy-start.9 = (f32[4,128,64]{2,1,0:T(8,128)}, f32[4,128,64]{2,1,0:T(8,128)S(1)}, u32[]{:S(2)}) copy-start(f32[4,128,64]{2,1,0:T(8,128)S(1)} %get-tuple-element.1317) | copy-start | bytes 393220 | tf_op jit(solution)/shard_map/while
  818.0 15.4 %copy-start.9 = (f32[4,128,64]{2,1,0:T(8,128)}, f32[4,128,64]{2,1,0:T(8,128)S(1)}, u32[]{:S(2)}) copy-start(f32[4,128,64]{2,1,0:T(8,128)S(1)} %get-tuple-element.1317) | copy-start | bytes 393220 | tf_op jit(solution)/shard_map/while
  844.3 15.4 %copy-start.9 = (f32[4,128,64]{2,1,0:T(8,128)}, f32[4,128,64]{2,1,0:T(8,128)S(1)}, u32[]{:S(2)}) copy-start(f32[4,128,64]{2,1,0:T(8,128)S(1)} %get-tuple-element.1317) | copy-start | bytes 393220 | tf_op jit(solution)/shard_map/while
  870.5 15.4 %copy-start.9 = (f32[4,128,64]{2,1,0:T(8,128)}, f32[4,128,64]{2,1,0:T(8,128)S(1)}, u32[]{:S(2)}) copy-start(f32[4,128,64]{2,1,0:T(8,128)S(1)} %get-tuple-element.1317) | copy-start | bytes 393220 | tf_op jit(solution)/shard_map/while
  896.7 15.4 %copy-start.9 = (f32[4,128,64]{2,1,0:T(8,128)}, f32[4,128,64]{2,1,0:T(8,128)S(1)}, u32[]{:S(2)}) copy-start(f32[4,128,64]{2,1,0:T(8,128)S(1)} %get-tuple-element.1317) | copy-start | bytes 393220 | tf_op jit(solution)/shard_map/while
  922.9 15.4 %copy-start.9 = (f32[4,128,64]{2,1,0:T(8,128)}, f32[4,128,64]{2,1,0:T(8,128)S(1)}, u32[]{:S(2)}) copy-start(f32[4,128,64]{2,1,0:T(8,128)S(1)} %get-tuple-element.1317) | copy-start | bytes 393220 | tf_op jit(solution)/shard_map/while
  949.1 15.4 %copy-start.9 = (f32[4,128,64]{2,1,0:T(8,128)}, f32[4,128,64]{2,1,0:T(8,128)S(1)}, u32[]{:S(2)}) copy-start(f32[4,128,64]{2,1,0:T(8,128)S(1)} %get-tuple-element.1317) | copy-start | bytes 393220 | tf_op jit(solution)/shard_map/while
  975.4 15.4 %copy-start.9 = (f32[4,128,64]{2,1,0:T(8,128)}, f32[4,128,64]{2,1,0:T(8,128)S(1)}, u32[]{:S(2)}) copy-start(f32[4,128,64]{2,1,0:T(8,128)S(1)} %get-tuple-element.1317) | copy-start | bytes 393220 | tf_op jit(solution)/shard_map/while
  1001.6 15.4 %copy-start.9 = (f32[4,128,64]{2,1,0:T(8,128)}, f32[4,128,64]{2,1,0:T(8,128)S(1)}, u32[]{:S(2)}) copy-start(f32[4,128,64]{2,1,0:T(8,128)S(1)} %get-tuple-element.1317) | copy-start | bytes 393220 | tf_op jit(solution)/shard_map/while
  1027.8 15.4 %copy-start.9 = (f32[4,128,64]{2,1,0:T(8,128)}, f32[4,128,64]{2,1,0:T(8,128)S(1)}, u32[]{:S(2)}) copy-start(f32[4,128,64]{2,1,0:T(8,128)S(1)} %get-tuple-element.1317) | copy-start | bytes 393220 | tf_op jit(solution)/shard_map/while
  1054.0 15.4 %copy-start.9 = (f32[4,128,64]{2,1,0:T(8,128)}, f32[4,128,64]{2,1,0:T(8,128)S(1)}, u32[]{:S(2)}) copy-start(f32[4,128,64]{2,1,0:T(8,128)S(1)} %get-tuple-element.1317) | copy-start | bytes 393220 | tf_op jit(solution)/shard_map/while
  1080.3 15.4 %copy-start.9 = (f32[4,128,64]{2,1,0:T(8,128)}, f32[4,128,64]{2,1,0:T(8,128)S(1)}, u32[]{:S(2)}) copy-start(f32[4,128,64]{2,1,0:T(8,128)S(1)} %get-tuple-element.1317) | copy-start | bytes 393220 | tf_op jit(solution)/shard_map/while
  1122.2 33.4 %collective-permute-start.12 = (bf16[3,3,33152]{2,1,0:T(4,128)(2,1)S(1)}, bf16[3,3,33152]{2,1,0:T(4,128)(2,1)S(1)}, u32[]{:S(2)}, u32[]{:S(2)}) collective-permute-start(bf16[3,3,33152]{2,1,0:T(4,128)(2,1)S(1)} %get-tuple-element.1032), channel_id=1, source_target_pairs={{0,4},{4,8},{8,12},{12,16},{16,20},{20,24},{24,28},{28,0},{1,5},{5... | collective-permute-start | bytes 1790216 | tf_op jit(solution)/shard_map/ppermute | solution.py:19
  1122.3 36.2 %collective-permute-start.13 = (bf16[3,3,33152]{2,1,0:T(4,128)(2,1)S(1)}, bf16[3,3,33152]{2,1,0:T(4,128)(2,1)S(1)}, u32[]{:S(2)}, u32[]{:S(2)}) collective-permute-start(bf16[3,3,33152]{2,1,0:T(4,128)(2,1)S(1)} %get-tuple-element.1033), channel_id=1, source_target_pairs={{0,28},{4,0},{8,4},{12,8},{16,12},{20,16},{24,20},{28,24},{1,29},{... | collective-permute-start | bytes 1790216 | tf_op jit(solution)/shard_map/ppermute | solution.py:19
  1159.5 1.6 collective-permute-start.14
  1159.6 1.9 collective-permute-start.15
  1161.9 6.5 collective-permute-start.16
  1163.5 6.9 collective-permute-start.17
  (394 other events, 1778.2 us)
where the time goes:
time: 1190 us; the launch traced here: 1170 us
  local copies, waits for them, and re-layouts  339 us (28%)
  other arithmetic  283 us (24%)
  loops' own time  230 us (19%)
  matrix products  217 us (18%)
  waiting for transfers between devices  81 us (7%)
  starting transfers between devices  20.8 us (2%)
    another operation x1, loops' own time, local(): lax.fori_loop(0, live_tiles, backward_tile, initial)  116 us
    another operation x1, loops' own time, local(): lax.fori_loop(0, live_tiles, forward_tile, jnp.zeros((own_cells, quad_row...  115 us
    dot_general x54, matrix products, tile_setup(): jnp.dot(onehot[own_cell].T, neighbour_geo[3:], precision=lax.Precision.HI...  105 us
    another operation x84, other arithmetic  80.4 us
    dynamic_slice x54, local copies, waits for them, and re-layouts, tile_setup(): listed_all[tile_index]  67.8 us
    while x891, local copies, waits for them, and re-layouts  59.4 us
    another operation x109, local copies, waits for them, and re-layouts  47.9 us
    scatter-add x27, local copies, waits for them, and re-layouts, backward_tile(): chan_grad = chan_grad.at[ext_place].add(to_chans)  46.2 us
  transfers between devices with their start and end apart: 18, of which 11 were waited for; matrix products, arithmetic and copies ran while one was open for 1% of the time, Pallas kernels for 0%

commit v1 on v0

v1 whole, which is shorter than its diff:
```python
import jax
import jax.numpy as jnp
from jax import lax
from jax.experimental import pallas as pl
from jax.experimental.pallas import tpu as pltpu
from jax.sharding import PartitionSpec as P

D = 256
CHANNELS = 64
NBASIS = 4
NSPEC = 6
SLOTS = 128
CUTOFF = 0.55
CENTRE = 0.5
ROWS = 80
POS_ROW = 64
CODE_ROW = 73
OFFSETS = 27
CHUNK = 16
CHUNKS = SLOTS // CHUNK
QUAD = NBASIS * SLOTS
WIDE = 4 * CHANNELS
LANES = 2 * SLOTS
PAIRS = (OFFSETS + 1) // 2
F32 = jnp.float32
BF16 = jnp.bfloat16


def dot_nn(a, b):
    return lax.dot_general(a, b, (((1,), (0,)), ((), ())), preferred_element_type=F32)


def dot_nt(a, b):
    return lax.dot_general(a, b, (((1,), (1,)), ((), ())), preferred_element_type=F32)


def split3(value):
    high = value.astype(BF16)
    rest = value - high.astype(F32)
    middle = rest.astype(BF16)
    low = (rest - middle.astype(F32)).astype(BF16)
    return high, middle, low


def pack_kernel(counts_ref, feats_ref, pos_ref, species_ref, w_env_ref, msg_ref):
    chans = lax.dot_general(
        w_env_ref[...],
        feats_ref[0, 0, 0],
        (((0,), (1,)), ((), ())),
        preferred_element_type=F32,
    )
    msg_ref[0, :CHANNELS] = chans.astype(BF16)
    pos = pos_ref[0, 0, 0]
    slots = lax.broadcasted_iota(jnp.int32, (1, SLOTS), 1)
    code = jnp.where(slots < counts_ref[0, 0, 0], species_ref[0, 0].astype(F32), -1.0)
    high = pos.astype(BF16).astype(F32)
    middle = (pos - high).astype(BF16).astype(F32)
    low = pos - high - middle
    tail = jnp.concatenate([high, middle, low, code, jnp.zeros((6, SLOTS), F32)], axis=0)
    msg_ref[0, CHANNELS:] = tail.astype(BF16)


def unique_of(offset, count):
    if count == 2:
        return jnp.where(offset == 0, 0, 1)
    return jnp.where(offset == 0, 0, jnp.where(offset > 0, 1, 2))


def main_kernel(shape, *refs):
    nxu, nyu, nzu, sizes = shape
    cells = nxu * nyu * nzu
    refs = list(refs)
    list_ref = refs.pop(0)
    msg_refs = [refs.pop(0) for _ in range(nxu)]
    (feats_ref, radial_ref, scale_ref, w_hidden_ref, w_zero_ref, w_one_ref, w_out_ref) = refs[:7]
    refs = refs[7:]
    energy_ref, direct_ref = refs[:2]
    out_refs = refs[2 : 2 + nyu]
    (
        order, xi, weight, xj, chan, tiles, rmat, s_all, r_all, wb_all,
        acc, pbuf, grad, gradt, fi, cg, pg,
    ) = refs[2 + nyu :]

    def count_listed(index, found):
        order[found] = index
        return found + list_ref[0, 0, 0, index]

    live = lax.fori_loop(0, OFFSETS, count_listed, jnp.int32(0))
    order[live] = jnp.int32(OFFSETS)
    trips = (live + 1) // 2

    code_rows = []
    for cell in range(cells):
        msg = msg_refs[cell // (nyu * nzu)]
        at = cell % (nyu * nzu)
        tail = msg[at, CHANNELS:].astype(F32)
        place = tail[0:3] + tail[3:6] + tail[6:9]
        xj[cell, 0:3] = (place - CENTRE) * (1.0 / CUTOFF)
        code_rows.append(tail[9:10])
        chan[cell] = msg[at, :CHANNELS]
        cg[cell] = jnp.zeros((CHANNELS, SLOTS), F32)
        pg[cell] = jnp.zeros((8, SLOTS), F32)
    for axis in range(3):
        row = jnp.broadcast_to(xj[0, axis : axis + 1], (SLOTS, SLOTS))
        xi[axis] = row.T
    code_i = jnp.broadcast_to(code_rows[0], (SLOTS, SLOTS)).T
    lane = lax.broadcasted_iota(jnp.int32, (SLOTS, SLOTS), 1)
    sub = lax.broadcasted_iota(jnp.int32, (SLOTS, SLOTS), 0)
    onehot = jnp.where((code_i == (lane % 8).astype(F32)) & (lane < 24), 1.0, 0.0)
    onehot = onehot.astype(BF16)
    scale = scale_ref[...]
    coef = []
    for cell in range(cells):
        total = jnp.zeros((8, SLOTS), F32)
        for kind in range(NSPEC):
            column = jnp.broadcast_to(scale[:, kind : kind + 1], (8, SLOTS))
            total = total + jnp.where(code_rows[cell] == float(kind), column, 0.0)
        high = total.astype(BF16).astype(F32)
        middle = (total - high).astype(BF16).astype(F32)
        low = total - high - middle
        coef.append(
            jnp.concatenate([high, middle, low, jnp.zeros((104, SLOTS), F32)], axis=0).astype(BF16)
        )
    for cell in range(cells):
        strength = dot_nn(onehot, coef[cell])
        if cell == 0:
            strength = jnp.where(lane == sub, 0.0, strength)
        weight[cell] = strength
    weight[cells] = jnp.zeros((SLOTS, SLOTS), F32)
    acc[...] = jnp.zeros_like(acc)
    fi[...] = jnp.zeros_like(fi)

    def place_of(tile):
        real = tile < OFFSETS
        held = jnp.where(real, tile, 13)
        ox = held // 9 - 1
        oy = held // 3 % 3 - 1
        oz = held % 3 - 1
        ux = unique_of(ox, sizes[0])
        uy = unique_of(oy, sizes[1])
        uz = unique_of(oz, sizes[2])
        cell = (ux * nzu + uz) * nyu + uy
        shifts = [o.astype(F32) * (1.0 / CUTOFF) for o in (ox, oy, oz)]
        return cell, jnp.where(real, cell, cells), shifts

    def rows_of(pair):
        first, second = order[2 * pair], order[2 * pair + 1]
        cell_a, weight_a, shift_a = place_of(first)
        cell_b, weight_b, shift_b = place_of(second)
        rows = [
            jnp.concatenate(
                [
                    xj[cell_a, axis : axis + 1] + shift_a[axis],
                    xj[cell_b, axis : axis + 1] + shift_b[axis],
                ],
                axis=1,
            )
            for axis in range(3)
        ]
        return cell_a, cell_b, weight_a, weight_b, rows

    def relative(rows, block):
        out = []
        for axis in range(3):
            own = xi[axis, block * CHUNK : (block + 1) * CHUNK]
            out.append(rows[axis] - jnp.concatenate([own, own], axis=1))
        return out

    def forward(pair, carry):
        cell_a, cell_b, weight_a, weight_b, rows = rows_of(pair)
        values = jnp.concatenate([chan[cell_a], chan[cell_b]], axis=1)
        rmat[pair, :CHANNELS] = values
        wide = values.astype(F32)
        for axis in range(3):
            base = (axis + 1) * CHANNELS
            rmat[pair, base : base + CHANNELS] = (wide * rows[axis]).astype(BF16)
        for block in range(CHUNKS):
            at = slice(block * CHUNK, (block + 1) * CHUNK)
            dx, dy, dz = relative(rows, block)
            s = jnp.minimum(dx * dx + dy * dy + dz * dz, 1.0)
            inside = 1.0 - s
            spread = 4.0 * s - 0.5
            ratio = jnp.exp(8.0 * s)
            strength = jnp.concatenate([weight[weight_a, at], weight[weight_b, at]], axis=1)
            wb = strength * jnp.exp(-(spread * spread))
            s_all[pair, at] = s
            r_all[pair, at] = ratio
            wb_all[pair, at] = wb
            tile = wb * (inside * inside)
            for k in range(NBASIS):
                base = block * 4 * CHUNK + k * CHUNK
                tiles[pair, base : base + CHUNK] = tile.astype(BF16)
                if k + 1 < NBASIS:
                    tile = tile * ratio
        acc[...] += dot_nt(tiles[pair], rmat[pair])
        return carry

    lax.fori_loop(0, trips, forward, 0)

    radial = radial_ref[...]
    weights_k = []
    for k in range(NBASIS):
        row = radial[k : k + 1] * LADDER[k]
        weights_k.append(jnp.concatenate([row] * 4, axis=1))
    mixed = []
    for block in range(CHUNKS):
        base = block * 4 * CHUNK
        total = weights_k[0] * acc[base : base + CHUNK]
        for k in range(1, NBASIS):
            total = total + weights_k[k] * acc[base + k * CHUNK : base + (k + 1) * CHUNK]
        mixed.append(total)
    mixed = jnp.concatenate(mixed, axis=0)
    scalar = mixed[:, :CHANNELS]
    vectors = [
        mixed[:, (axis + 1) * CHANNELS : (axis + 2) * CHANNELS] - xi[axis][:, :CHANNELS] * scalar
        for axis in range(3)
    ]
    norms = vectors[0] * vectors[0] + vectors[1] * vectors[1] + vectors[2] * vectors[2]
    pre = dot_nn(feats_ref[0, 0, 0], w_hidden_ref[...])
    pre = pre + dot_nn(scalar.astype(BF16), w_zero_ref[...])
    pre = pre + dot_nn(norms.astype(BF16), w_one_ref[...])
    gate = jax.nn.sigmoid(pre)
    w_out = w_out_ref[...]
    occupied = code_i >= 0.0
    energy = jnp.sum(pre * gate * w_out, axis=1, keepdims=True)
    energy = jnp.where(occupied, jnp.broadcast_to(energy, (SLOTS, SLOTS)), 0.0).T
    energy_ref[0, 0] = energy[0:1]
    occupied_wide = jnp.concatenate([occupied, occupied], axis=1)
    pre_grad = jnp.where(occupied_wide, w_out * gate * (1.0 + pre * (1.0 - gate)), 0.0)
    pre_grad = pre_grad.astype(BF16)
    direct_ref[...] = dot_nt(pre_grad, w_hidden_ref[...])
    zero_grad = dot_nt(pre_grad, w_zero_ref[...])
    one_grad = 2.0 * dot_nt(pre_grad, w_one_ref[...])
    parts = [vector * one_grad for vector in vectors]
    own_force = [jnp.sum(part * scalar, axis=1, keepdims=True) for part in parts]
    head = zero_grad
    for axis in range(3):
        head = head - xi[axis][:, :CHANNELS] * parts[axis]
    full = jnp.concatenate([head] + parts, axis=1)
    for block in range(CHUNKS):
        piece = full[block * CHUNK : (block + 1) * CHUNK]
        for k in range(NBASIS):
            base = block * 4 * CHUNK + k * CHUNK
            scaled = weights_k[k] * piece
            grad[base : base + CHUNK] = scaled.astype(BF16)
            pbuf[base : base + CHUNK] = scaled
    for step in range(QUAD // SLOTS):
        for half in range(WIDE // SLOTS):
            lanes = slice(half * SLOTS, (half + 1) * SLOTS)
            rows = slice(step * SLOTS, (step + 1) * SLOTS)
            gradt[lanes, rows] = pbuf[rows, lanes].T.astype(BF16)

    def backward(pair, carry):
        cell_a, cell_b, weight_a, weight_b, rows = rows_of(pair)
        pbuf[...] = dot_nn(grad[...], rmat[pair])
        back = dot_nn(gradt[...], tiles[pair])
        values = rmat[pair, :CHANNELS].astype(F32)
        sums = back[:CHANNELS]
        along = []
        for axis in range(3):
            part = back[(axis + 1) * CHANNELS : (axis + 2) * CHANNELS]
            sums = sums + rows[axis] * part
            along.append(jnp.sum(values * part, axis=0, keepdims=True))
        cg[cell_a] += sums[:, :SLOTS]
        cg[cell_b] += sums[:, SLOTS:]
        totals = [jnp.zeros((CHUNK, LANES), F32) for _ in range(3)]
        for block in range(CHUNKS):
            at = slice(block * CHUNK, (block + 1) * CHUNK)
            s = s_all[pair, at]
            ratio = r_all[pair, at]
            inside = 1.0 - s
            step = 8.0 * inside
            level = -2.0 - step * (4.0 * s - 0.5)
            levels = [level]
            for k in range(1, NBASIS):
                levels.append(levels[-1] + step)
            base = block * 4 * CHUNK
            slope = levels[3] * pbuf[base + 3 * CHUNK : base + 4 * CHUNK]
            for k in (2, 1, 0):
                slope = slope * ratio + levels[k] * pbuf[base + k * CHUNK : base + (k + 1) * CHUNK]
            slope = slope * (wb_all[pair, at] * inside)
            for axis, delta in enumerate(relative(rows, block)):
                push = slope * delta
                totals[axis] = totals[axis] + push
                fi[axis, at] += push[:, :SLOTS] + push[:, SLOTS:]
        for axis in range(3):
            total = jnp.sum(totals[axis], axis=0, keepdims=True) * 2.0 + along[axis]
            pg[cell_a, axis : axis + 1] += total[:, :SLOTS]
            pg[cell_b, axis : axis + 1] += total[:, SLOTS:]
        return carry

    lax.fori_loop(0, trips, backward, 0)

    for axis in range(3):
        column = jnp.sum(fi[axis], axis=1, keepdims=True) * 2.0 + own_force[axis]
        row = jnp.broadcast_to(column, (SLOTS, SLOTS)).T
        pg[0, axis : axis + 1] -= row[0:1]
    for uy in range(nyu):
        for uz in range(nzu):
            for ux in range(nxu):
                cell = (ux * nzu + uz) * nyu + uy
                kind = out_refs[uy].dtype
                at = uz * nxu + ux
                out_refs[uy][at, :CHANNELS] = cg[cell].astype(kind)
                tail = jnp.concatenate([pg[cell], jnp.zeros((8, SLOTS), F32)], axis=0)
                out_refs[uy][at, CHANNELS:] = (tail * (1.0 / CUTOFF)).astype(kind)


LADDER = (1.0, 0.1353352832366127, 0.0024787521766663585, 6.14421235332821e-06)


def finish_kernel(count, *refs):
    keep_ref = refs[0]
    got_refs = refs[1 : 1 + count]
    direct_ref, w_env_ref, force_ref, grad_ref = refs[1 + count :]
    total = keep_ref[0]
    for got in got_refs:
        total = total + got[0].astype(F32)
    chan = total[:CHANNELS]
    high = chan.astype(BF16)
    low = (chan - high.astype(F32)).astype(BF16)
    both = jnp.concatenate([high, low], axis=0)
    w_env = w_env_ref[...]
    weights = jnp.concatenate([w_env, w_env], axis=1)
    part = lax.dot_general(both, weights, (((0,), (1,)), ((), ())), preferred_element_type=F32)
    grad_ref[0, 0, 0] = (direct_ref[...] + part).astype(BF16)
    force_ref[0, 0, 0] = -total[POS_ROW : POS_ROW + 3]


def shifted(value, axis, steps):
    count = lax.axis_size(axis)
    return lax.ppermute(value, axis, [(i, (i + steps) % count) for i in range(count)])


def gathered(value, axis):
    if lax.axis_size(axis) == 2:
        return [value, shifted(value, axis, 1)]
    return [value, shifted(value, axis, -1), shifted(value, axis, 1)]


def returned(parts, axis):
    if lax.axis_size(axis) == 2:
        return [shifted(parts[0], axis, 1)]
    return [shifted(parts[0], axis, 1), shifted(parts[1], axis, -1)]


VMEM = pl.BlockSpec(memory_space=pltpu.VMEM)
SMEM = pl.BlockSpec(memory_space=pltpu.SMEM)


def local(
    feats, positions, species, cell_counts, pair_list, w_env, radial, pair_scale, w_hidden,
    w_zero, w_one, w_out,
):
    sizes = [lax.axis_size(axis) for axis in ("gx", "gy", "gz")]
    nxu, nyu, nzu = [2 if size == 2 else 3 for size in sizes]
    cells = nxu * nyu * nzu
    msg = pl.pallas_call(
        pack_kernel,
        out_shape=jax.ShapeDtypeStruct((1, ROWS, SLOTS), BF16),
        in_specs=[SMEM, VMEM, VMEM, VMEM, VMEM],
        out_specs=VMEM,
        name="pack",
    )(cell_counts, feats, positions, species, w_env)
    block = jnp.concatenate(gathered(msg, "gy"), axis=0)
    block = jnp.concatenate(gathered(block, "gz"), axis=0)
    blocks = gathered(block, "gx")

    scale = jnp.pad(pair_scale, ((0, 2), (0, 2)))
    out_cells = nxu * nzu
    out_shape = [
        jax.ShapeDtypeStruct((1, 1, 1, SLOTS), F32),
        jax.ShapeDtypeStruct((SLOTS, D), F32),
        jax.ShapeDtypeStruct((out_cells, ROWS, SLOTS), F32),
    ] + [jax.ShapeDtypeStruct((out_cells, ROWS, SLOTS), BF16)] * (nyu - 1)
    scratch = [
        pltpu.SMEM((OFFSETS + 5,), jnp.int32),
        pltpu.VMEM((3, SLOTS, SLOTS), F32),
        pltpu.VMEM((cells + 1, SLOTS, SLOTS), F32),
        pltpu.VMEM((cells, 8, SLOTS), F32),
        pltpu.VMEM((cells, CHANNELS, SLOTS), BF16),
        pltpu.VMEM((PAIRS, QUAD, LANES), BF16),
        pltpu.VMEM((PAIRS, WIDE, LANES), BF16),
        pltpu.VMEM((PAIRS, SLOTS, LANES), F32),
        pltpu.VMEM((PAIRS, SLOTS, LANES), F32),
        pltpu.VMEM((PAIRS, SLOTS, LANES), F32),
        pltpu.VMEM((QUAD, WIDE), F32),
        pltpu.VMEM((QUAD, WIDE), F32),
        pltpu.VMEM((QUAD, WIDE), BF16),
        pltpu.VMEM((WIDE, QUAD), BF16),
        pltpu.VMEM((3, SLOTS, SLOTS), F32),
        pltpu.VMEM((cells, CHANNELS, SLOTS), F32),
        pltpu.VMEM((cells, 8, SLOTS), F32),
    ]
    results = pl.pallas_call(
        lambda *refs: main_kernel((nxu, nyu, nzu, sizes), *refs),
        out_shape=out_shape,
        in_specs=[SMEM] + [VMEM] * (nxu + 7),
        out_specs=[VMEM] * len(out_shape),
        scratch_shapes=scratch,
        name="pairs",
    )(
        pair_list, *blocks, feats, radial, scale, w_hidden, w_zero, w_one, w_out.reshape(1, D)
    )
    energy, direct, keep = results[:3]
    total = keep
    for got in returned(results[3:], "gy"):
        total = total + got.astype(F32)
    sends = [total[uz * nxu : (uz + 1) * nxu].astype(BF16) for uz in range(1, nzu)]
    total = total[:nxu]
    for got in returned(sends, "gz"):
        total = total + got.astype(F32)
    sends = [total[ux : ux + 1].astype(BF16) for ux in range(1, nxu)]
    keep = total[:1]
    arrived = returned(sends, "gx")
    forces, feat_grad = pl.pallas_call(
        lambda *refs: finish_kernel(len(arrived), *refs),
        out_shape=[
            jax.ShapeDtypeStruct((1, 1, 1, 3, SLOTS), F32),
            jax.ShapeDtypeStruct((1, 1, 1, SLOTS, D), BF16),
        ],
        in_specs=[VMEM] * (3 + len(arrived)),
        out_specs=[VMEM] * 2,
        name="finish",
    )(keep, *arrived, direct, w_env)
    return energy, forces, feat_grad


def solution(mesh):
    cell = P("gx", "gy", "gz")
    in_specs = (cell,) * 5 + (P(),) * 7
    return jax.shard_map(
        local, mesh=mesh, in_specs=in_specs, out_specs=(cell,) * 3, check_vma=False
    )
```

time: 1190 us -> 53.7 us (0.05); the launches traced: 1170 us -> 52.9 us
  local copies, waits for them, and re-layouts: 339 us -> 5.8 us
  other arithmetic: 283 us -> 1.73 us
  loops' own time: 230 us -> 0 us
  matrix products: 217 us -> 0 us
  waiting for transfers between devices: 81 us -> 15.6 us
  Pallas kernels: 0 us -> 13.7 us
    another operation x2 -> x0, loops' own time: 230 us -> none  [the longest x1 116 us: local(): lax.fori_loop(0, live_tiles, backward_tile, initial)]
    dot_general x145 -> x0, matrix products: 217 us -> none  [the longest x54 105 us: tile_setup(): jnp.dot(onehot[own_cell].T, neighbour_geo[3:], precision=lax.Precision.HI...]
    dynamic_slice x108 -> x0, local copies, waits for them, and re-layouts: 104 us -> none  [the longest x54 67.8 us: tile_setup(): listed_all[tile_index]]
    reduce_sum x163 -> x0, other arithmetic: 99.2 us -> none  [the longest x27 37 us: pair_grad(): value_part = jnp.sum(through_basis * radial_basis, axis=0)]
    another operation x84 -> x1, other arithmetic: 80.4 us -> 0.02 us
    ppermute x18 -> x8, waiting for transfers between devices: 81 us -> 15.6 us  [shifted(): lax.ppermute(value, axis, [(i, (i + steps) % count) for i in range(count)])]
    while x892 -> x0, local copies, waits for them, and re-layouts: 60 us -> none
    another operation x109 -> x0, local copies, waits for them, and re-layouts: 47.9 us -> none
  transfers between devices with their start and end apart: 18 -> 8, of which waited for: 11 -> 7; matrix products, arithmetic and copies ran while one was open for 1% -> 2% of each run, Pallas kernels for 0% -> 0%
where the time goes in v1:
time: 53.7 us; the launch traced here: 52.9 us
  waiting for transfers between devices  15.6 us (29%)
  starting transfers between devices  14.7 us (27%)
  Pallas kernels  13.7 us (26%)
  local copies, waits for them, and re-layouts  5.8 us (11%)
  other arithmetic  1.73 us (3%)
  between operations  1.36 us (3%)
    ppermute x8, waiting for transfers between devices, shifted(): lax.ppermute(value, axis, [(i, (i + steps) % count) for i in range(count)])  15.6 us
    ppermute x8, starting transfers between devices, shifted(): lax.ppermute(value, axis, [(i, (i + steps) % count) for i in range(count)])  14.7 us
    pallas_call x1, Pallas kernels, local(): pl.pallas_call(lambda *refs: main_kernel((nxu, nyu, nzu, sizes), *refs),...  10.2 us
    unnamed x19, local copies, waits for them, and re-layouts  4.58 us
    pallas_call x1, Pallas kernels, local(): pl.pallas_call(lambda *refs: finish_kernel(len(arrived), *refs), out_shap...  1.83 us
    pallas_call x1, Pallas kernels, local(): pl.pallas_call(pack_kernel, out_shape=jax.ShapeDtypeStruct((1, ROWS, SLOT...  1.68 us
  transfers between devices with their start and end apart: 8, of which 7 were waited for; matrix products, arithmetic and copies ran while one was open for 2% of the time, Pallas kernels for 0%

profile of v1, /device:TPU:0, one launch (start us, length us, event | category | flops | bytes accessed | tf_op | source)
XLA Modules:
  0.0 52.9 jit_solution(854363614441368137)
XLA Ops:
  0.6 0.0 copy-start.7
  1.3 0.0 copy-done.7
  1.3 0.6 %copy.15.pos_ref = f32[1,1,1,3,128]{4,3,2,1,0:T(4,128)} copy(f32[1,1,1,3,128]{4,2,3,1,0:T(1,128)S(1)} %copy-done.7) | data formatting | bytes 3072 | tf_op args[1]
  1.9 1.5 %copy.16.w_env_ref.refs_4_ = bf16[256,64]{1,0:T(8,128)(2,1)} copy(bf16[256,64]{0,1:T(8,128)(2,1)} %param.17) | data formatting | bytes 65536 | tf_op args[5]
  3.4 1.7 %pack.1 = bf16[1,80,128]{2,1,0:T(8,128)(2,1)} custom-call(s32[1,1,1]{2,1,0:T(1,128)S(6)} %copy.19.counts_ref, bf16[1,1,1,128,256]{4,3,2,1,0:T(8,128)(2,1)} %refs_4_.2, f32[1,1,1,3,128]{4,3,2,1,0:T(4,128)} %copy.15.pos_ref, s32[1,1,1,128]{3,2,1,0:T(1,128)} %species_ref.1, bf16[256,64]{1,0:T(8,128)(2,1)} %copy.16.w_env_ref.refs_4_), custom_call_target="tpu_custom_call" | custom-call | tf_op jit(solution)/shard_map/pack/pallas_call | solution.py:358
  5.1 0.0 copy-start.1
  5.1 0.5 collective-permute-start
  5.6 1.1 %collective-permute-done = bf16[1,80,128]{2,1,0:T(8,128)(2,1)S(1)} collective-permute-done((bf16[1,80,128]{2,1,0:T(8,128)(2,1)}, bf16[1,80,128]{2,1,0:T(8,128)(2,1)S(1)}, u32[]{:S(2)}, u32[]{:S(2)}) %collective-permute-start) | collective-permute-done | bytes 20512 | tf_op jit(solution)/shard_map/ppermute | solution.py:332
  6.6 0.7 %pad_maximum_fusion.1 = bf16[2,80,128]{2,1,0:T(8,128)(2,1)S(1)} fusion(bf16[1,80,128]{2,1,0:T(8,128)(2,1)S(1)} %collective-permute-done, bf16[1,80,128]{2,1,0:T(8,128)(2,1)} %pack.1), kind=kLoop, calls=%fused_computation.4 | loop fusion | flops 20480 | bytes 81920 | tf_op jit(solution)/shard_map/concatenate | solution.py:365
  7.3 0.0 copy-start.6
  7.4 2.8 %collective-permute-start.1 = (bf16[2,80,128]{2,1,0:T(8,128)(2,1)S(1)}, bf16[2,80,128]{2,1,0:T(8,128)(2,1)S(1)}, u32[]{:S(2)}, u32[]{:S(2)}) collective-permute-start(bf16[2,80,128]{2,1,0:T(8,128)(2,1)S(1)} %pad_maximum_fusion.1), channel_id=1, source_target_pairs={{0,1},{1,0},{2,3},{3,2},{4,5},{5,4},{6,7},{7,6},{8,9},{9,8},{10,11... | collective-permute-start | bytes 122888 | tf_op jit(solution)/shard_map/ppermute | solution.py:332
  10.2 2.0 %collective-permute-done.1 = bf16[2,80,128]{2,1,0:T(8,128)(2,1)S(1)} collective-permute-done((bf16[2,80,128]{2,1,0:T(8,128)(2,1)S(1)}, bf16[2,80,128]{2,1,0:T(8,128)(2,1)S(1)}, u32[]{:S(2)}, u32[]{:S(2)}) %collective-permute-start.1) | collective-permute-done | bytes 40992 | tf_op jit(solution)/shard_map/ppermute | solution.py:332
  12.2 0.0 copy-done.1
  12.2 0.0 copy-start
  12.2 2.0 %collective-permute-start.3 = (bf16[4,80,128]{2,1,0:T(8,128)(2,1)S(1)}, bf16[4,80,128]{2,1,0:T(8,128)(2,1)S(1)}, u32[]{:S(2)}, u32[]{:S(2)}) collective-permute-start(bf16[4,80,128]{2,1,0:T(8,128)(2,1)S(1)} %pad_maximum_fusion.refs_1_), channel_id=1, source_target_pairs={{0,4},{4,8},{8,12},{12,16},{16,20},{20,24},{24,28},{28,0},{1,5},{5... | collective-permute-start | bytes 245768 | tf_op jit(solution)/shard_map/ppermute | solution.py:332
  14.3 3.1 %collective-permute-start.2 = (bf16[4,80,128]{2,1,0:T(8,128)(2,1)S(1)}, bf16[4,80,128]{2,1,0:T(8,128)(2,1)S(1)}, u32[]{:S(2)}, u32[]{:S(2)}) collective-permute-start(bf16[4,80,128]{2,1,0:T(8,128)(2,1)S(1)} %pad_maximum_fusion.refs_1_), channel_id=1, source_target_pairs={{0,28},{4,0},{8,4},{12,8},{16,12},{20,16},{24,20},{28,24},{1,29},{... | collective-permute-start | bytes 245768 | tf_op jit(solution)/shard_map/ppermute | solution.py:332
  17.4 0.0 copy-done.6
  17.4 0.6 %pad.4.refs_6_ = f32[8,8]{1,0:T(8,128)} pad(f32[6,6]{1,0:T(8,128)S(1)} %copy-done.6, f32[]{:T(128)} %constant.2.clone.1), padding=0_2x0_2 | pad | bytes 404 | tf_op jit(solution)/shard_map/jit(_pad)/pad | solution.py:369
  18.0 1.8 %collective-permute-done.3.refs_3_ = bf16[4,80,128]{2,1,0:T(8,128)(2,1)S(1)} collective-permute-done((bf16[4,80,128]{2,1,0:T(8,128)(2,1)S(1)}, bf16[4,80,128]{2,1,0:T(8,128)(2,1)S(1)}, u32[]{:S(2)}, u32[]{:S(2)}) %collective-permute-start.3) | collective-permute-done | bytes 81952 | tf_op jit(solution)/shard_map/ppermute | solution.py:332
  19.8 0.0 copy-start.2
  19.8 0.0 collective-permute-done.2.refs_2_
  19.8 0.0 copy-start.3
  19.8 0.0 copy-done
  19.8 0.6 %copy-done.2 = bf16[4,80,128]{2,1,0:T(8,128)(2,1)} copy-done((bf16[4,80,128]{2,1,0:T(8,128)(2,1)}, bf16[4,80,128]{2,1,0:T(8,128)(2,1)S(1)}, u32[]{:S(2)}) %copy-start.2) | copy-done | bytes 81944
  20.4 0.0 copy-done.3
  20.5 10.2 %pairs.1 = (f32[1,1,1,128]{3,2,1,0:T(1,128)}, f32[128,256]{1,0:T(8,128)}, f32[6,80,128]{2,1,0:T(8,128)}, bf16[6,80,128]{2,1,0:T(8,128)(2,1)}) custom-call(s32[1,1,1,27]{3,2,1,0:T(1,128)} %refs_0_.1, bf16[4,80,128]{2,1,0:T(8,128)(2,1)} %copy-done, bf16[4,80,128]{2,1,0:T(8,128)(2,1)} %copy-done.3, bf16[4,80,128]{2,1,0:T(8,128)(2,1)} %copy-done.2, ...), custom_call_target="tpu_custom_call" | custom-call | tf_op jit(solution)/shard_map/pairs/pallas_call | solution.py:395
  30.7 0.0 collective-permute-start.4
  30.7 1.5 %collective-permute-done.4 = bf16[6,80,128]{2,1,0:T(8,128)(2,1)S(1)} collective-permute-done((bf16[6,80,128]{2,1,0:T(8,128)(2,1)}, bf16[6,80,128]{2,1,0:T(8,128)(2,1)S(1)}, u32[]{:S(2)}, u32[]{:S(2)}) %collective-permute-start.4) | collective-permute-done | bytes 122912 | tf_op jit(solution)/shard_map/ppermute | solution.py:332
  32.2 1.0 %convert_add_fusion = f32[6,80,128]{2,1,0:T(8,128)S(1)} fusion(f32[6,80,128]{2,1,0:T(8,128)} %get-tuple-element.10, bf16[6,80,128]{2,1,0:T(8,128)(2,1)S(1)} %collective-permute-done.4), kind=kLoop, calls=%fused_computation | loop fusion | flops 122880 | bytes 614400 | tf_op jit(solution)/shard_map/add | solution.py:408
  33.2 1.0 %collective-permute-start.5 = (bf16[3,80,128]{2,1,0:T(8,128)(2,1)S(1)}, bf16[3,80,128]{2,1,0:T(8,128)(2,1)S(1)}, u32[]{:S(2)}, u32[]{:S(2)}) collective-permute-start(bf16[3,80,128]{2,1,0:T(8,128)(2,1)S(1)} %slice.30), channel_id=1, source_target_pairs={{0,1},{1,0},{2,3},{3,2},{4,5},{5,4},{6,7},{7,6},{8,9},{9,8},{10,11... | collective-permute-start | bytes 184328 | tf_op jit(solution)/shard_map/ppermute | solution.py:332
  34.2 3.3 %collective-permute-done.5 = bf16[3,80,128]{2,1,0:T(8,128)(2,1)S(1)} collective-permute-done((bf16[3,80,128]{2,1,0:T(8,128)(2,1)S(1)}, bf16[3,80,128]{2,1,0:T(8,128)(2,1)S(1)}, u32[]{:S(2)}, u32[]{:S(2)}) %collective-permute-start.5) | collective-permute-done | bytes 61472 | tf_op jit(solution)/shard_map/ppermute | solution.py:332
  37.5 5.2 %collective-permute-start.7 = (bf16[1,80,128]{2,1,0:T(8,128)(2,1)S(1)}, bf16[1,80,128]{2,1,0:T(8,128)(2,1)S(1)}, u32[]{:S(2)}, u32[]{:S(2)}) collective-permute-start(bf16[1,80,128]{2,1,0:T(8,128)(2,1)S(1)} %get-tuple-element.20), channel_id=1, source_target_pairs={{0,28},{4,0},{8,4},{12,8},{16,12},{20,16},{24,20},{28,24},{1,29},{... | collective-permute-start | bytes 61448 | tf_op jit(solution)/shard_map/ppermute | solution.py:332
  42.8 0.0 collective-permute-start.6
  42.8 0.6 %slice.25.refs_0_ = f32[1,80,128]{2,1,0:T(8,128)} slice(f32[3,80,128]{2,1,0:T(8,128)S(1)} %get-tuple-element.19), slice={[0:1], [0:80], [0:128]} | slice | bytes 81920 | tf_op jit(solution)/shard_map/slice | solution.py:414
  43.4 0.9 %collective-permute-done.7.refs_2_ = bf16[1,80,128]{2,1,0:T(8,128)(2,1)S(1)} collective-permute-done((bf16[1,80,128]{2,1,0:T(8,128)(2,1)S(1)}, bf16[1,80,128]{2,1,0:T(8,128)(2,1)S(1)}, u32[]{:S(2)}, u32[]{:S(2)}) %collective-permute-start.7) | collective-permute-done | bytes 20512 | tf_op jit(solution)/shard_map/ppermute | solution.py:332
  44.2 0.0 copy-start.4
  44.2 5.0 %collective-permute-done.6.refs_1_ = bf16[1,80,128]{2,1,0:T(8,128)(2,1)S(1)} collective-permute-done((bf16[1,80,128]{2,1,0:T(8,128)(2,1)S(1)}, bf16[1,80,128]{2,1,0:T(8,128)(2,1)S(1)}, u32[]{:S(2)}, u32[]{:S(2)}) %collective-permute-start.6) | collective-permute-done | bytes 20512 | tf_op jit(solution)/shard_map/ppermute | solution.py:332
  49.2 0.0 copy-start.5
  49.2 0.0 copy-done.4
  49.2 0.6 %copy-done.5 = bf16[1,80,128]{2,1,0:T(8,128)(2,1)} copy-done((bf16[1,80,128]{2,1,0:T(8,128)(2,1)}, bf16[1,80,128]{2,1,0:T(8,128)(2,1)S(1)}, u32[]{:S(2)}) %copy-start.5) | copy-done | bytes 20504
  49.8 1.8 %finish.1 = (f32[1,1,1,3,128]{4,3,2,1,0:T(4,128)}, bf16[1,1,1,128,256]{4,3,2,1,0:T(8,128)(2,1)}) custom-call(f32[1,80,128]{2,1,0:T(8,128)} %slice.25.refs_0_, bf16[1,80,128]{2,1,0:T(8,128)(2,1)} %copy-done.5, bf16[1,80,128]{2,1,0:T(8,128)(2,1)} %copy-done.4, f32[128,256]{1,0:T(8,128)} %get-tuple-element.12.refs_3_, bf16[256,64]{1,0:T(8,128)(2,1)} %copy.16.w_env_ref.refs_4_), custom_call_target="tpu_custom_call" | custom-call | tf_op jit(solution)/shard_map/finish/pallas_call | solution.py:416
  51.7 1.2 %copy.18 = f32[1,1,1,3,128]{4,2,3,1,0:T(1,128)} copy(f32[1,1,1,3,128]{4,3,2,1,0:T(4,128)} %get-tuple-element.16) | data formatting | bytes 3072
  (4 shorter events, 0.0 us)
Async XLA Ops:
  0.6 0.7 %copy-start.7 = (f32[1,1,1,3,128]{4,2,3,1,0:T(1,128)S(1)}, f32[1,1,1,3,128]{4,2,3,1,0:T(1,128)}, u32[]{:S(2)}) copy-start(f32[1,1,1,3,128]{4,2,3,1,0:T(1,128)} %param.13) | copy-start | bytes 4612
  5.1 7.1 %copy-start.1 = (bf16[1,80,128]{2,1,0:T(8,128)(2,1)S(1)}, bf16[1,80,128]{2,1,0:T(8,128)(2,1)}, u32[]{:S(2)}) copy-start(bf16[1,80,128]{2,1,0:T(8,128)(2,1)} %pack.1) | copy-start | bytes 61444
  5.1 1.5 %collective-permute-start = (bf16[1,80,128]{2,1,0:T(8,128)(2,1)}, bf16[1,80,128]{2,1,0:T(8,128)(2,1)S(1)}, u32[]{:S(2)}, u32[]{:S(2)}) collective-permute-start(bf16[1,80,128]{2,1,0:T(8,128)(2,1)} %pack.1), channel_id=1, source_target_pairs={{0,2},{2,0},{1,3},{3,1},{4,6},{6,4},{5,7},{7,5},{8,10},{10,8},{9,1... | collective-permute-start | bytes 61448 | tf_op jit(solution)/shard_map/ppermute | solution.py:332
  7.3 10.0 %copy-start.6 = (f32[6,6]{1,0:T(8,128)S(1)}, f32[6,6]{1,0:T(8,128)}, u32[]{:S(2)}) copy-start(f32[6,6]{1,0:T(8,128)} %param.19) | copy-start | bytes 436
  7.4 4.8 %collective-permute-start.1 = (bf16[2,80,128]{2,1,0:T(8,128)(2,1)S(1)}, bf16[2,80,128]{2,1,0:T(8,128)(2,1)S(1)}, u32[]{:S(2)}, u32[]{:S(2)}) collective-permute-start(bf16[2,80,128]{2,1,0:T(8,128)(2,1)S(1)} %pad_maximum_fusion.1), channel_id=1, source_target_pairs={{0,1},{1,0},{2,3},{3,2},{4,5},{5,4},{6,7},{7,6},{8,9},{9,8},{10,11... | collective-permute-start | bytes 122888 | tf_op jit(solution)/shard_map/ppermute | solution.py:332
  12.2 7.6 %copy-start = (bf16[4,80,128]{2,1,0:T(8,128)(2,1)}, bf16[4,80,128]{2,1,0:T(8,128)(2,1)S(1)}, u32[]{:S(2)}) copy-start(bf16[4,80,128]{2,1,0:T(8,128)(2,1)S(1)} %pad_maximum_fusion.refs_1_) | copy-start | bytes 245764
  12.2 7.6 %collective-permute-start.3 = (bf16[4,80,128]{2,1,0:T(8,128)(2,1)S(1)}, bf16[4,80,128]{2,1,0:T(8,128)(2,1)S(1)}, u32[]{:S(2)}, u32[]{:S(2)}) collective-permute-start(bf16[4,80,128]{2,1,0:T(8,128)(2,1)S(1)} %pad_maximum_fusion.refs_1_), channel_id=1, source_target_pairs={{0,4},{4,8},{8,12},{12,16},{16,20},{20,24},{24,28},{28,0},{1,5},{5... | collective-permute-start | bytes 245768 | tf_op jit(solution)/shard_map/ppermute | solution.py:332
  14.3 5.5 %collective-permute-start.2 = (bf16[4,80,128]{2,1,0:T(8,128)(2,1)S(1)}, bf16[4,80,128]{2,1,0:T(8,128)(2,1)S(1)}, u32[]{:S(2)}, u32[]{:S(2)}) collective-permute-start(bf16[4,80,128]{2,1,0:T(8,128)(2,1)S(1)} %pad_maximum_fusion.refs_1_), channel_id=1, source_target_pairs={{0,28},{4,0},{8,4},{12,8},{16,12},{20,16},{24,20},{28,24},{1,29},{... | collective-permute-start | bytes 245768 | tf_op jit(solution)/shard_map/ppermute | solution.py:332
  19.8 0.6 %copy-start.2 = (bf16[4,80,128]{2,1,0:T(8,128)(2,1)}, bf16[4,80,128]{2,1,0:T(8,128)(2,1)S(1)}, u32[]{:S(2)}) copy-start(bf16[4,80,128]{2,1,0:T(8,128)(2,1)S(1)} %collective-permute-done.3.refs_3_) | copy-start | bytes 245764
  19.8 0.7 %copy-start.3 = (bf16[4,80,128]{2,1,0:T(8,128)(2,1)}, bf16[4,80,128]{2,1,0:T(8,128)(2,1)S(1)}, u32[]{:S(2)}) copy-start(bf16[4,80,128]{2,1,0:T(8,128)(2,1)S(1)} %collective-permute-done.2.refs_2_) | copy-start | bytes 245764
  30.7 1.5 %collective-permute-start.4 = (bf16[6,80,128]{2,1,0:T(8,128)(2,1)}, bf16[6,80,128]{2,1,0:T(8,128)(2,1)S(1)}, u32[]{:S(2)}, u32[]{:S(2)}) collective-permute-start(bf16[6,80,128]{2,1,0:T(8,128)(2,1)} %get-tuple-element.11), channel_id=1, source_target_pairs={{0,2},{2,0},{1,3},{3,1},{4,6},{6,4},{5,7},{7,5},{8,10},{10,8},{9,1... | collective-permute-start | bytes 368648 | tf_op jit(solution)/shard_map/ppermute | solution.py:332
  33.2 4.3 %collective-permute-start.5 = (bf16[3,80,128]{2,1,0:T(8,128)(2,1)S(1)}, bf16[3,80,128]{2,1,0:T(8,128)(2,1)S(1)}, u32[]{:S(2)}, u32[]{:S(2)}) collective-permute-start(bf16[3,80,128]{2,1,0:T(8,128)(2,1)S(1)} %slice.30), channel_id=1, source_target_pairs={{0,1},{1,0},{2,3},{3,2},{4,5},{5,4},{6,7},{7,6},{8,9},{9,8},{10,11... | collective-permute-start | bytes 184328 | tf_op jit(solution)/shard_map/ppermute | solution.py:332
  37.5 6.7 %collective-permute-start.7 = (bf16[1,80,128]{2,1,0:T(8,128)(2,1)S(1)}, bf16[1,80,128]{2,1,0:T(8,128)(2,1)S(1)}, u32[]{:S(2)}, u32[]{:S(2)}) collective-permute-start(bf16[1,80,128]{2,1,0:T(8,128)(2,1)S(1)} %get-tuple-element.20), channel_id=1, source_target_pairs={{0,28},{4,0},{8,4},{12,8},{16,12},{20,16},{24,20},{28,24},{1,29},{... | collective-permute-start | bytes 61448 | tf_op jit(solution)/shard_map/ppermute | solution.py:332
  42.8 6.5 %collective-permute-start.6 = (bf16[1,80,128]{2,1,0:T(8,128)(2,1)S(1)}, bf16[1,80,128]{2,1,0:T(8,128)(2,1)S(1)}, u32[]{:S(2)}, u32[]{:S(2)}) collective-permute-start(bf16[1,80,128]{2,1,0:T(8,128)(2,1)S(1)} %get-tuple-element.21), channel_id=1, source_target_pairs={{0,4},{4,8},{8,12},{12,16},{16,20},{20,24},{24,28},{28,0},{1,5},{5... | collective-permute-start | bytes 61448 | tf_op jit(solution)/shard_map/ppermute | solution.py:332
  44.2 5.0 %copy-start.4 = (bf16[1,80,128]{2,1,0:T(8,128)(2,1)}, bf16[1,80,128]{2,1,0:T(8,128)(2,1)S(1)}, u32[]{:S(2)}) copy-start(bf16[1,80,128]{2,1,0:T(8,128)(2,1)S(1)} %collective-permute-done.7.refs_2_) | copy-start | bytes 61444
  49.2 0.6 %copy-start.5 = (bf16[1,80,128]{2,1,0:T(8,128)(2,1)}, bf16[1,80,128]{2,1,0:T(8,128)(2,1)S(1)}, u32[]{:S(2)}) copy-start(bf16[1,80,128]{2,1,0:T(8,128)(2,1)S(1)} %collective-permute-done.6.refs_1_) | copy-start | bytes 61444

commit v2 on v1

--- a/solution.py
+++ b/solution.py
@@ -43,16 +43,12 @@
 
 
 def pack_kernel(counts_ref, feats_ref, pos_ref, species_ref, w_env_ref, msg_ref):
-    chans = lax.dot_general(
-        w_env_ref[...],
-        feats_ref[0, 0, 0],
-        (((0,), (1,)), ((), ())),
-        preferred_element_type=F32,
-    )
+    chans = dot_nt(w_env_ref[...], feats_ref[0, 0, 0])
     msg_ref[0, :CHANNELS] = chans.astype(BF16)
-    pos = pos_ref[0, 0, 0]
+    pos = jnp.concatenate([pos_ref[0, 0, axis] for axis in range(3)], axis=0)
     slots = lax.broadcasted_iota(jnp.int32, (1, SLOTS), 1)
-    code = jnp.where(slots < counts_ref[0, 0, 0], species_ref[0, 0].astype(F32), -1.0)
+    counts = jnp.broadcast_to(counts_ref[0], (1, SLOTS))
+    code = jnp.where(slots < counts, species_ref[0, 0].astype(F32), -1.0)
     high = pos.astype(BF16).astype(F32)
     middle = (pos - high).astype(BF16).astype(F32)
     low = pos - high - middle
@@ -61,9 +57,9 @@
 
 
 def unique_of(offset, count):
-    if count == 2:
-        return jnp.where(offset == 0, 0, 1)
-    return jnp.where(offset == 0, 0, jnp.where(offset > 0, 1, 2))
+    if offset == 0 or count == 2:
+        return abs(offset)
+    return 1 if offset > 0 else 2
 
 
 def main_kernel(shape, *refs):
@@ -77,16 +73,24 @@
     energy_ref, direct_ref = refs[:2]
     out_refs = refs[2 : 2 + nyu]
     (
-        order, xi, weight, xj, chan, tiles, rmat, s_all, r_all, wb_all,
+        cell_of, slot_of, shift_of, xi, weight, xj, chan, tiles, rmat, s_all, r_all, wb_all,
         acc, pbuf, grad, gradt, fi, cg, pg,
     ) = refs[2 + nyu :]
 
-    def count_listed(index, found):
-        order[found] = index
-        return found + list_ref[0, 0, 0, index]
-
-    live = lax.fori_loop(0, OFFSETS, count_listed, jnp.int32(0))
-    order[live] = jnp.int32(OFFSETS)
+    live = jnp.int32(0)
+    for tile in range(OFFSETS):
+        offset = (tile // 9 - 1, tile // 3 % 3 - 1, tile % 3 - 1)
+        ux, uy, uz = [unique_of(o, size) for o, size in zip(offset, sizes)]
+        cell = (ux * nzu + uz) * nyu + uy
+        cell_of[live] = jnp.int32(cell)
+        slot_of[live] = jnp.int32(cell)
+        for axis in range(3):
+            shift_of[axis, live] = jnp.float32(offset[axis] / CUTOFF)
+        live = live + list_ref[0, 0, 0, tile]
+    cell_of[live] = jnp.int32(0)
+    slot_of[live] = jnp.int32(cells)
+    for axis in range(3):
+        shift_of[axis, live] = jnp.float32(0.0)
     trips = (live + 1) // 2
 
     code_rows = []
@@ -108,7 +112,7 @@
     sub = lax.broadcasted_iota(jnp.int32, (SLOTS, SLOTS), 0)
     onehot = jnp.where((code_i == (lane % 8).astype(F32)) & (lane < 24), 1.0, 0.0)
     onehot = onehot.astype(BF16)
-    scale = scale_ref[...]
+    scale = jnp.concatenate([scale_ref[...], jnp.zeros((8 - NSPEC, NSPEC), F32)], axis=0)
     coef = []
     for cell in range(cells):
         total = jnp.zeros((8, SLOTS), F32)
@@ -121,43 +125,30 @@
         coef.append(
             jnp.concatenate([high, middle, low, jnp.zeros((104, SLOTS), F32)], axis=0).astype(BF16)
         )
-    for cell in range(cells):
-        strength = dot_nn(onehot, coef[cell])
-        if cell == 0:
-            strength = jnp.where(lane == sub, 0.0, strength)
-        weight[cell] = strength
+    for cell in range(0, cells, 2):
+        strength = dot_nn(onehot, jnp.concatenate(coef[cell : cell + 2], axis=1))
+        first = strength[:, :SLOTS]
+        weight[cell] = jnp.where(lane == sub, 0.0, first) if cell == 0 else first
+        if cell + 1 < cells:
+            weight[cell + 1] = strength[:, SLOTS:]
     weight[cells] = jnp.zeros((SLOTS, SLOTS), F32)
     acc[...] = jnp.zeros_like(acc)
     fi[...] = jnp.zeros_like(fi)
 
-    def place_of(tile):
-        real = tile < OFFSETS
-        held = jnp.where(real, tile, 13)
-        ox = held // 9 - 1
-        oy = held // 3 % 3 - 1
-        oz = held % 3 - 1
-        ux = unique_of(ox, sizes[0])
-        uy = unique_of(oy, sizes[1])
-        uz = unique_of(oz, sizes[2])
-        cell = (ux * nzu + uz) * nyu + uy
-        shifts = [o.astype(F32) * (1.0 / CUTOFF) for o in (ox, oy, oz)]
-        return cell, jnp.where(real, cell, cells), shifts
-
     def rows_of(pair):
-        first, second = order[2 * pair], order[2 * pair + 1]
-        cell_a, weight_a, shift_a = place_of(first)
-        cell_b, weight_b, shift_b = place_of(second)
+        first, second = 2 * pair, 2 * pair + 1
+        cell_a, cell_b = cell_of[first], cell_of[second]
         rows = [
             jnp.concatenate(
                 [
-                    xj[cell_a, axis : axis + 1] + shift_a[axis],
-                    xj[cell_b, axis : axis + 1] + shift_b[axis],
+                    xj[cell_a, axis : axis + 1] + shift_of[axis, first],
+                    xj[cell_b, axis : axis + 1] + shift_of[axis, second],
                 ],
                 axis=1,
             )
             for axis in range(3)
         ]
-        return cell_a, cell_b, weight_a, weight_b, rows
+        return cell_a, cell_b, slot_of[first], slot_of[second], rows
 
     def relative(rows, block):
         out = []
@@ -243,26 +234,27 @@
             base = block * 4 * CHUNK + k * CHUNK
             scaled = weights_k[k] * piece
             grad[base : base + CHUNK] = scaled.astype(BF16)
-            pbuf[base : base + CHUNK] = scaled
-    for step in range(QUAD // SLOTS):
-        for half in range(WIDE // SLOTS):
-            lanes = slice(half * SLOTS, (half + 1) * SLOTS)
-            rows = slice(step * SLOTS, (step + 1) * SLOTS)
-            gradt[lanes, rows] = pbuf[rows, lanes].T.astype(BF16)
+    place = lax.broadcasted_iota(jnp.int32, (WIDE, WIDE), 0)
+    held = place % CHUNK + place // (4 * CHUNK) * CHUNK + place // CHUNK % 4 * CHANNELS
+    picked = lax.broadcasted_iota(jnp.int32, (WIDE, WIDE), 1) == held
+    gradt[...] = dot_nt(jnp.where(picked, 1.0, 0.0).astype(BF16), grad[...]).astype(BF16)
 
     def backward(pair, carry):
         cell_a, cell_b, weight_a, weight_b, rows = rows_of(pair)
         pbuf[...] = dot_nn(grad[...], rmat[pair])
         back = dot_nn(gradt[...], tiles[pair])
-        values = rmat[pair, :CHANNELS].astype(F32)
-        sums = back[:CHANNELS]
-        along = []
-        for axis in range(3):
-            part = back[(axis + 1) * CHANNELS : (axis + 2) * CHANNELS]
-            sums = sums + rows[axis] * part
-            along.append(jnp.sum(values * part, axis=0, keepdims=True))
-        cg[cell_a] += sums[:, :SLOTS]
-        cg[cell_b] += sums[:, SLOTS:]
+        along = [jnp.zeros((CHUNK, LANES), F32) for _ in range(3)]
+        for part in range(CHANNELS // CHUNK):
+            at = slice(part * CHUNK, (part + 1) * CHUNK)
+            values = rmat[pair, at].astype(F32)
+            sums = back[part * 4 * CHUNK : part * 4 * CHUNK + CHUNK]
+            for axis in range(3):
+                base = part * 4 * CHUNK + (axis + 1) * CHUNK
+                piece = back[base : base + CHUNK]
+                sums = sums + rows[axis] * piece
+                along[axis] = along[axis] + values * piece
+            cg[cell_a, at] += sums[:, :SLOTS]
+            cg[cell_b, at] += sums[:, SLOTS:]
         totals = [jnp.zeros((CHUNK, LANES), F32) for _ in range(3)]
         for block in range(CHUNKS):
             at = slice(block * CHUNK, (block + 1) * CHUNK)
@@ -284,7 +276,7 @@
                 totals[axis] = totals[axis] + push
                 fi[axis, at] += push[:, :SLOTS] + push[:, SLOTS:]
         for axis in range(3):
-            total = jnp.sum(totals[axis], axis=0, keepdims=True) * 2.0 + along[axis]
+            total = jnp.sum(totals[axis] * 2.0 + along[axis], axis=0, keepdims=True)
             pg[cell_a, axis : axis + 1] += total[:, :SLOTS]
             pg[cell_b, axis : axis + 1] += total[:, SLOTS:]
         return carry
@@ -321,10 +313,11 @@
     low = (chan - high.astype(F32)).astype(BF16)
     both = jnp.concatenate([high, low], axis=0)
     w_env = w_env_ref[...]
-    weights = jnp.concatenate([w_env, w_env], axis=1)
-    part = lax.dot_general(both, weights, (((0,), (1,)), ((), ())), preferred_element_type=F32)
+    weights = jnp.concatenate([w_env, w_env], axis=0)
+    part = lax.dot_general(both, weights, (((0,), (0,)), ((), ())), preferred_element_type=F32)
     grad_ref[0, 0, 0] = (direct_ref[...] + part).astype(BF16)
-    force_ref[0, 0, 0] = -total[POS_ROW : POS_ROW + 3]
+    for axis in range(3):
+        force_ref[0, 0, axis] = -total[POS_ROW + axis : POS_ROW + axis + 1]
 
 
 def shifted(value, axis, steps):
@@ -346,6 +339,7 @@
 
 VMEM = pl.BlockSpec(memory_space=pltpu.VMEM)
 SMEM = pl.BlockSpec(memory_space=pltpu.SMEM)
+SMALL = pltpu.CompilerParams(vmem_limit_bytes=4 << 20)
 
 
 def local(
@@ -358,15 +352,14 @@
     msg = pl.pallas_call(
         pack_kernel,
         out_shape=jax.ShapeDtypeStruct((1, ROWS, SLOTS), BF16),
-        in_specs=[SMEM, VMEM, VMEM, VMEM, VMEM],
+        in_specs=[VMEM] * 5,
         out_specs=VMEM,
         name="pack",
-    )(cell_counts, feats, positions, species, w_env)
+    )(cell_counts, feats, positions.transpose(0, 1, 3, 2, 4), species, w_env.T)
     block = jnp.concatenate(gathered(msg, "gy"), axis=0)
     block = jnp.concatenate(gathered(block, "gz"), axis=0)
     blocks = gathered(block, "gx")
 
-    scale = jnp.pad(pair_scale, ((0, 2), (0, 2)))
     out_cells = nxu * nzu
     out_shape = [
         jax.ShapeDtypeStruct((1, 1, 1, SLOTS), F32),
@@ -375,6 +368,8 @@
     ] + [jax.ShapeDtypeStruct((out_cells, ROWS, SLOTS), BF16)] * (nyu - 1)
     scratch = [
         pltpu.SMEM((OFFSETS + 5,), jnp.int32),
+        pltpu.SMEM((OFFSETS + 5,), jnp.int32),
+        pltpu.SMEM((3, OFFSETS + 5), F32),
         pltpu.VMEM((3, SLOTS, SLOTS), F32),
         pltpu.VMEM((cells + 1, SLOTS, SLOTS), F32),
         pltpu.VMEM((cells, 8, SLOTS), F32),
@@ -398,9 +393,10 @@
         in_specs=[SMEM] + [VMEM] * (nxu + 7),
         out_specs=[VMEM] * len(out_shape),
         scratch_shapes=scratch,
+        compiler_params=pltpu.CompilerParams(vmem_limit_bytes=24 << 20),
         name="pairs",
     )(
-        pair_list, *blocks, feats, radial, scale, w_hidden, w_zero, w_one, w_out.reshape(1, D)
+        pair_list, *blocks, feats, radial, pair_scale, w_hidden, w_zero, w_one, w_out.reshape(1, D)
     )
     energy, direct, keep = results[:3]
     total = keep
@@ -416,14 +412,15 @@
     forces, feat_grad = pl.pallas_call(
         lambda *refs: finish_kernel(len(arrived), *refs),
         out_shape=[
-            jax.ShapeDtypeStruct((1, 1, 1, 3, SLOTS), F32),
+            jax.ShapeDtypeStruct((1, 1, 3, 1, SLOTS), F32),
             jax.ShapeDtypeStruct((1, 1, 1, SLOTS, D), BF16),
         ],
         in_specs=[VMEM] * (3 + len(arrived)),
         out_specs=[VMEM] * 2,
+        compiler_params=SMALL,
         name="finish",
-    )(keep, *arrived, direct, w_env)
-    return energy, forces, feat_grad
+    )(keep, *arrived, direct, w_env.T)
+    return energy, forces.transpose(0, 1, 3, 2, 4), feat_grad
 
 
 def solution(mesh):

time: 53.7 us -> 45.1 us (0.84); the launches traced: 52.9 us -> 44.8 us
  local copies, waits for them, and re-layouts: 5.8 us -> 0.06 us
  Pallas kernels: 13.7 us -> 10.9 us
  starting transfers between devices: 14.7 us -> 15.3 us
    unnamed x19 -> x18, local copies, waits for them, and re-layouts: 4.58 us -> 0.04 us
    pallas_call x1, Pallas kernels: 10.2 us -> 8.47 us  [local(): pl.pallas_call(lambda *refs: main_kernel((nxu, nyu, nzu, sizes), *refs),...]
    pallas_call x1, Pallas kernels: 1.83 us -> 0.84 us  [local(): pl.pallas_call(lambda *refs: finish_kernel(len(arrived), *refs), out_shap...]
    add x1, other arithmetic: 0.97 us -> 0.02 us  [local(): total = total + got.astype(F32)]
    concatenate x1, other arithmetic: 0.01 us -> 0.76 us  [local(): block = jnp.concatenate(gathered(block, 'gz'), axis=0)]
    ppermute x8, starting transfers between devices: 14.7 us -> 15.3 us  [shifted(): lax.ppermute(value, axis, [(i, (i + steps) % count) for i in range(count)])]
    slice x1, local copies, waits for them, and re-layouts: 0.62 us -> 0.01 us  [local(): keep = total[:1]]
    pad x1 -> x0, local copies, waits for them, and re-layouts: 0.6 us -> none  [local(): scale = jnp.pad(pair_scale, ((0, 2), (0, 2)))]
  transfers between devices with their start and end apart: 8 -> 8, of which waited for: 7 -> 7; matrix products, arithmetic and copies ran while one was open for 2% -> 0% of each run, Pallas kernels for 0% -> 0%
where the time goes in v2:
time: 45.1 us; the launch traced here: 44.8 us
  waiting for transfers between devices  15.6 us (35%)
  starting transfers between devices  15.3 us (34%)
  Pallas kernels  10.9 us (24%)
  other arithmetic  1.54 us (3%)
  between operations  1.4 us (3%)
    ppermute x8, waiting for transfers between devices, shifted(): lax.ppermute(value, axis, [(i, (i + steps) % count) for i in range(count)])  15.6 us
    ppermute x8, starting transfers between devices, shifted(): lax.ppermute(value, axis, [(i, (i + steps) % count) for i in range(count)])  15.3 us
    pallas_call x1, Pallas kernels, local(): pl.pallas_call(lambda *refs: main_kernel((nxu, nyu, nzu, sizes), *refs),...  8.47 us
    pallas_call x1, Pallas kernels, local(): pl.pallas_call(pack_kernel, out_shape=jax.ShapeDtypeStruct((1, ROWS, SLOT...  1.63 us
  transfers between devices with their start and end apart: 8, of which 7 were waited for; matrix products, arithmetic and copies ran while one was open for 0% of the time, Pallas kernels for 0%

profile of v2, /device:TPU:0, one launch (start us, length us, event | category | flops | bytes accessed | tf_op | source)
XLA Modules:
  0.0 44.8 jit_solution(10692723603041679532)
XLA Ops:
  1.3 0.0 copy-start.4
  1.3 1.6 %pack.1 = bf16[1,80,128]{2,1,0:T(8,128)(2,1)} custom-call(s32[1,1,1]{2,1,0:T(1,128)S(6)} %copy.16.counts_ref, bf16[1,1,1,128,256]{4,3,2,1,0:T(8,128)(2,1)} %refs_4_.1, f32[1,1,3,1,128]{4,3,2,1,0:T(1,128)} %bitcast.9, s32[1,1,1,128]{3,2,1,0:T(1,128)} %species_ref.1, bf16[64,256]{1,0:T(8,128)(2,1)} %bitcast.6), custom_call_target="tpu_custom_call" | custom-call | tf_op jit(solution)/shard_map/pack/pallas_call | solution.py:352
  2.9 0.0 copy-start.1
  2.9 0.5 %collective-permute-start = (bf16[1,80,128]{2,1,0:T(8,128)(2,1)}, bf16[1,80,128]{2,1,0:T(8,128)(2,1)S(1)}, u32[]{:S(2)}, u32[]{:S(2)}) collective-permute-start(bf16[1,80,128]{2,1,0:T(8,128)(2,1)} %pack.1), channel_id=1, source_target_pairs={{0,2},{2,0},{1,3},{3,1},{4,6},{6,4},{5,7},{7,5},{8,10},{10,8},{9,1... | collective-permute-start | bytes 61448 | tf_op jit(solution)/shard_map/ppermute | solution.py:325
  3.4 1.1 %collective-permute-done = bf16[1,80,128]{2,1,0:T(8,128)(2,1)S(1)} collective-permute-done((bf16[1,80,128]{2,1,0:T(8,128)(2,1)}, bf16[1,80,128]{2,1,0:T(8,128)(2,1)S(1)}, u32[]{:S(2)}, u32[]{:S(2)}) %collective-permute-start) | collective-permute-done | bytes 20512 | tf_op jit(solution)/shard_map/ppermute | solution.py:325
  4.5 0.7 %pad_maximum_fusion.1 = bf16[2,80,128]{2,1,0:T(8,128)(2,1)S(1)} fusion(bf16[1,80,128]{2,1,0:T(8,128)(2,1)S(1)} %collective-permute-done, bf16[1,80,128]{2,1,0:T(8,128)(2,1)} %pack.1), kind=kLoop, calls=%fused_computation.4 | loop fusion | flops 20480 | bytes 81920 | tf_op jit(solution)/shard_map/concatenate | solution.py:359
  5.2 0.0 copy-start
  5.2 0.0 copy-start.3
  5.2 2.9 %collective-permute-start.1 = (bf16[2,80,128]{2,1,0:T(8,128)(2,1)S(1)}, bf16[2,80,128]{2,1,0:T(8,128)(2,1)S(1)}, u32[]{:S(2)}, u32[]{:S(2)}) collective-permute-start(bf16[2,80,128]{2,1,0:T(8,128)(2,1)S(1)} %pad_maximum_fusion.1), channel_id=1, source_target_pairs={{0,1},{1,0},{2,3},{3,2},{4,5},{5,4},{6,7},{7,6},{8,9},{9,8},{10,11... | collective-permute-start | bytes 122888 | tf_op jit(solution)/shard_map/ppermute | solution.py:325
  8.1 2.0 %collective-permute-done.1 = bf16[2,80,128]{2,1,0:T(8,128)(2,1)S(1)} collective-permute-done((bf16[2,80,128]{2,1,0:T(8,128)(2,1)S(1)}, bf16[2,80,128]{2,1,0:T(8,128)(2,1)S(1)}, u32[]{:S(2)}, u32[]{:S(2)}) %collective-permute-start.1) | collective-permute-done | bytes 40992 | tf_op jit(solution)/shard_map/ppermute | solution.py:325
  10.1 0.0 copy-start.5
  10.1 0.0 copy-start.6
  10.1 0.8 %pad_maximum_fusion.refs_1_ = bf16[4,80,128]{2,1,0:T(8,128)(2,1)S(1)} fusion(bf16[2,80,128]{2,1,0:T(8,128)(2,1)S(1)} %collective-permute-done.1, bf16[1,80,128]{2,1,0:T(8,128)(2,1)S(1)} %collective-permute-done, bf16[1,80,128]{2,1,0:T(8,128)(2,1)} %pack.1), kind=kLoop, calls=%fused_computation.3 | loop fusion | flops 81920 | bytes 163840 | tf_op jit(solution)/shard_map/concatenate | solution.py:360
  10.9 0.0 copy-start.7
  10.9 0.0 copy-start.8
  10.9 2.0 %collective-permute-start.3 = (bf16[4,80,128]{2,1,0:T(8,128)(2,1)S(1)}, bf16[4,80,128]{2,1,0:T(8,128)(2,1)S(1)}, u32[]{:S(2)}, u32[]{:S(2)}) collective-permute-start(bf16[4,80,128]{2,1,0:T(8,128)(2,1)S(1)} %pad_maximum_fusion.refs_1_), channel_id=1, source_target_pairs={{0,4},{4,8},{8,12},{12,16},{16,20},{20,24},{24,28},{28,0},{1,5},{5... | collective-permute-start | bytes 245768 | tf_op jit(solution)/shard_map/ppermute | solution.py:325
  12.9 3.1 %collective-permute-start.2 = (bf16[4,80,128]{2,1,0:T(8,128)(2,1)S(1)}, bf16[4,80,128]{2,1,0:T(8,128)(2,1)S(1)}, u32[]{:S(2)}, u32[]{:S(2)}) collective-permute-start(bf16[4,80,128]{2,1,0:T(8,128)(2,1)S(1)} %pad_maximum_fusion.refs_1_), channel_id=1, source_target_pairs={{0,28},{4,0},{8,4},{12,8},{16,12},{20,16},{24,20},{28,24},{1,29},{... | collective-permute-start | bytes 245768 | tf_op jit(solution)/shard_map/ppermute | solution.py:325
  16.0 2.4 %collective-permute-done.3.refs_3_ = bf16[4,80,128]{2,1,0:T(8,128)(2,1)S(1)} collective-permute-done((bf16[4,80,128]{2,1,0:T(8,128)(2,1)S(1)}, bf16[4,80,128]{2,1,0:T(8,128)(2,1)S(1)}, u32[]{:S(2)}, u32[]{:S(2)}) %collective-permute-start.3) | collective-permute-done | bytes 81952 | tf_op jit(solution)/shard_map/ppermute | solution.py:325
  18.5 0.0 collective-permute-done.2.refs_2_
  18.5 0.0 copy-done.4
  18.5 0.0 copy-done.1
  18.5 0.0 copy-done
  18.5 0.0 copy-done.3
  18.5 0.0 copy-done.5
  18.5 0.0 copy-done.6
  18.5 0.0 copy-done.7
  18.5 0.0 copy-done.8
  18.5 8.5 %pairs.1 = (f32[1,1,1,128]{3,2,1,0:T(1,128)}, f32[128,256]{1,0:T(8,128)S(1)}, f32[6,80,128]{2,1,0:T(8,128)S(1)}, bf16[6,80,128]{2,1,0:T(8,128)(2,1)S(1)}) custom-call(s32[1,1,1,27]{3,2,1,0:T(1,128)S(1)} %copy-done.8, bf16[4,80,128]{2,1,0:T(8,128)(2,1)S(1)} %pad_maximum_fusion.refs_1_, bf16[4,80,128]{2,1,0:T(8,128)(2,1)S(1)} %collective-permute-done.2.refs_2_, ...), custom_call_target="tpu_custom_call" | custom-call | tf_op jit(solution)/shard_map/pairs/pallas_call | solution.py:390
  27.0 0.0 collective-permute-start.4
  27.0 1.3 %collective-permute-done.4 = bf16[6,80,128]{2,1,0:T(8,128)(2,1)S(1)} collective-permute-done((bf16[6,80,128]{2,1,0:T(8,128)(2,1)S(1)}, bf16[6,80,128]{2,1,0:T(8,128)(2,1)S(1)}, u32[]{:S(2)}, u32[]{:S(2)}) %collective-permute-start.4) | collective-permute-done | bytes 122912 | tf_op jit(solution)/shard_map/ppermute | solution.py:325
  28.4 3.0 %collective-permute-start.5 = (bf16[3,80,128]{2,1,0:T(8,128)(2,1)S(1)}, bf16[3,80,128]{2,1,0:T(8,128)(2,1)S(1)}, u32[]{:S(2)}, u32[]{:S(2)}) collective-permute-start(bf16[3,80,128]{2,1,0:T(8,128)(2,1)S(1)} %slice.30), channel_id=1, source_target_pairs={{0,1},{1,0},{2,3},{3,2},{4,5},{5,4},{6,7},{7,6},{8,9},{9,8},{10,11... | collective-permute-start | bytes 184328 | tf_op jit(solution)/shard_map/ppermute | solution.py:325
  31.4 2.3 %collective-permute-done.5 = bf16[3,80,128]{2,1,0:T(8,128)(2,1)S(1)} collective-permute-done((bf16[3,80,128]{2,1,0:T(8,128)(2,1)S(1)}, bf16[3,80,128]{2,1,0:T(8,128)(2,1)S(1)}, u32[]{:S(2)}, u32[]{:S(2)}) %collective-permute-start.5) | collective-permute-done | bytes 61472 | tf_op jit(solution)/shard_map/ppermute | solution.py:325
  33.8 3.7 %collective-permute-start.7 = (bf16[1,80,128]{2,1,0:T(8,128)(2,1)S(1)}, bf16[1,80,128]{2,1,0:T(8,128)(2,1)S(1)}, u32[]{:S(2)}, u32[]{:S(2)}) collective-permute-start(bf16[1,80,128]{2,1,0:T(8,128)(2,1)S(1)} %get-tuple-element.20), channel_id=1, source_target_pairs={{0,28},{4,0},{8,4},{12,8},{16,12},{20,16},{24,20},{28,24},{1,29},{... | collective-permute-start | bytes 61448 | tf_op jit(solution)/shard_map/ppermute | solution.py:325
  37.5 0.0 collective-permute-start.6
  37.5 0.0 copy-start.2
  37.5 1.5 %collective-permute-done.7.refs_2_ = bf16[1,80,128]{2,1,0:T(8,128)(2,1)S(1)} collective-permute-done((bf16[1,80,128]{2,1,0:T(8,128)(2,1)S(1)}, bf16[1,80,128]{2,1,0:T(8,128)(2,1)S(1)}, u32[]{:S(2)}, u32[]{:S(2)}) %collective-permute-start.7) | collective-permute-done | bytes 20512 | tf_op jit(solution)/shard_map/ppermute | solution.py:325
  39.0 5.0 %collective-permute-done.6.refs_1_ = bf16[1,80,128]{2,1,0:T(8,128)(2,1)S(1)} collective-permute-done((bf16[1,80,128]{2,1,0:T(8,128)(2,1)S(1)}, bf16[1,80,128]{2,1,0:T(8,128)(2,1)S(1)}, u32[]{:S(2)}, u32[]{:S(2)}) %collective-permute-start.6) | collective-permute-done | bytes 20512 | tf_op jit(solution)/shard_map/ppermute | solution.py:325
  44.0 0.0 copy-done.2
  44.0 0.8 %finish.1 = (f32[1,1,3,1,128]{4,3,2,1,0:T(1,128)}, bf16[1,1,1,128,256]{4,3,2,1,0:T(8,128)(2,1)}) custom-call(f32[1,80,128]{2,1,0:T(8,128)S(1)} %slice.25.refs_0_, bf16[1,80,128]{2,1,0:T(8,128)(2,1)S(1)} %collective-permute-done.6.refs_1_, bf16[1,80,128]{2,1,0:T(8,128)(2,1)S(1)} %collective-permute-done.7.refs_2_, f32[128,256]{1,0:T(8,128)S(1)} %get-tuple-element.12.refs_3_, ...), custom_call_target="tpu_custom_call" | custom-call | tf_op jit(solution)/shard_map/finish/pallas_call | solution.py:412
  (5 shorter events, 0.1 us)
Async XLA Ops:
  1.3 17.2 %copy-start.4 = (bf16[64,256]{1,0:T(8,128)(2,1)S(1)}, bf16[64,256]{1,0:T(8,128)(2,1)}, u32[]{:S(2)}) copy-start(bf16[64,256]{1,0:T(8,128)(2,1)} %refs_9_.1) | copy-start | bytes 98308
  2.9 15.6 %copy-start.1 = (bf16[256,256]{1,0:T(8,128)(2,1)S(1)}, bf16[256,256]{1,0:T(8,128)(2,1)}, u32[]{:S(2)}) copy-start(bf16[256,256]{1,0:T(8,128)(2,1)} %refs_7_.1) | copy-start | bytes 393220
  2.9 1.5 %collective-permute-start = (bf16[1,80,128]{2,1,0:T(8,128)(2,1)}, bf16[1,80,128]{2,1,0:T(8,128)(2,1)S(1)}, u32[]{:S(2)}, u32[]{:S(2)}) collective-permute-start(bf16[1,80,128]{2,1,0:T(8,128)(2,1)} %pack.1), channel_id=1, source_target_pairs={{0,2},{2,0},{1,3},{3,1},{4,6},{6,4},{5,7},{7,5},{8,10},{10,8},{9,1... | collective-permute-start | bytes 61448 | tf_op jit(solution)/shard_map/ppermute | solution.py:325
  5.2 13.3 %copy-start = (bf16[1,1,1,128,256]{4,3,2,1,0:T(8,128)(2,1)S(1)}, bf16[1,1,1,128,256]{4,3,2,1,0:T(8,128)(2,1)}, u32[]{:S(2)}) copy-start(bf16[1,1,1,128,256]{4,3,2,1,0:T(8,128)(2,1)} %refs_4_.1) | copy-start | bytes 196612
  5.2 13.3 %copy-start.3 = (bf16[64,256]{1,0:T(8,128)(2,1)S(1)}, bf16[64,256]{1,0:T(8,128)(2,1)}, u32[]{:S(2)}) copy-start(bf16[64,256]{1,0:T(8,128)(2,1)} %refs_8_.1) | copy-start | bytes 98308
  5.2 4.9 %collective-permute-start.1 = (bf16[2,80,128]{2,1,0:T(8,128)(2,1)S(1)}, bf16[2,80,128]{2,1,0:T(8,128)(2,1)S(1)}, u32[]{:S(2)}, u32[]{:S(2)}) collective-permute-start(bf16[2,80,128]{2,1,0:T(8,128)(2,1)S(1)} %pad_maximum_fusion.1), channel_id=1, source_target_pairs={{0,1},{1,0},{2,3},{3,2},{4,5},{5,4},{6,7},{7,6},{8,9},{9,8},{10,11... | collective-permute-start | bytes 122888 | tf_op jit(solution)/shard_map/ppermute | solution.py:325
  10.1 8.4 %copy-start.5 = (f32[6,6]{1,0:T(8,128)S(1)}, f32[6,6]{1,0:T(8,128)}, u32[]{:S(2)}) copy-start(f32[6,6]{1,0:T(8,128)} %refs_6_.1) | copy-start | bytes 436
  10.1 8.4 %copy-start.6 = (f32[4,64]{1,0:T(4,128)S(1)}, f32[4,64]{1,0:T(4,128)}, u32[]{:S(2)}) copy-start(f32[4,64]{1,0:T(4,128)} %refs_5_.1) | copy-start | bytes 3076
  10.9 7.7 %copy-start.7 = (f32[256]{0:T(256)S(1)}, f32[256]{0:T(256)}, u32[]{:S(2)}) copy-start(f32[256]{0:T(256)} %param.23) | copy-start | bytes 3076
  10.9 7.7 %copy-start.8 = (s32[1,1,1,27]{3,2,1,0:T(1,128)S(1)}, s32[1,1,1,27]{3,2,1,0:T(1,128)}, u32[]{:S(2)}) copy-start(s32[1,1,1,27]{3,2,1,0:T(1,128)} %refs_0_.1) | copy-start | bytes 328
  10.9 7.6 %collective-permute-start.3 = (bf16[4,80,128]{2,1,0:T(8,128)(2,1)S(1)}, bf16[4,80,128]{2,1,0:T(8,128)(2,1)S(1)}, u32[]{:S(2)}, u32[]{:S(2)}) collective-permute-start(bf16[4,80,128]{2,1,0:T(8,128)(2,1)S(1)} %pad_maximum_fusion.refs_1_), channel_id=1, source_target_pairs={{0,4},{4,8},{8,12},{12,16},{16,20},{20,24},{24,28},{28,0},{1,5},{5... | collective-permute-start | bytes 245768 | tf_op jit(solution)/shard_map/ppermute | solution.py:325
  12.9 5.5 %collective-permute-start.2 = (bf16[4,80,128]{2,1,0:T(8,128)(2,1)S(1)}, bf16[4,80,128]{2,1,0:T(8,128)(2,1)S(1)}, u32[]{:S(2)}, u32[]{:S(2)}) collective-permute-start(bf16[4,80,128]{2,1,0:T(8,128)(2,1)S(1)} %pad_maximum_fusion.refs_1_), channel_id=1, source_target_pairs={{0,28},{4,0},{8,4},{12,8},{16,12},{20,16},{24,20},{28,24},{1,29},{... | collective-permute-start | bytes 245768 | tf_op jit(solution)/shard_map/ppermute | solution.py:325
  27.0 1.3 %collective-permute-start.4 = (bf16[6,80,128]{2,1,0:T(8,128)(2,1)S(1)}, bf16[6,80,128]{2,1,0:T(8,128)(2,1)S(1)}, u32[]{:S(2)}, u32[]{:S(2)}) collective-permute-start(bf16[6,80,128]{2,1,0:T(8,128)(2,1)S(1)} %get-tuple-element.11), channel_id=1, source_target_pairs={{0,2},{2,0},{1,3},{3,1},{4,6},{6,4},{5,7},{7,5},{8,10},{10,8},{9,1... | collective-permute-start | bytes 368648 | tf_op jit(solution)/shard_map/ppermute | solution.py:325
  28.4 5.4 %collective-permute-start.5 = (bf16[3,80,128]{2,1,0:T(8,128)(2,1)S(1)}, bf16[3,80,128]{2,1,0:T(8,128)(2,1)S(1)}, u32[]{:S(2)}, u32[]{:S(2)}) collective-permute-start(bf16[3,80,128]{2,1,0:T(8,128)(2,1)S(1)} %slice.30), channel_id=1, source_target_pairs={{0,1},{1,0},{2,3},{3,2},{4,5},{5,4},{6,7},{7,6},{8,9},{9,8},{10,11... | collective-permute-start | bytes 184328 | tf_op jit(solution)/shard_map/ppermute | solution.py:325
  33.8 5.2 %collective-permute-start.7 = (bf16[1,80,128]{2,1,0:T(8,128)(2,1)S(1)}, bf16[1,80,128]{2,1,0:T(8,128)(2,1)S(1)}, u32[]{:S(2)}, u32[]{:S(2)}) collective-permute-start(bf16[1,80,128]{2,1,0:T(8,128)(2,1)S(1)} %get-tuple-element.20), channel_id=1, source_target_pairs={{0,28},{4,0},{8,4},{12,8},{16,12},{20,16},{24,20},{28,24},{1,29},{... | collective-permute-start | bytes 61448 | tf_op jit(solution)/shard_map/ppermute | solution.py:325
  37.5 6.5 %collective-permute-start.6 = (bf16[1,80,128]{2,1,0:T(8,128)(2,1)S(1)}, bf16[1,80,128]{2,1,0:T(8,128)(2,1)S(1)}, u32[]{:S(2)}, u32[]{:S(2)}) collective-permute-start(bf16[1,80,128]{2,1,0:T(8,128)(2,1)S(1)} %get-tuple-element.21), channel_id=1, source_target_pairs={{0,4},{4,8},{8,12},{12,16},{16,20},{20,24},{24,28},{28,0},{1,5},{5... | collective-permute-start | bytes 61448 | tf_op jit(solution)/shard_map/ppermute | solution.py:325
  37.5 6.5 %copy-start.2 = (bf16[256,64]{0,1:T(8,128)(2,1)S(1)}, bf16[256,64]{0,1:T(8,128)(2,1)}, u32[]{:S(2)}) copy-start(bf16[256,64]{0,1:T(8,128)(2,1)} %param.17) | copy-start | bytes 98308

commit v3 on v2

--- a/solution.py
+++ b/solution.py
@@ -4,6 +4,7 @@
 from jax.experimental import pallas as pl
 from jax.experimental.pallas import tpu as pltpu
 from jax.sharding import PartitionSpec as P
+
 
 D = 256
 CHANNELS = 64
@@ -14,7 +15,6 @@
 CENTRE = 0.5
 ROWS = 80
 POS_ROW = 64
-CODE_ROW = 73
 OFFSETS = 27
 CHUNK = 16
 CHUNKS = SLOTS // CHUNK
@@ -56,6 +56,13 @@
     msg_ref[0, CHANNELS:] = tail.astype(BF16)
 
 
+def row_sums(value):
+    ones = jnp.ones((8, value.shape[1]), BF16)
+    high, middle, low = split3(value)
+    total = dot_nt(ones, high) + dot_nt(ones, middle) + dot_nt(ones, low)
+    return total[0:1]
+
+
 def unique_of(offset, count):
     if offset == 0 or count == 2:
         return abs(offset)
@@ -68,13 +75,15 @@
     refs = list(refs)
     list_ref = refs.pop(0)
     msg_refs = [refs.pop(0) for _ in range(nxu)]
-    (feats_ref, radial_ref, scale_ref, w_hidden_ref, w_zero_ref, w_one_ref, w_out_ref) = refs[:7]
-    refs = refs[7:]
+    (
+        feats_ref, radial_ref, scale_ref, w_hidden_ref, w_zero_ref, w_one_ref, w_out_ref, swap_ref,
+    ) = refs[:8]
+    refs = refs[8:]
     energy_ref, direct_ref = refs[:2]
     out_refs = refs[2 : 2 + nyu]
     (
         cell_of, slot_of, shift_of, xi, weight, xj, chan, tiles, rmat, s_all, r_all, wb_all,
-        acc, pbuf, grad, gradt, fi, cg, pg,
+        acc, pbuf, bbuf, hbuf, tile_now, rmat_now, grad, gradt, fi, cg, pg,
     ) = refs[2 + nyu :]
 
     live = jnp.int32(0)
@@ -92,6 +101,7 @@
     for axis in range(3):
         shift_of[axis, live] = jnp.float32(0.0)
     trips = (live + 1) // 2
+    hbuf[...] = dot_nn(feats_ref[0, 0, 0], w_hidden_ref[...])
 
     code_rows = []
     for cell in range(cells):
@@ -133,7 +143,8 @@
             weight[cell + 1] = strength[:, SLOTS:]
     weight[cells] = jnp.zeros((SLOTS, SLOTS), F32)
     acc[...] = jnp.zeros_like(acc)
-    fi[...] = jnp.zeros_like(fi)
+    tile_now[...] = jnp.zeros_like(tile_now)
+    rmat_now[...] = jnp.zeros_like(rmat_now)
 
     def rows_of(pair):
         first, second = 2 * pair, 2 * pair + 1
@@ -158,13 +169,8 @@
         return out
 
     def forward(pair, carry):
+        acc[...] += dot_nt(tile_now[...], rmat_now[...])
         cell_a, cell_b, weight_a, weight_b, rows = rows_of(pair)
-        values = jnp.concatenate([chan[cell_a], chan[cell_b]], axis=1)
-        rmat[pair, :CHANNELS] = values
-        wide = values.astype(F32)
-        for axis in range(3):
-            base = (axis + 1) * CHANNELS
-            rmat[pair, base : base + CHANNELS] = (wide * rows[axis]).astype(BF16)
         for block in range(CHUNKS):
             at = slice(block * CHUNK, (block + 1) * CHUNK)
             dx, dy, dz = relative(rows, block)
@@ -180,13 +186,24 @@
             tile = wb * (inside * inside)
             for k in range(NBASIS):
                 base = block * 4 * CHUNK + k * CHUNK
-                tiles[pair, base : base + CHUNK] = tile.astype(BF16)
+                rounded = tile.astype(BF16)
+                tiles[pair, base : base + CHUNK] = rounded
+                tile_now[base : base + CHUNK] = rounded
                 if k + 1 < NBASIS:
                     tile = tile * ratio
-        acc[...] += dot_nt(tiles[pair], rmat[pair])
+        values = jnp.concatenate([chan[cell_a], chan[cell_b]], axis=1)
+        rmat[pair, :CHANNELS] = values
+        rmat_now[:CHANNELS] = values
+        wide = values.astype(F32)
+        for axis in range(3):
+            base = (axis + 1) * CHANNELS
+            scaled = (wide * rows[axis]).astype(BF16)
+            rmat[pair, base : base + CHANNELS] = scaled
+            rmat_now[base : base + CHANNELS] = scaled
         return carry
 
     lax.fori_loop(0, trips, forward, 0)
+    acc[...] += dot_nt(tile_now[...], rmat_now[...])
 
     radial = radial_ref[...]
     weights_k = []
@@ -201,60 +218,47 @@
             total = total + weights_k[k] * acc[base + k * CHUNK : base + (k + 1) * CHUNK]
         mixed.append(total)
     mixed = jnp.concatenate(mixed, axis=0)
-    scalar = mixed[:, :CHANNELS]
-    vectors = [
-        mixed[:, (axis + 1) * CHANNELS : (axis + 2) * CHANNELS] - xi[axis][:, :CHANNELS] * scalar
-        for axis in range(3)
-    ]
-    norms = vectors[0] * vectors[0] + vectors[1] * vectors[1] + vectors[2] * vectors[2]
-    pre = dot_nn(feats_ref[0, 0, 0], w_hidden_ref[...])
-    pre = pre + dot_nn(scalar.astype(BF16), w_zero_ref[...])
-    pre = pre + dot_nn(norms.astype(BF16), w_one_ref[...])
+    low = lane < CHANNELS
+    left, right = mixed[:, :SLOTS], mixed[:, SLOTS:]
+    scalar = jnp.where(low, left, pltpu.roll(left, CHANNELS, 1))
+    own_left = jnp.where(low, 0.0, xi[0])
+    own_right = jnp.where(low, xi[1], xi[2])
+    left = left - own_left * scalar
+    right = right - own_right * scalar
+    features = [jnp.where(low, left, left * left), right * right]
+    features = jnp.concatenate(features, axis=1).astype(BF16)
+    w_one = w_one_ref[...]
+    w_all = jnp.concatenate([w_zero_ref[...], w_one, w_one, w_one], axis=0)
+    pre = hbuf[...] + dot_nn(features, w_all)
     gate = jax.nn.sigmoid(pre)
-    w_out = w_out_ref[...]
-    occupied = code_i >= 0.0
-    energy = jnp.sum(pre * gate * w_out, axis=1, keepdims=True)
-    energy = jnp.where(occupied, jnp.broadcast_to(energy, (SLOTS, SLOTS)), 0.0).T
-    energy_ref[0, 0] = energy[0:1]
-    occupied_wide = jnp.concatenate([occupied, occupied], axis=1)
-    pre_grad = jnp.where(occupied_wide, w_out * gate * (1.0 + pre * (1.0 - gate)), 0.0)
-    pre_grad = pre_grad.astype(BF16)
-    direct_ref[...] = dot_nt(pre_grad, w_hidden_ref[...])
-    zero_grad = dot_nt(pre_grad, w_zero_ref[...])
-    one_grad = 2.0 * dot_nt(pre_grad, w_one_ref[...])
-    parts = [vector * one_grad for vector in vectors]
-    own_force = [jnp.sum(part * scalar, axis=1, keepdims=True) for part in parts]
-    head = zero_grad
-    for axis in range(3):
-        head = head - xi[axis][:, :CHANNELS] * parts[axis]
-    full = jnp.concatenate([head] + parts, axis=1)
+    occupied = jnp.concatenate([code_i, code_i], axis=1) >= 0.0
+    w_out = jnp.where(occupied, w_out_ref[...], 0.0)
+    pre_grad = (w_out * gate * (1.0 + pre * (1.0 - gate))).astype(BF16)
+    back_all = dot_nt(pre_grad, w_all)
+    back_left, back_right = back_all[:, :SLOTS], back_all[:, SLOTS:]
+    part_left = jnp.where(low, back_left, 2.0 * left * back_left)
+    part_right = 2.0 * right * back_right
+    fold = own_left * part_left + own_right * part_right
+    fold = fold + pltpu.roll(fold, CHANNELS, 1)
+    full = jnp.concatenate([part_left - jnp.where(low, fold, 0.0), part_right], axis=1)
+    half = 0.5 * scalar
+    fi[0] = jnp.where(low, 0.0, half * part_left)
+    fi[1] = jnp.where(low, half * part_right, 0.0)
+    fi[2] = jnp.where(low, 0.0, half * part_right)
     for block in range(CHUNKS):
         piece = full[block * CHUNK : (block + 1) * CHUNK]
         for k in range(NBASIS):
             base = block * 4 * CHUNK + k * CHUNK
             scaled = weights_k[k] * piece
             grad[base : base + CHUNK] = scaled.astype(BF16)
-    place = lax.broadcasted_iota(jnp.int32, (WIDE, WIDE), 0)
-    held = place % CHUNK + place // (4 * CHUNK) * CHUNK + place // CHUNK % 4 * CHANNELS
-    picked = lax.broadcasted_iota(jnp.int32, (WIDE, WIDE), 1) == held
-    gradt[...] = dot_nt(jnp.where(picked, 1.0, 0.0).astype(BF16), grad[...]).astype(BF16)
+    pbuf[...] = dot_nn(grad[...], rmat[0])
+    gradt[...] = dot_nt(swap_ref[...], grad[...]).astype(BF16)
+    energy_ref[0, 0] = row_sums(pre * gate * w_out)
+    direct_ref[...] = dot_nt(pre_grad, w_hidden_ref[...])
 
     def backward(pair, carry):
-        cell_a, cell_b, weight_a, weight_b, rows = rows_of(pair)
-        pbuf[...] = dot_nn(grad[...], rmat[pair])
-        back = dot_nn(gradt[...], tiles[pair])
-        along = [jnp.zeros((CHUNK, LANES), F32) for _ in range(3)]
-        for part in range(CHANNELS // CHUNK):
-            at = slice(part * CHUNK, (part + 1) * CHUNK)
-            values = rmat[pair, at].astype(F32)
-            sums = back[part * 4 * CHUNK : part * 4 * CHUNK + CHUNK]
-            for axis in range(3):
-                base = part * 4 * CHUNK + (axis + 1) * CHUNK
-                piece = back[base : base + CHUNK]
-                sums = sums + rows[axis] * piece
-                along[axis] = along[axis] + values * piece
-            cg[cell_a, at] += sums[:, :SLOTS]
-            cg[cell_b, at] += sums[:, SLOTS:]
+        cell_a, cell_b, _, _, rows = rows_of(pair)
+        bbuf[...] = dot_nn(gradt[...], tiles[pair])
         totals = [jnp.zeros((CHUNK, LANES), F32) for _ in range(3)]
         for block in range(CHUNKS):
             at = slice(block * CHUNK, (block + 1) * CHUNK)
@@ -264,7 +268,7 @@
             step = 8.0 * inside
             level = -2.0 - step * (4.0 * s - 0.5)
             levels = [level]
-            for k in range(1, NBASIS):
+            for _ in range(1, NBASIS):
                 levels.append(levels[-1] + step)
             base = block * 4 * CHUNK
             slope = levels[3] * pbuf[base + 3 * CHUNK : base + 4 * CHUNK]
@@ -275,8 +279,21 @@
                 push = slope * delta
                 totals[axis] = totals[axis] + push
                 fi[axis, at] += push[:, :SLOTS] + push[:, SLOTS:]
+        pbuf[...] = dot_nn(grad[...], rmat[pair + 1])
+        totals = [2.0 * total for total in totals]
+        for part in range(CHANNELS // CHUNK):
+            at = slice(part * CHUNK, (part + 1) * CHUNK)
+            values = rmat[pair, at].astype(F32)
+            sums = bbuf[part * 4 * CHUNK : part * 4 * CHUNK + CHUNK]
+            for axis in range(3):
+                base = part * 4 * CHUNK + (axis + 1) * CHUNK
+                piece = bbuf[base : base + CHUNK]
+                sums = sums + rows[axis] * piece
+                totals[axis] = totals[axis] + values * piece
+            cg[cell_a, at] += sums[:, :SLOTS]
+            cg[cell_b, at] += sums[:, SLOTS:]
         for axis in range(3):
-            total = jnp.sum(totals[axis] * 2.0 + along[axis], axis=0, keepdims=True)
+            total = jnp.sum(totals[axis], axis=0, keepdims=True)
             pg[cell_a, axis : axis + 1] += total[:, :SLOTS]
             pg[cell_b, axis : axis + 1] += total[:, SLOTS:]
         return carry
@@ -284,9 +301,7 @@
     lax.fori_loop(0, trips, backward, 0)
 
     for axis in range(3):
-        column = jnp.sum(fi[axis], axis=1, keepdims=True) * 2.0 + own_force[axis]
-        row = jnp.broadcast_to(column, (SLOTS, SLOTS)).T
-        pg[0, axis : axis + 1] -= row[0:1]
+        pg[0, axis : axis + 1] -= 2.0 * row_sums(fi[axis])
     for uy in range(nyu):
         for uz in range(nzu):
             for ux in range(nxu):
@@ -328,13 +343,25 @@
 def gathered(value, axis):
     if lax.axis_size(axis) == 2:
         return [value, shifted(value, axis, 1)]
-    return [value, shifted(value, axis, -1), shifted(value, axis, 1)]
+    up = shifted(value, axis, -1)
+    down = shifted(value, axis, 1)
+    return [value, up, down]
 
 
 def returned(parts, axis):
-    if lax.axis_size(axis) == 2:
+    count = lax.axis_size(axis)
+    if count == 2:
         return [shifted(parts[0], axis, 1)]
-    return [shifted(parts[0], axis, 1), shifted(parts[1], axis, -1)]
+    if count % 2:
+        return [shifted(parts[1], axis, -1), shifted(parts[0], axis, 1)]
+    even = lax.axis_index(axis) % 2 == 0
+    near = jnp.where(even, parts[0], parts[1])
+    far = jnp.where(even, parts[1], parts[0])
+    ring = [(i, (((i + 1) % count) ^ 1) - 1) for i in range(count)]
+    ring = [(source, target % count) for source, target in ring]
+    far = lax.ppermute(far, axis, ring)
+    near = lax.ppermute(near, axis, [(i, i ^ 1) for i in range(count)])
+    return [far, near]
 
 
 VMEM = pl.BlockSpec(memory_space=pltpu.VMEM)
@@ -342,7 +369,7 @@
 SMALL = pltpu.CompilerParams(vmem_limit_bytes=4 << 20)
 
 
-def local(
+def layer(
     feats, positions, species, cell_counts, pair_list, w_env, radial, pair_scale, w_hidden,
     w_zero, w_one, w_out,
 ):
@@ -360,6 +387,9 @@
     block = jnp.concatenate(gathered(block, "gz"), axis=0)
     blocks = gathered(block, "gx")
 
+    place = jnp.arange(WIDE)
+    held = place % CHUNK + place // (4 * CHUNK) * CHUNK + place // CHUNK % 4 * CHANNELS
+    swap = (held[:, None] == place[None, :]).astype(BF16)
     out_cells = nxu * nzu
     out_shape = [
         jax.ShapeDtypeStruct((1, 1, 1, SLOTS), F32),
@@ -375,12 +405,16 @@
         pltpu.VMEM((cells, 8, SLOTS), F32),
         pltpu.VMEM((cells, CHANNELS, SLOTS), BF16),
         pltpu.VMEM((PAIRS, QUAD, LANES), BF16),
-        pltpu.VMEM((PAIRS, WIDE, LANES), BF16),
+        pltpu.VMEM((PAIRS + 1, WIDE, LANES), BF16),
         pltpu.VMEM((PAIRS, SLOTS, LANES), F32),
         pltpu.VMEM((PAIRS, SLOTS, LANES), F32),
         pltpu.VMEM((PAIRS, SLOTS, LANES), F32),
         pltpu.VMEM((QUAD, WIDE), F32),
         pltpu.VMEM((QUAD, WIDE), F32),
+        pltpu.VMEM((WIDE, LANES), F32),
+        pltpu.VMEM((SLOTS, D), F32),
+        pltpu.VMEM((QUAD, LANES), BF16),
+        pltpu.VMEM((WIDE, LANES), BF16),
         pltpu.VMEM((QUAD, WIDE), BF16),
         pltpu.VMEM((WIDE, QUAD), BF16),
         pltpu.VMEM((3, SLOTS, SLOTS), F32),
@@ -390,13 +424,13 @@
     results = pl.pallas_call(
         lambda *refs: main_kernel((nxu, nyu, nzu, sizes), *refs),
         out_shape=out_shape,
-        in_specs=[SMEM] + [VMEM] * (nxu + 7),
+        in_specs=[SMEM] + [VMEM] * (nxu + 8),
         out_specs=[VMEM] * len(out_shape),
         scratch_shapes=scratch,
         compiler_params=pltpu.CompilerParams(vmem_limit_bytes=24 << 20),
         name="pairs",
     )(
-        pair_list, *blocks, feats, radial, pair_scale, w_hidden, w_zero, w_one, w_out.reshape(1, D)
+        pair_list, *blocks, feats, radial, pair_scale, w_hidden, w_zero, w_one, w_out.reshape(1, D), swap
     )
     energy, direct, keep = results[:3]
     total = keep
@@ -427,5 +461,5 @@
     cell = P("gx", "gy", "gz")
     in_specs = (cell,) * 5 + (P(),) * 7
     return jax.shard_map(
-        local, mesh=mesh, in_specs=in_specs, out_specs=(cell,) * 3, check_vma=False
+        layer, mesh=mesh, in_specs=in_specs, out_specs=(cell,) * 3, check_vma=False
     )

time: 45.1 us -> 43.6 us (0.967)
  starting transfers between devices: 15.3 us -> 10.4 us
  waiting for transfers between devices: 15.6 us -> 20.3 us
  other arithmetic: 1.54 us -> 0.9 us
  Pallas kernels: 10.9 us -> 10.4 us
    ppermute x0 -> x2, waiting for transfers between devices: none -> 6.2 us  [the longest x1 6.19 us: returned(): far = lax.ppermute(far, axis, ring)]
    ppermute x8 -> x6, starting transfers between devices: 15.3 us -> 10 us  [shifted(): lax.ppermute(value, axis, [(i, (i + steps) % count) for i in range(count)])]
    ppermute x8 -> x6, waiting for transfers between devices: 15.6 us -> 14.1 us  [shifted(): lax.ppermute(value, axis, [(i, (i + steps) % count) for i in range(count)])]
    concatenate x2, other arithmetic: 1.5 us -> 0.74 us  [the longest x1 0.73 us: layer(): block = jnp.concatenate(gathered(msg, 'gy'), axis=0)]
    pallas_call x3, Pallas kernels: 10.9 us -> 10.4 us  [the longest x1 7.91 us: layer(): pl.pallas_call(lambda *refs: main_kernel((nxu, nyu, nzu, sizes), *refs),...]
where the time goes in v3:
time: 43.6 us; the launch traced here: 43.4 us
  waiting for transfers between devices  20.3 us (47%)
  Pallas kernels  10.4 us (24%)
  starting transfers between devices  10.4 us (24%)
  between operations  1.4 us (3%)
  other arithmetic  0.9 us (2%)
    ppermute x6, waiting for transfers between devices, shifted(): lax.ppermute(value, axis, [(i, (i + steps) % count) for i in range(count)])  14.1 us
    ppermute x6, starting transfers between devices, shifted(): lax.ppermute(value, axis, [(i, (i + steps) % count) for i in range(count)])  10 us
    pallas_call x1, Pallas kernels, layer(): pl.pallas_call(lambda *refs: main_kernel((nxu, nyu, nzu, sizes), *refs),...  7.91 us
    ppermute x1, waiting for transfers between devices, returned(): far = lax.ppermute(far, axis, ring)  6.19 us
    pallas_call x1, Pallas kernels, layer(): pl.pallas_call(pack_kernel, out_shape=jax.ShapeDtypeStruct((1, ROWS, SLOT...  1.62 us
  transfers between devices with their start and end apart: 8, of which 7 were waited for; matrix products, arithmetic and copies ran while one was open for 0% of the time, Pallas kernels for 0%

profile of v3, /device:TPU:0, one launch (start us, length us, event | category | flops | bytes accessed | tf_op | source)
XLA Modules:
  0.0 43.4 jit_solution(13336587972258219036)
XLA Ops:
  1.3 1.6 %pack.1 = bf16[1,80,128]{2,1,0:T(8,128)(2,1)} custom-call(s32[1,1,1]{2,1,0:T(1,128)S(6)} %copy.16.counts_ref, bf16[1,1,1,128,256]{4,3,2,1,0:T(8,128)(2,1)} %refs_4_.1, f32[1,1,3,1,128]{4,3,2,1,0:T(1,128)} %bitcast.9, s32[1,1,1,128]{3,2,1,0:T(1,128)} %species_ref.1, bf16[64,256]{1,0:T(8,128)(2,1)} %bitcast.6), custom_call_target="tpu_custom_call" | custom-call | tf_op jit(solution)/shard_map/pack/pallas_call | solution.py:379
  2.9 0.0 copy-start.9
  2.9 0.5 %collective-permute-start = (bf16[1,80,128]{2,1,0:T(8,128)(2,1)}, bf16[1,80,128]{2,1,0:T(8,128)(2,1)S(1)}, u32[]{:S(2)}, u32[]{:S(2)}) collective-permute-start(bf16[1,80,128]{2,1,0:T(8,128)(2,1)} %pack.1), channel_id=1, source_target_pairs={{0,2},{2,0},{1,3},{3,1},{4,6},{6,4},{5,7},{7,5},{8,10},{10,8},{9,1... | collective-permute-start | bytes 61448 | tf_op jit(solution)/shard_map/ppermute | solution.py:340
  3.4 1.1 %collective-permute-done = bf16[1,80,128]{2,1,0:T(8,128)(2,1)S(1)} collective-permute-done((bf16[1,80,128]{2,1,0:T(8,128)(2,1)}, bf16[1,80,128]{2,1,0:T(8,128)(2,1)S(1)}, u32[]{:S(2)}, u32[]{:S(2)}) %collective-permute-start) | collective-permute-done | bytes 20512 | tf_op jit(solution)/shard_map/ppermute | solution.py:340
  4.5 0.7 %pad_maximum_fusion.1 = bf16[2,80,128]{2,1,0:T(8,128)(2,1)S(1)} fusion(bf16[1,80,128]{2,1,0:T(8,128)(2,1)S(1)} %collective-permute-done, bf16[1,80,128]{2,1,0:T(8,128)(2,1)} %pack.1), kind=kLoop, calls=%fused_computation.6 | loop fusion | flops 20480 | bytes 81920 | tf_op jit(solution)/shard_map/concatenate | solution.py:386
  5.2 2.8 %collective-permute-start.1 = (bf16[2,80,128]{2,1,0:T(8,128)(2,1)S(1)}, bf16[2,80,128]{2,1,0:T(8,128)(2,1)S(1)}, u32[]{:S(2)}, u32[]{:S(2)}) collective-permute-start(bf16[2,80,128]{2,1,0:T(8,128)(2,1)S(1)} %pad_maximum_fusion.1), channel_id=1, source_target_pairs={{0,1},{1,0},{2,3},{3,2},{4,5},{5,4},{6,7},{7,6},{8,9},{9,8},{10,11... | collective-permute-start | bytes 122888 | tf_op jit(solution)/shard_map/ppermute | solution.py:340
  8.0 0.0 copy-start.2
  8.0 2.0 %collective-permute-done.1 = bf16[2,80,128]{2,1,0:T(8,128)(2,1)S(1)} collective-permute-done((bf16[2,80,128]{2,1,0:T(8,128)(2,1)S(1)}, bf16[2,80,128]{2,1,0:T(8,128)(2,1)S(1)}, u32[]{:S(2)}, u32[]{:S(2)}) %collective-permute-start.1) | collective-permute-done | bytes 40992 | tf_op jit(solution)/shard_map/ppermute | solution.py:340
  10.0 0.0 copy-done.9
  10.0 0.0 copy-start.5
  10.0 0.0 copy-start.7
  10.0 0.0 copy-start
  10.0 0.0 copy-start.3
  10.1 0.0 copy-start.4
  10.1 5.1 %collective-permute-start.2 = (bf16[4,80,128]{2,1,0:T(8,128)(2,1)S(1)}, bf16[4,80,128]{2,1,0:T(8,128)(2,1)S(1)}, u32[]{:S(2)}, u32[]{:S(2)}) collective-permute-start(bf16[4,80,128]{2,1,0:T(8,128)(2,1)S(1)} %pad_maximum_fusion.refs_1_), channel_id=1, source_target_pairs={{0,28},{4,0},{8,4},{12,8},{16,12},{20,16},{24,20},{28,24},{1,29},{... | collective-permute-start | bytes 245768 | tf_op jit(solution)/shard_map/ppermute | solution.py:340
  15.2 0.0 collective-permute-start.3
  15.2 0.0 copy-start.6
  15.2 0.1 fusion.refs_11_
  15.3 0.0 copy-start.8
  15.3 1.9 %collective-permute-done.2.refs_2_ = bf16[4,80,128]{2,1,0:T(8,128)(2,1)S(1)} collective-permute-done((bf16[4,80,128]{2,1,0:T(8,128)(2,1)S(1)}, bf16[4,80,128]{2,1,0:T(8,128)(2,1)S(1)}, u32[]{:S(2)}, u32[]{:S(2)}) %collective-permute-start.2) | collective-permute-done | bytes 81952 | tf_op jit(solution)/shard_map/ppermute | solution.py:340
  17.2 5.1 %collective-permute-done.3.refs_3_ = bf16[4,80,128]{2,1,0:T(8,128)(2,1)S(1)} collective-permute-done((bf16[4,80,128]{2,1,0:T(8,128)(2,1)S(1)}, bf16[4,80,128]{2,1,0:T(8,128)(2,1)S(1)}, u32[]{:S(2)}, u32[]{:S(2)}) %collective-permute-start.3) | collective-permute-done | bytes 81952 | tf_op jit(solution)/shard_map/ppermute | solution.py:340
  22.3 0.0 copy-done.2
  22.3 0.0 copy-done.5
  22.3 0.0 copy-done.7
  22.3 0.0 copy-done
  22.3 0.0 copy-done.3
  22.3 0.0 copy-done.4
  22.3 0.0 copy-done.6
  22.3 0.0 copy-done.8
  22.4 7.9 %pairs.1 = (f32[1,1,1,128]{3,2,1,0:T(1,128)}, f32[128,256]{1,0:T(8,128)S(1)}, f32[6,80,128]{2,1,0:T(8,128)S(1)}, bf16[6,80,128]{2,1,0:T(8,128)(2,1)S(1)}) custom-call(s32[1,1,1,27]{3,2,1,0:T(1,128)S(1)} %copy-done.8, bf16[4,80,128]{2,1,0:T(8,128)(2,1)S(1)} %pad_maximum_fusion.refs_1_, bf16[4,80,128]{2,1,0:T(8,128)(2,1)S(1)} %collective-permute-done.2.refs_2_, ...), custom_call_target="tpu_custom_call" | custom-call | tf_op jit(solution)/shard_map/pairs/pallas_call | solution.py:424
  30.3 0.0 collective-permute-start.4
  30.3 1.3 %collective-permute-done.4 = bf16[6,80,128]{2,1,0:T(8,128)(2,1)S(1)} collective-permute-done((bf16[6,80,128]{2,1,0:T(8,128)(2,1)S(1)}, bf16[6,80,128]{2,1,0:T(8,128)(2,1)S(1)}, u32[]{:S(2)}, u32[]{:S(2)}) %collective-permute-start.4) | collective-permute-done | bytes 122912 | tf_op jit(solution)/shard_map/ppermute | solution.py:340
  31.6 1.6 %collective-permute-start.5 = (bf16[3,80,128]{2,1,0:T(8,128)(2,1)S(1)}, bf16[3,80,128]{2,1,0:T(8,128)(2,1)S(1)}, u32[]{:S(2)}, u32[]{:S(2)}) collective-permute-start(bf16[3,80,128]{2,1,0:T(8,128)(2,1)S(1)} %slice.34), channel_id=1, source_target_pairs={{0,1},{1,0},{2,3},{3,2},{4,5},{5,4},{6,7},{7,6},{8,9},{9,8},{10,11... | collective-permute-start | bytes 184328 | tf_op jit(solution)/shard_map/ppermute | solution.py:340
  33.2 2.7 %collective-permute-done.5 = bf16[3,80,128]{2,1,0:T(8,128)(2,1)S(1)} collective-permute-done((bf16[3,80,128]{2,1,0:T(8,128)(2,1)S(1)}, bf16[3,80,128]{2,1,0:T(8,128)(2,1)S(1)}, u32[]{:S(2)}, u32[]{:S(2)}) %collective-permute-start.5) | collective-permute-done | bytes 61472 | tf_op jit(solution)/shard_map/ppermute | solution.py:340
  36.0 0.3 collective-permute-start.6
  36.3 0.0 collective-permute-start.7
  36.3 0.0 copy-start.1
  36.3 6.2 %collective-permute-done.6.refs_1_ = bf16[1,80,128]{2,1,0:T(8,128)(2,1)S(1)} collective-permute-done((bf16[1,80,128]{2,1,0:T(8,128)(2,1)S(1)}, bf16[1,80,128]{2,1,0:T(8,128)(2,1)S(1)}, u32[]{:S(2)}, u32[]{:S(2)}) %collective-permute-start.6) | collective-permute-done | bytes 20512 | tf_op jit(solution)/shard_map/ppermute | solution.py:362
  42.5 0.0 collective-permute-done.7.refs_2_
  42.5 0.0 copy-done.1
  42.5 0.8 %finish.1 = (f32[1,1,3,1,128]{4,3,2,1,0:T(1,128)}, bf16[1,1,1,128,256]{4,3,2,1,0:T(8,128)(2,1)}) custom-call(f32[1,80,128]{2,1,0:T(8,128)S(1)} %slice.25.refs_0_, bf16[1,80,128]{2,1,0:T(8,128)(2,1)S(1)} %collective-permute-done.6.refs_1_, bf16[1,80,128]{2,1,0:T(8,128)(2,1)S(1)} %collective-permute-done.7.refs_2_, f32[128,256]{1,0:T(8,128)S(1)} %get-tuple-element.12.refs_3_, ...), custom_call_target="tpu_custom_call" | custom-call | tf_op jit(solution)/shard_map/finish/pallas_call | solution.py:446
  (7 shorter events, 0.1 us)
Async XLA Ops:
  2.9 7.1 %copy-start.9 = (bf16[1,80,128]{2,1,0:T(8,128)(2,1)S(1)}, bf16[1,80,128]{2,1,0:T(8,128)(2,1)}, u32[]{:S(2)}) copy-start(bf16[1,80,128]{2,1,0:T(8,128)(2,1)} %pack.1) | copy-start | bytes 61444
  2.9 1.5 %collective-permute-start = (bf16[1,80,128]{2,1,0:T(8,128)(2,1)}, bf16[1,80,128]{2,1,0:T(8,128)(2,1)S(1)}, u32[]{:S(2)}, u32[]{:S(2)}) collective-permute-start(bf16[1,80,128]{2,1,0:T(8,128)(2,1)} %pack.1), channel_id=1, source_target_pairs={{0,2},{2,0},{1,3},{3,1},{4,6},{6,4},{5,7},{7,5},{8,10},{10,8},{9,1... | collective-permute-start | bytes 61448 | tf_op jit(solution)/shard_map/ppermute | solution.py:340
  5.2 4.8 %collective-permute-start.1 = (bf16[2,80,128]{2,1,0:T(8,128)(2,1)S(1)}, bf16[2,80,128]{2,1,0:T(8,128)(2,1)S(1)}, u32[]{:S(2)}, u32[]{:S(2)}) collective-permute-start(bf16[2,80,128]{2,1,0:T(8,128)(2,1)S(1)} %pad_maximum_fusion.1), channel_id=1, source_target_pairs={{0,1},{1,0},{2,3},{3,2},{4,5},{5,4},{6,7},{7,6},{8,9},{9,8},{10,11... | collective-permute-start | bytes 122888 | tf_op jit(solution)/shard_map/ppermute | solution.py:340
  8.0 14.3 %copy-start.2 = (bf16[256,256]{1,0:T(8,128)(2,1)S(1)}, bf16[256,256]{1,0:T(8,128)(2,1)}, u32[]{:S(2)}) copy-start(bf16[256,256]{1,0:T(8,128)(2,1)} %refs_7_.1) | copy-start | bytes 393220
  10.0 12.3 %copy-start.5 = (f32[6,6]{1,0:T(8,128)S(1)}, f32[6,6]{1,0:T(8,128)}, u32[]{:S(2)}) copy-start(f32[6,6]{1,0:T(8,128)} %refs_6_.1) | copy-start | bytes 436
  10.0 12.3 %copy-start.7 = (f32[256]{0:T(256)S(1)}, f32[256]{0:T(256)}, u32[]{:S(2)}) copy-start(f32[256]{0:T(256)} %param.23) | copy-start | bytes 3076
  10.0 12.3 %copy-start = (bf16[1,1,1,128,256]{4,3,2,1,0:T(8,128)(2,1)S(1)}, bf16[1,1,1,128,256]{4,3,2,1,0:T(8,128)(2,1)}, u32[]{:S(2)}) copy-start(bf16[1,1,1,128,256]{4,3,2,1,0:T(8,128)(2,1)} %refs_4_.1) | copy-start | bytes 196612
  10.0 12.3 %copy-start.3 = (bf16[64,256]{1,0:T(8,128)(2,1)S(1)}, bf16[64,256]{1,0:T(8,128)(2,1)}, u32[]{:S(2)}) copy-start(bf16[64,256]{1,0:T(8,128)(2,1)} %refs_8_.1) | copy-start | bytes 98308
  10.1 12.3 %copy-start.4 = (bf16[64,256]{1,0:T(8,128)(2,1)S(1)}, bf16[64,256]{1,0:T(8,128)(2,1)}, u32[]{:S(2)}) copy-start(bf16[64,256]{1,0:T(8,128)(2,1)} %refs_9_.1) | copy-start | bytes 98308
  10.1 7.1 %collective-permute-start.2 = (bf16[4,80,128]{2,1,0:T(8,128)(2,1)S(1)}, bf16[4,80,128]{2,1,0:T(8,128)(2,1)S(1)}, u32[]{:S(2)}, u32[]{:S(2)}) collective-permute-start(bf16[4,80,128]{2,1,0:T(8,128)(2,1)S(1)} %pad_maximum_fusion.refs_1_), channel_id=1, source_target_pairs={{0,28},{4,0},{8,4},{12,8},{16,12},{20,16},{24,20},{28,24},{1,29},{... | collective-permute-start | bytes 245768 | tf_op jit(solution)/shard_map/ppermute | solution.py:340
  15.2 7.1 %collective-permute-start.3 = (bf16[4,80,128]{2,1,0:T(8,128)(2,1)S(1)}, bf16[4,80,128]{2,1,0:T(8,128)(2,1)S(1)}, u32[]{:S(2)}, u32[]{:S(2)}) collective-permute-start(bf16[4,80,128]{2,1,0:T(8,128)(2,1)S(1)} %pad_maximum_fusion.refs_1_), channel_id=1, source_target_pairs={{0,4},{4,8},{8,12},{12,16},{16,20},{20,24},{24,28},{28,0},{1,5},{5... | collective-permute-start | bytes 245768 | tf_op jit(solution)/shard_map/ppermute | solution.py:340
  15.2 7.2 %copy-start.6 = (f32[4,64]{1,0:T(4,128)S(1)}, f32[4,64]{1,0:T(4,128)}, u32[]{:S(2)}) copy-start(f32[4,64]{1,0:T(4,128)} %refs_5_.1) | copy-start | bytes 3076
  15.3 7.1 %copy-start.8 = (s32[1,1,1,27]{3,2,1,0:T(1,128)S(1)}, s32[1,1,1,27]{3,2,1,0:T(1,128)}, u32[]{:S(2)}) copy-start(s32[1,1,1,27]{3,2,1,0:T(1,128)} %refs_0_.1) | copy-start | bytes 328
  30.3 1.3 %collective-permute-start.4 = (bf16[6,80,128]{2,1,0:T(8,128)(2,1)S(1)}, bf16[6,80,128]{2,1,0:T(8,128)(2,1)S(1)}, u32[]{:S(2)}, u32[]{:S(2)}) collective-permute-start(bf16[6,80,128]{2,1,0:T(8,128)(2,1)S(1)} %get-tuple-element.11), channel_id=1, source_target_pairs={{0,2},{2,0},{1,3},{3,1},{4,6},{6,4},{5,7},{7,5},{8,10},{10,8},{9,1... | collective-permute-start | bytes 368648 | tf_op jit(solution)/shard_map/ppermute | solution.py:340
  31.6 4.3 %collective-permute-start.5 = (bf16[3,80,128]{2,1,0:T(8,128)(2,1)S(1)}, bf16[3,80,128]{2,1,0:T(8,128)(2,1)S(1)}, u32[]{:S(2)}, u32[]{:S(2)}) collective-permute-start(bf16[3,80,128]{2,1,0:T(8,128)(2,1)S(1)} %slice.34), channel_id=1, source_target_pairs={{0,1},{1,0},{2,3},{3,2},{4,5},{5,4},{6,7},{7,6},{8,9},{9,8},{10,11... | collective-permute-start | bytes 184328 | tf_op jit(solution)/shard_map/ppermute | solution.py:340
  36.0 6.5 %collective-permute-start.6 = (bf16[1,80,128]{2,1,0:T(8,128)(2,1)S(1)}, bf16[1,80,128]{2,1,0:T(8,128)(2,1)S(1)}, u32[]{:S(2)}, u32[]{:S(2)}) collective-permute-start(bf16[1,80,128]{2,1,0:T(8,128)(2,1)S(1)} %get-tuple-element.21), channel_id=1, source_target_pairs={{0,28},{4,8},{8,4},{12,16},{16,12},{20,24},{24,20},{28,0},{1,29},{... | collective-permute-start | bytes 61448 | tf_op jit(solution)/shard_map/ppermute | solution.py:362
  36.3 6.2 %collective-permute-start.7 = (bf16[1,80,128]{2,1,0:T(8,128)(2,1)S(1)}, bf16[1,80,128]{2,1,0:T(8,128)(2,1)S(1)}, u32[]{:S(2)}, u32[]{:S(2)}) collective-permute-start(bf16[1,80,128]{2,1,0:T(8,128)(2,1)S(1)} %get-tuple-element.20), channel_id=1, source_target_pairs={{0,4},{4,0},{8,12},{12,8},{16,20},{20,16},{24,28},{28,24},{1,5},{5... | collective-permute-start | bytes 61448 | tf_op jit(solution)/shard_map/ppermute | solution.py:363
  36.3 6.2 %copy-start.1 = (bf16[256,64]{0,1:T(8,128)(2,1)S(1)}, bf16[256,64]{0,1:T(8,128)(2,1)}, u32[]{:S(2)}) copy-start(bf16[256,64]{0,1:T(8,128)(2,1)} %param.17) | copy-start | bytes 98308

commit v4 on v3

v4 whole, which is shorter than its diff:
```python
import jax
import jax.numpy as jnp
from jax import lax
from jax.experimental import pallas as pl
from jax.experimental.pallas import tpu as pltpu
from jax.sharding import PartitionSpec as P


D = 256
CHANNELS = 64
NBASIS = 4
NSPEC = 6
SLOTS = 128
CUTOFF = 0.55
CENTRE = 0.5
ROWS = 80
POS_ROW = 64
EXTRA_ROW = 74
LIST_LANE = 32
OFFSETS = 27
CHUNK = 16
CHUNKS = SLOTS // CHUNK
QUAD = NBASIS * SLOTS
WIDE = 4 * CHANNELS
LANES = 2 * SLOTS
NEAR_PAIRS = 5
FAR_PAIRS = 9
TOP = 8.0 * 1.4426950408889634
KAPPA = TOP**0.5
SLOPE = 4.0 * 1.4426950408889634**0.5 / TOP
SHIFT = 0.5 * 1.4426950408889634**0.5
LADDER = (1.0, 0.1353352832366127, 0.0024787521766663585, 6.14421235332821e-06)
F32 = jnp.float32
BF16 = jnp.bfloat16


def dot_nn(a, b):
    return lax.dot_general(a, b, (((1,), (0,)), ((), ())), preferred_element_type=F32)


def dot_nt(a, b):
    return lax.dot_general(a, b, (((1,), (1,)), ((), ())), preferred_element_type=F32)


def split3(value):
    high = value.astype(BF16)
    rest = value - high.astype(F32)
    middle = rest.astype(BF16)
    low = (rest - middle.astype(F32)).astype(BF16)
    return high, middle, low


def pack_kernel(
    counts_ref, feats_ref, pos_ref, species_ref, w_env_ref, list_ref, scale_ref, msg_ref, extra
):
    chans = dot_nt(w_env_ref[...], feats_ref[0, 0, 0])
    msg_ref[0, :CHANNELS] = chans.astype(BF16)
    pos = jnp.concatenate([pos_ref[0, 0, axis] for axis in range(3)], axis=0)
    slots = lax.broadcasted_iota(jnp.int32, (1, SLOTS), 1)
    counts = jnp.broadcast_to(counts_ref[0], (1, SLOTS))
    code = jnp.where(slots < counts, species_ref[0, 0].astype(F32), -1.0)
    high = pos.astype(BF16).astype(F32)
    middle = (pos - high).astype(BF16).astype(F32)
    low = pos - high - middle
    extra[...] = jnp.zeros_like(extra)
    for piece, value in enumerate(split3(scale_ref[...])):
        extra[:NSPEC, 8 * piece : 8 * piece + NSPEC] = value.astype(F32)
    extra[:1, LIST_LANE : LIST_LANE + OFFSETS] = list_ref[0, 0].astype(F32)
    tail = jnp.concatenate([high, middle, low, code, extra[:NSPEC]], axis=0)
    msg_ref[0, CHANNELS:] = tail.astype(BF16)


def row_sums(value):
    ones = jnp.ones((8, value.shape[1]), BF16)
    high, middle, low = split3(value)
    total = dot_nt(ones, high) + dot_nt(ones, middle) + dot_nt(ones, low)
    return total[0:1]


def unique_of(offset, count):
    if offset == 0 or count == 2:
        return abs(offset)
    return 1 if offset > 0 else 2


def tabulate(listed, tables, zone, sizes, counts):
    cell_of, slot_of, shift_of = tables
    nxu, nyu, nzu = counts
    live = jnp.int32(0)
    for tile in range(OFFSETS):
        offset = (tile // 9 - 1, tile // 3 % 3 - 1, tile % 3 - 1)
        if (offset[0] != 0) != zone:
            continue
        ux, uy, uz = [unique_of(o, size) for o, size in zip(offset, sizes)]
        cell = (max(ux - 1, 0) * nzu + uz) * nyu + uy
        cell_of[live] = jnp.int32(cell)
        slot_of[live] = jnp.int32(cell)
        for axis in range(3):
            shift_of[axis, live] = jnp.float32(offset[axis] * KAPPA / CUTOFF)
        live = live + listed(tile)
    for spare in (live, live + 1):
        cell_of[spare] = jnp.int32(0)
        slot_of[spare] = jnp.int32((nxu - 1 if zone else 1) * nyu * nzu)
        for axis in range(3):
            shift_of[axis, spare] = jnp.float32(0.0)
    return (live + 1) // 2


def unpack(msg_refs, counts, xj, chan):
    nyu, nzu = counts[1:]
    codes = []
    for cell in range(xj.shape[0]):
        msg = msg_refs[cell // (nyu * nzu) * nyu + cell % nyu]
        at = cell // nyu % nzu * ROWS
        tail = msg[0, at + CHANNELS : at + ROWS].astype(F32)
        place = tail[0:3] + tail[3:6] + tail[6:9]
        xj[cell, 0:3] = (place - CENTRE) * (KAPPA / CUTOFF)
        codes.append(tail[9:10])
        chan[cell] = msg[0, at : at + CHANNELS]
    return codes


def strengths(codes, onehot, scale, weight):
    scale = scale * (1.0 / (TOP * TOP))
    scale = jnp.concatenate([scale, jnp.zeros((8 - NSPEC, NSPEC), F32)], axis=0)
    coef = []
    for code in codes:
        total = jnp.zeros((8, SLOTS), F32)
        for kind in range(NSPEC):
            column = jnp.broadcast_to(scale[:, kind : kind + 1], (8, SLOTS))
            total = total + jnp.where(code == float(kind), column, 0.0)
        high = total.astype(BF16).astype(F32)
        middle = (total - high).astype(BF16).astype(F32)
        low = total - high - middle
        coef.append(
            jnp.concatenate([high, middle, low, jnp.zeros((104, SLOTS), F32)], axis=0).astype(BF16)
        )
    for cell in range(0, len(codes), 2):
        strength = dot_nn(onehot, jnp.concatenate(coef[cell : cell + 2], axis=1))
        weight[cell] = strength[:, :SLOTS]
        if cell + 1 < len(codes):
            weight[cell + 1] = strength[:, SLOTS:]
    weight[len(codes)] = jnp.zeros((SLOTS, SLOTS), F32)


def rows_of(pair, tables, xj):
    cell_of, slot_of, shift_of = tables
    first, second = 2 * pair, 2 * pair + 1
    cell_a, cell_b = cell_of[first], cell_of[second]
    rows = [
        jnp.concatenate(
            [
                xj[cell_a, axis : axis + 1] + shift_of[axis, first],
                xj[cell_b, axis : axis + 1] + shift_of[axis, second],
            ],
            axis=1,
        )
        for axis in range(3)
    ]
    return cell_a, cell_b, slot_of[first], slot_of[second], rows


def relative(rows, xi, block):
    out = []
    for axis in range(3):
        own = xi[axis, block * CHUNK : (block + 1) * CHUNK]
        out.append(rows[axis] - jnp.concatenate([own, own], axis=1))
    return out


def forward_tiles(trips, tables, xi, xj, chan, weight, saved, acc, tile_now, rmat_now):
    tiles, rmat, s_all, r_all, wb_all = saved
    tile_now[...] = jnp.zeros_like(tile_now)
    rmat_now[...] = jnp.zeros_like(rmat_now)

    def forward(pair, carry):
        acc[...] += dot_nt(tile_now[...], rmat_now[...])
        cell_a, cell_b, weight_a, weight_b, rows = rows_of(pair, tables, xj)
        for block in range(CHUNKS):
            at = slice(block * CHUNK, (block + 1) * CHUNK)
            dx, dy, dz = relative(rows, xi, block)
            s = jnp.minimum(dx * dx + dy * dy + dz * dz, TOP)
            inside = TOP - s
            spread = SLOPE * s - SHIFT
            ratio = jnp.exp2(s)
            strength = jnp.concatenate([weight[weight_a, at], weight[weight_b, at]], axis=1)
            wb = strength * jnp.exp2(-(spread * spread))
            s_all[pair, at] = s
            r_all[pair, at] = ratio
            wb_all[pair, at] = wb
            tile = wb * (inside * inside)
            for k in range(NBASIS):
                base = block * 4 * CHUNK + k * CHUNK
                rounded = tile.astype(BF16)
                tiles[pair, base : base + CHUNK] = rounded
                tile_now[base : base + CHUNK] = rounded
                if k + 1 < NBASIS:
                    tile = tile * ratio
        values = jnp.concatenate([chan[cell_a], chan[cell_b]], axis=1)
        rmat[pair, :CHANNELS] = values
        rmat_now[:CHANNELS] = values
        wide = values.astype(F32)
        for axis in range(3):
            base = (axis + 1) * CHANNELS
            scaled = (wide * rows[axis]).astype(BF16)
            rmat[pair, base : base + CHANNELS] = scaled
            rmat_now[base : base + CHANNELS] = scaled
        return carry

    lax.fori_loop(0, trips, forward, 0)
    acc[...] += dot_nt(tile_now[...], rmat_now[...])


def backward_tiles(trips, tables, xi, xj, saved, grad, gradt, pbuf, bbuf, fi, cg, pg):
    tiles, rmat, s_all, r_all, wb_all = saved
    pbuf[...] = dot_nn(grad[...], rmat[0])
    bbuf[...] = jnp.zeros_like(bbuf)
    cg[...] = jnp.zeros_like(cg)
    pg[...] = jnp.zeros_like(pg)

    def settle(pair):
        cell_a, cell_b, _, _, rows = rows_of(pair, tables, xj)
        along = [jnp.zeros((CHUNK, LANES), F32) for _ in range(3)]
        for part in range(CHANNELS // CHUNK):
            at = slice(part * CHUNK, (part + 1) * CHUNK)
            values = rmat[pair, at].astype(F32)
            sums = bbuf[part * 4 * CHUNK : part * 4 * CHUNK + CHUNK]
            for axis in range(3):
                base = part * 4 * CHUNK + (axis + 1) * CHUNK
                piece = bbuf[base : base + CHUNK]
                sums = sums + rows[axis] * piece
                along[axis] = along[axis] + values * piece
            cg[cell_a, at] += sums[:, :SLOTS]
            cg[cell_b, at] += sums[:, SLOTS:]
        for axis in range(3):
            total = KAPPA * jnp.sum(along[axis], axis=0, keepdims=True)
            pg[cell_a, axis : axis + 1] += total[:, :SLOTS]
            pg[cell_b, axis : axis + 1] += total[:, SLOTS:]

    def backward(pair, carry):
        cell_a, cell_b, _, _, rows = rows_of(pair, tables, xj)
        totals = [jnp.zeros((CHUNK, LANES), F32) for _ in range(3)]
        for block in range(CHUNKS):
            at = slice(block * CHUNK, (block + 1) * CHUNK)
            s = s_all[pair, at]
            ratio = r_all[pair, at]
            inside = TOP - s
            step = 8.0 * inside
            level = -2.0 * TOP - inside * ((32.0 / TOP) * s - 4.0)
            levels = [level]
            for _ in range(1, NBASIS):
                levels.append(levels[-1] + step)
            base = block * 4 * CHUNK
            slope = levels[3] * pbuf[base + 3 * CHUNK : base + 4 * CHUNK]
            for k in (2, 1, 0):
                slope = slope * ratio + levels[k] * pbuf[base + k * CHUNK : base + (k + 1) * CHUNK]
            slope = slope * (wb_all[pair, at] * inside)
            for axis, delta in enumerate(relative(rows, xi, block)):
                push = slope * delta
                totals[axis] = totals[axis] + push
                fi[axis, at] += push[:, :SLOTS] + push[:, SLOTS:]
        for axis in range(3):
            total = (2.0 / KAPPA) * jnp.sum(totals[axis], axis=0, keepdims=True)
            pg[cell_a, axis : axis + 1] += total[:, :SLOTS]
            pg[cell_b, axis : axis + 1] += total[:, SLOTS:]
        settle(jnp.maximum(pair - 1, 0))
        pbuf[...] = dot_nn(grad[...], rmat[pair + 1])
        bbuf[...] = dot_nn(gradt[...], tiles[pair])
        return carry

    lax.fori_loop(0, trips, backward, 0)

    @pl.when(trips > 0)
    def _():
        settle(trips - 1)


def write_out(out_refs, counts, cg, pg, slots):
    nyu, nzu = counts[1:]
    for cell in range(cg.shape[0]):
        out = out_refs[cell % nyu]
        at = slots[cell // (nyu * nzu)] * nzu + cell // nyu % nzu
        out[at, :CHANNELS] = cg[cell].astype(out.dtype)
        tail = jnp.concatenate([pg[cell], jnp.zeros((8, SLOTS), F32)], axis=0)
        out[at, CHANNELS:] = (tail * (1.0 / CUTOFF)).astype(out.dtype)


def inner_kernel(sizes, counts, *refs):
    _, nyu, _ = counts
    msg_refs = refs[:nyu]
    xi, code_ref, onehot_ref, xj, acc, *saved = refs[nyu : 10 + nyu]
    (
        cell_of, slot_of, shift_of, weight, chan, tile_now, rmat_now, list_row, list_ref, sem,
    ) = refs[10 + nyu :]
    tables = (cell_of, slot_of, shift_of)
    tail = msg_refs[0][0, CHANNELS:ROWS].astype(F32)
    extra = tail[EXTRA_ROW - CHANNELS : EXTRA_ROW - CHANNELS + NSPEC]
    list_row[...] = extra[:1].astype(jnp.int32)
    list_copy = pltpu.make_async_copy(list_row, list_ref, sem)
    list_copy.start()
    scale = extra[:, :NSPEC] + extra[:, 8 : 8 + NSPEC] + extra[:, 16 : 16 + NSPEC]
    codes = unpack(msg_refs, counts, xj, chan)
    for axis in range(3):
        xi[axis] = jnp.broadcast_to(xj[0, axis : axis + 1], (SLOTS, SLOTS)).T
    code_i = jnp.broadcast_to(codes[0], (SLOTS, SLOTS)).T
    code_ref[...] = code_i
    lane = lax.broadcasted_iota(jnp.int32, (SLOTS, SLOTS), 1)
    sub = lax.broadcasted_iota(jnp.int32, (SLOTS, SLOTS), 0)
    onehot = jnp.where((code_i == (lane % 8).astype(F32)) & (lane < 24), 1.0, 0.0)
    onehot = onehot.astype(BF16)
    onehot_ref[...] = onehot
    strengths(codes, onehot, scale, weight)
    list_copy.wait()
    trips = tabulate(lambda tile: list_ref[0, LIST_LANE + tile], tables, False, sizes, counts)
    weight[0] = jnp.where(lane == sub, 0.0, weight[0])
    acc[...] = jnp.zeros_like(acc)
    forward_tiles(trips, tables, xi, xj, chan, weight, saved, acc, tile_now, rmat_now)


def outer_kernel(sizes, counts, *refs):
    nxu, nyu, _ = counts
    far = (nxu - 1) * nyu
    list_ref, msg_refs = refs[0], refs[1 : 1 + far]
    refs = refs[1 + far :]
    scale_ref, radial_ref, w_zero_ref, w_one_ref, w_out_ref, swap_ref = refs[:6]
    feats_ref, w_hidden_ref, xi, code_ref, onehot_ref, acc_in = refs[6:12]
    grad, gradt, fi, pre_ref, heat_ref = refs[12:17]
    out_refs = refs[17 : 17 + nyu]
    (
        cell_of, slot_of, shift_of, weight, xj, chan, tiles, rmat, s_all, r_all, wb_all,
        acc, pbuf, bbuf, tile_now, rmat_now, cg, pg, hbuf,
    ) = refs[17 + nyu :]
    tables = (cell_of, slot_of, shift_of)
    saved = (tiles, rmat, s_all, r_all, wb_all)
    trips = tabulate(lambda tile: list_ref[0, 0, 0, tile], tables, True, sizes, counts)
    codes = unpack(msg_refs, counts, xj, chan)
    strengths(codes, onehot_ref[...], scale_ref[...], weight)
    acc[...] = acc_in[...]
    hbuf[...] = dot_nn(feats_ref[0, 0, 0], w_hidden_ref[...])
    forward_tiles(trips, tables, xi, xj, chan, weight, saved, acc, tile_now, rmat_now)

    radial = radial_ref[...]
    weights_k = []
    for k in range(NBASIS):
        row = radial[k : k + 1] * LADDER[k]
        weights_k.append(jnp.concatenate([row] + [row * (1.0 / KAPPA)] * 3, axis=1))
    mixed = []
    for block in range(CHUNKS):
        base = block * 4 * CHUNK
        total = weights_k[0] * acc[base : base + CHUNK]
        for k in range(1, NBASIS):
            total = total + weights_k[k] * acc[base + k * CHUNK : base + (k + 1) * CHUNK]
        mixed.append(total)
    mixed = jnp.concatenate(mixed, axis=0)
    low = lax.broadcasted_iota(jnp.int32, (SLOTS, SLOTS), 1) < CHANNELS
    left, right = mixed[:, :SLOTS], mixed[:, SLOTS:]
    scalar = jnp.where(low, left, pltpu.roll(left, CHANNELS, 1))
    own_left = jnp.where(low, 0.0, xi[0]) * (1.0 / KAPPA)
    own_right = jnp.where(low, xi[1], xi[2]) * (1.0 / KAPPA)
    left = left - own_left * scalar
    right = right - own_right * scalar
    features = [jnp.where(low, left, left * left), right * right]
    features = jnp.concatenate(features, axis=1).astype(BF16)
    w_one = w_one_ref[...]
    w_all = jnp.concatenate([w_zero_ref[...], w_one, w_one, w_one], axis=0)
    pre = hbuf[...] + dot_nn(features, w_all)
    gate = jax.nn.sigmoid(pre)
    occupied = jnp.concatenate([code_ref[...], code_ref[...]], axis=1) >= 0.0
    w_out = jnp.where(occupied, w_out_ref[...], 0.0)
    pre_grad = (w_out * gate * (1.0 + pre * (1.0 - gate))).astype(BF16)
    back_all = dot_nt(pre_grad, w_all)
    back_left, back_right = back_all[:, :SLOTS], back_all[:, SLOTS:]
    part_left = jnp.where(low, back_left, 2.0 * left * back_left)
    part_right = 2.0 * right * back_right
    fold = own_left * part_left + own_right * part_right
    fold = fold + pltpu.roll(fold, CHANNELS, 1)
    full = jnp.concatenate([part_left - jnp.where(low, fold, 0.0), part_right], axis=1)
    half = (0.5 * KAPPA) * scalar
    fi[0] = jnp.where(low, 0.0, half * part_left)
    fi[1] = jnp.where(low, half * part_right, 0.0)
    fi[2] = jnp.where(low, 0.0, half * part_right)
    for block in range(CHUNKS):
        piece = full[block * CHUNK : (block + 1) * CHUNK]
        for k in range(NBASIS):
            base = block * 4 * CHUNK + k * CHUNK
            scaled = weights_k[k] * piece
            grad[base : base + CHUNK] = scaled.astype(BF16)
    gradt[...] = dot_nt(swap_ref[...], grad[...]).astype(BF16)
    pre_ref[...] = pre_grad
    heat_ref[...] = pre * gate * w_out
    backward_tiles(trips, tables, xi, xj, saved, grad, gradt, pbuf, bbuf, fi, cg, pg)
    slots = [0, 1]
    if sizes[0] > 2 and sizes[0] % 2 == 0:
        odd = lax.rem(lax.axis_index("gx"), 2)
        slots = [1 - odd, odd]
    write_out(out_refs, counts, cg, pg, slots)


def rest_kernel(sizes, counts, *refs):
    nyu = counts[1]
    list_ref, w_hidden_ref, xi, xj, *saved = refs[:9]
    grad, gradt, fi_in, pre_ref, heat_ref = refs[9:14]
    energy_ref, direct_ref = refs[14:16]
    out_refs = refs[16 : 16 + nyu]
    cell_of, slot_of, shift_of, pbuf, bbuf, fi, cg, pg = refs[16 + nyu :]
    tables = (cell_of, slot_of, shift_of)
    trips = tabulate(lambda tile: list_ref[0, 0, 0, tile], tables, False, sizes, counts)
    energy_ref[0, 0] = row_sums(heat_ref[...])
    direct_ref[...] = dot_nt(pre_ref[...], w_hidden_ref[...])
    fi[...] = fi_in[...]
    backward_tiles(trips, tables, xi, xj, saved, grad, gradt, pbuf, bbuf, fi, cg, pg)
    for axis in range(3):
        pg[0, axis : axis + 1] -= (2.0 / KAPPA) * row_sums(fi[axis])
    write_out(out_refs, counts, cg, pg, [0])


def finish_kernel(count, *refs):
    keep_ref = refs[0]
    got_refs = refs[1 : 1 + count]
    direct_ref, w_env_ref, force_ref, grad_ref = refs[1 + count :]
    total = keep_ref[0]
    for got in got_refs:
        total = total + got[0].astype(F32)
    chan = total[:CHANNELS]
    high = chan.astype(BF16)
    low = (chan - high.astype(F32)).astype(BF16)
    both = jnp.concatenate([high, low], axis=0)
    w_env = w_env_ref[...]
    weights = jnp.concatenate([w_env, w_env], axis=0)
    part = lax.dot_general(both, weights, (((0,), (0,)), ((), ())), preferred_element_type=F32)
    grad_ref[0, 0, 0] = (direct_ref[...] + part).astype(BF16)
    for axis in range(3):
        force_ref[0, 0, axis] = -total[POS_ROW + axis : POS_ROW + axis + 1]


def shifted(value, axis, steps):
    count = lax.axis_size(axis)
    return lax.ppermute(value, axis, [(i, (i + steps) % count) for i in range(count)])


def gathered(value, axis):
    if lax.axis_size(axis) == 2:
        return [value, shifted(value, axis, 1)]
    up = shifted(value, axis, -1)
    down = shifted(value, axis, 1)
    return [value, up, down]


def returned(parts, axis):
    count = lax.axis_size(axis)
    if count == 2:
        return [shifted(parts[0], axis, 1)]
    return [shifted(parts[1], axis, -1), shifted(parts[0], axis, 1)]


def swapped(parts, axis):
    count = lax.axis_size(axis)
    if count == 2 or count % 2:
        return returned(parts, axis)
    ring = [(i, ((((i + 1) % count) ^ 1) - 1) % count) for i in range(count)]
    far = lax.ppermute(parts[0], axis, ring)
    near = lax.ppermute(parts[1], axis, [(i, i ^ 1) for i in range(count)])
    return [far, near]


VMEM = pl.BlockSpec(memory_space=pltpu.VMEM)
SMEM = pl.BlockSpec(memory_space=pltpu.SMEM)
SMALL = pltpu.CompilerParams(vmem_limit_bytes=4 << 20)


def layer(
    feats, positions, species, cell_counts, pair_list, w_env, radial, pair_scale, w_hidden,
    w_zero, w_one, w_out,
):
    sizes = [lax.axis_size(axis) for axis in ("gx", "gy", "gz")]
    nxu, nyu, nzu = [2 if size == 2 else 3 for size in sizes]
    msg = pl.pallas_call(
        pack_kernel,
        out_shape=jax.ShapeDtypeStruct((1, ROWS, SLOTS), BF16),
        in_specs=[VMEM] * 7,
        out_specs=VMEM,
        scratch_shapes=[pltpu.VMEM((8, SLOTS), F32)],
        name="pack",
    )(
        cell_counts, feats, positions.transpose(0, 1, 3, 2, 4), species, w_env.T, pair_list,
        pair_scale,
    )
    stack = gathered(msg, "gz")
    column = jnp.pad(msg, ((0, 0), (0, ROWS * (nzu - 1)), (0, 0)))
    column = lax.optimization_barrier(column)
    for uz in range(1, nzu):
        column = lax.dynamic_update_slice(column, stack[uz], (0, uz * ROWS, 0))
    blocks = [gathered(part, "gy") for part in gathered(column, "gx")]
    near_blocks = blocks[0]
    far_blocks = [block for part in blocks[1:] for block in part]
    counts = (nxu, nyu, nzu)
    near_cells, far_cells = nyu * nzu, (nxu - 1) * nyu * nzu

    def table_scratch():
        return [
            pltpu.SMEM((OFFSETS + 5,), jnp.int32),
            pltpu.SMEM((OFFSETS + 5,), jnp.int32),
            pltpu.SMEM((3, OFFSETS + 5), F32),
        ]

    def saved_shapes(pairs):
        return [
            ((pairs, QUAD, LANES), BF16),
            ((pairs + 1, WIDE, LANES), BF16),
            ((pairs, SLOTS, LANES), F32),
            ((pairs, SLOTS, LANES), F32),
            ((pairs, SLOTS, LANES), F32),
        ]

    square = (SLOTS, SLOTS)
    now_scratch = [pltpu.VMEM((QUAD, LANES), BF16), pltpu.VMEM((WIDE, LANES), BF16)]
    buffers = [pltpu.VMEM((QUAD, WIDE), F32), pltpu.VMEM((WIDE, LANES), F32)]

    def sums_scratch(cells):
        return [pltpu.VMEM((cells, CHANNELS, SLOTS), F32), pltpu.VMEM((cells, 8, SLOTS), F32)]

    def call(kernel, shapes, scratch, megabytes, first, *operands):
        return pl.pallas_call(
            lambda *refs: kernel(sizes, counts, *refs),
            out_shape=[jax.ShapeDtypeStruct(*shape) for shape in shapes],
            in_specs=first + [VMEM] * (len(operands) - len(first)),
            out_specs=[VMEM] * len(shapes),
            scratch_shapes=scratch,
            compiler_params=pltpu.CompilerParams(vmem_limit_bytes=megabytes << 20),
            cost_estimate=pl.CostEstimate(
                flops=1000000000, bytes_accessed=4000000, transcendentals=0
            ),
        )(*operands)

    inner = call(
        inner_kernel,
        [
            ((3,) + square, F32),
            (square, F32),
            (square, BF16),
            ((near_cells, 8, SLOTS), F32),
            ((QUAD, WIDE), F32),
        ]
        + saved_shapes(NEAR_PAIRS),
        table_scratch()
        + [pltpu.VMEM((near_cells + 1,) + square, F32)]
        + [pltpu.VMEM((near_cells, CHANNELS, SLOTS), BF16)]
        + now_scratch
        + [
            pltpu.VMEM((1, SLOTS), jnp.int32),
            pltpu.SMEM((1, SLOTS), jnp.int32),
            pltpu.SemaphoreType.DMA,
        ],
        12,
        [],
        *near_blocks,
    )
    xi, code, onehot, xj, acc = inner[:5]
    saved = inner[5:]
    place = jnp.arange(WIDE)
    held = place % CHUNK + place // (4 * CHUNK) * CHUNK + place // CHUNK % 4 * CHANNELS
    swap = (held[:, None] == place[None, :]).astype(BF16)
    far_out = (nxu - 1) * nzu
    outer = call(
        outer_kernel,
        [
            ((QUAD, WIDE), BF16),
            ((WIDE, QUAD), BF16),
            ((3,) + square, F32),
            ((SLOTS, D), BF16),
            ((SLOTS, D), F32),
            ((far_out, ROWS, SLOTS), F32),
        ]
        + [((far_out, ROWS, SLOTS), BF16)] * (nyu - 1),
        table_scratch()
        + [pltpu.VMEM((far_cells + 1,) + square, F32)]
        + [pltpu.VMEM((far_cells, 8, SLOTS), F32)]
        + [pltpu.VMEM((far_cells, CHANNELS, SLOTS), BF16)]
        + [pltpu.VMEM(*shape) for shape in saved_shapes(FAR_PAIRS)]
        + [pltpu.VMEM((QUAD, WIDE), F32)]
        + buffers
        + now_scratch
        + sums_scratch(far_cells)
        + [pltpu.VMEM((SLOTS, D), F32)],
        20,
        [SMEM],
        pair_list, *far_blocks, pair_scale, radial, w_zero, w_one, w_out.reshape(1, D), swap,
        feats, w_hidden, xi, code, onehot, acc,
    )
    grad, gradt, force_in, pre_grad, heat = outer[:5]
    total = outer[5]
    for got in returned(outer[6:], "gy"):
        total = total + got.astype(F32)
    sends = [total[ux * nzu : (ux + 1) * nzu].astype(BF16) for ux in range(nxu - 1)]
    from_far = swapped(sends, "gx")
    rest = call(
        rest_kernel,
        [((1, 1, 1, SLOTS), F32), ((SLOTS, D), F32), ((nzu, ROWS, SLOTS), F32)]
        + [((nzu, ROWS, SLOTS), BF16)] * (nyu - 1),
        table_scratch()
        + buffers
        + [pltpu.VMEM((3,) + square, F32)]
        + sums_scratch(near_cells),
        12,
        [SMEM],
        pair_list, w_hidden, xi, xj, *saved, grad, gradt, force_in, pre_grad, heat,
    )
    energy, direct, total = rest[:3]
    for got in returned(rest[3:], "gy"):
        total = total + got.astype(F32)
    for got in from_far:
        total = total + got.astype(F32)
    sends = [total[uz : uz + 1].astype(BF16) for uz in range(1, nzu)]
    keep = total[:1]
    arrived = returned(sends, "gz")
    forces, feat_grad = pl.pallas_call(
        lambda *refs: finish_kernel(len(arrived), *refs),
        out_shape=[
            jax.ShapeDtypeStruct((1, 1, 3, 1, SLOTS), F32),
            jax.ShapeDtypeStruct((1, 1, 1, SLOTS, D), BF16),
        ],
        in_specs=[VMEM] * (3 + len(arrived)),
        out_specs=[VMEM] * 2,
        compiler_params=SMALL,
        name="finish",
    )(keep, *arrived, direct, w_env.T)
    return energy, forces.transpose(0, 1, 3, 2, 4), feat_grad


def solution(mesh):
    cell = P("gx", "gy", "gz")
    in_specs = (cell,) * 5 + (P(),) * 7
    return jax.shard_map(
        layer, mesh=mesh, in_specs=in_specs, out_specs=(cell,) * 3, check_vma=False
    )
```

time: 43.6 us -> 39.7 us (0.911)
  waiting for transfers between devices: 20.3 us -> 8.74 us
  starting transfers between devices: 10.4 us -> 15.5 us
  Pallas kernels: 10.4 us -> 12.7 us
  local copies, waits for them, and re-layouts: 0.06 us -> 0.84 us
  other arithmetic: 0.9 us -> 0.15 us
    ppermute x6 -> x9, waiting for transfers between devices: 14.1 us -> 4.69 us  [shifted(): lax.ppermute(value, axis, [(i, (i + steps) % count) for i in range(count)])]
    ppermute x2, starting transfers between devices: 0.34 us -> 3.58 us  [the longest x1 3.58 us: swapped(): far = lax.ppermute(parts[0], axis, ring)]
    pallas_call x1 -> x3, Pallas kernels: 7.91 us -> 10.2 us  [call(): pl.pallas_call(lambda *refs: kernel(sizes, counts, *refs), out_shape=[jax...]
    ppermute x2, waiting for transfers between devices: 6.2 us -> 4.04 us  [the longest x1 3.28 us: swapped(): far = lax.ppermute(parts[0], axis, ring)]
    ppermute x6 -> x9, starting transfers between devices: 10 us -> 12 us  [shifted(): lax.ppermute(value, axis, [(i, (i + steps) % count) for i in range(count)])]
    pad x0 -> x1, local copies, waits for them, and re-layouts: none -> 0.76 us  [layer(): column = jnp.pad(msg, ((0, 0), (0, ROWS * (nzu - 1)), (0, 0)))]
    concatenate x2 -> x0, other arithmetic: 0.74 us -> none  [the longest x1 0.73 us: layer(): block = jnp.concatenate(gathered(msg, 'gy'), axis=0)]
  transfers between devices with their start and end apart: 8 -> 11, of which waited for: 7 -> 5; matrix products, arithmetic and copies ran while one was open for 0% -> 2% of each run, Pallas kernels for 0% -> 13%
where the time goes in v4:
time: 39.7 us; the launch traced here: 39.4 us
  starting transfers between devices  15.5 us (39%)
  Pallas kernels  12.7 us (32%)
  waiting for transfers between devices  8.74 us (22%)
  between operations  1.48 us (4%)
  local copies, waits for them, and re-layouts  0.84 us (2%)
    ppermute x9, starting transfers between devices, shifted(): lax.ppermute(value, axis, [(i, (i + steps) % count) for i in range(count)])  12 us
    pallas_call x3, Pallas kernels, call(): pl.pallas_call(lambda *refs: kernel(sizes, counts, *refs), out_shape=[jax...  10.2 us
    ppermute x9, waiting for transfers between devices, shifted(): lax.ppermute(value, axis, [(i, (i + steps) % count) for i in range(count)])  4.69 us
    ppermute x1, starting transfers between devices, swapped(): far = lax.ppermute(parts[0], axis, ring)  3.58 us
    ppermute x1, waiting for transfers between devices, swapped(): far = lax.ppermute(parts[0], axis, ring)  3.28 us
    pallas_call x1, Pallas kernels, layer(): pl.pallas_call(pack_kernel, out_shape=jax.ShapeDtypeStruct((1, ROWS, SLOT...  1.65 us
    pallas_call x1, Pallas kernels, layer(): pl.pallas_call(lambda *refs: finish_kernel(len(arrived), *refs), out_shap...  0.84 us
  transfers between devices with their start and end apart: 11, of which 5 were waited for; matrix products, arithmetic and copies ran while one was open for 2% of the time, Pallas kernels for 13%

profile of v4, /device:TPU:0, one launch (start us, length us, event | category | flops | bytes accessed | tf_op | source)
XLA Modules:
  0.0 39.4 jit_solution(4826084437469136726)
XLA Ops:
  1.3 1.6 %pack.1 = bf16[1,80,128]{2,1,0:T(8,128)(2,1)} custom-call(s32[1,1,1]{2,1,0:T(1,128)S(6)} %copy.17.counts_ref, bf16[1,1,1,128,256]{4,3,2,1,0:T(8,128)(2,1)} %refs_11_.1, f32[1,1,3,1,128]{4,3,2,1,0:T(1,128)} %bitcast.9, s32[1,1,1,128]{3,2,1,0:T(1,128)} %species_ref.1, bf16[64,256]{1,0:T(8,128)(2,1)} %bitcast.6, s32[1,1,1,27]{3,2,1,0:T(1,128)} %refs_0_.3, ...), custom_call_target="tpu_custom_call" | custom-call | tf_op jit(solution)/shard_map/pack/pallas_call | solution.py:477
  2.9 3.0 %collective-permute-start = (bf16[1,80,128]{2,1,0:T(8,128)(2,1)}, bf16[1,80,128]{2,1,0:T(8,128)(2,1)S(1)}, u32[]{:S(2)}, u32[]{:S(2)}) collective-permute-start(bf16[1,80,128]{2,1,0:T(8,128)(2,1)} %pack.1), channel_id=1, source_target_pairs={{0,1},{1,0},{2,3},{3,2},{4,5},{5,4},{6,7},{7,6},{8,9},{9,8},{10,11... | collective-permute-start | bytes 61448 | tf_op jit(solution)/shard_map/ppermute | solution.py:438
  5.9 0.8 %pad.4 = bf16[1,160,128]{2,1,0:T(8,128)(2,1)S(1)} pad(bf16[1,80,128]{2,1,0:T(8,128)(2,1)} %pack.1, bf16[]{:T(256)} %constant.50.clone.1), padding=0_0x0_80x0_0 | pad | bytes 61442 | tf_op jit(solution)/shard_map/jit(_pad)/pad | solution.py:489
  6.7 1.2 %collective-permute-done = bf16[1,80,128]{2,1,0:T(8,128)(2,1)S(1)} collective-permute-done((bf16[1,80,128]{2,1,0:T(8,128)(2,1)}, bf16[1,80,128]{2,1,0:T(8,128)(2,1)S(1)}, u32[]{:S(2)}, u32[]{:S(2)}) %collective-permute-start) | collective-permute-done | bytes 20512 | tf_op jit(solution)/shard_map/ppermute | solution.py:438
  7.9 2.0 %collective-permute-start.4 = (bf16[1,160,128]{2,1,0:T(8,128)(2,1)S(1)}, bf16[1,160,128]{2,1,0:T(8,128)(2,1)S(1)}, u32[]{:S(2)}, u32[]{:S(2)}) collective-permute-start(bf16[1,160,128]{2,1,0:T(8,128)(2,1)S(1)} %constant_dynamic-update-slice_fusion.refs_0_), channel_id=1, source_target_pairs={{0,4},{4,8},{8,12},{12,16},{16,20},{20,24},{24,28},{28,0},{1,5},{5... | collective-permute-start | bytes 122888 | tf_op jit(solution)/shard_map/ppermute | solution.py:438
  9.9 3.1 %collective-permute-start.2 = (bf16[1,160,128]{2,1,0:T(8,128)(2,1)S(1)}, bf16[1,160,128]{2,1,0:T(8,128)(2,1)S(1)}, u32[]{:S(2)}, u32[]{:S(2)}) collective-permute-start(bf16[1,160,128]{2,1,0:T(8,128)(2,1)S(1)} %constant_dynamic-update-slice_fusion.refs_0_), channel_id=1, source_target_pairs={{0,28},{4,0},{8,4},{12,8},{16,12},{20,16},{24,20},{28,24},{1,29},{... | collective-permute-start | bytes 122888 | tf_op jit(solution)/shard_map/ppermute | solution.py:438
  13.0 0.0 collective-permute-start.1
  13.0 0.1 fusion.refs_10_
  13.1 0.0 copy-start
  13.1 0.0 copy-start.2
  13.1 0.0 copy-start.3
  13.1 0.0 copy-start.4
  13.1 0.0 copy-start.5
  13.2 0.0 copy-start.6
  13.2 0.0 copy-start.7
  13.2 0.0 copy-start.8
  13.2 1.7 %collective-permute-done.4.refs_3_ = bf16[1,160,128]{2,1,0:T(8,128)(2,1)S(1)} collective-permute-done((bf16[1,160,128]{2,1,0:T(8,128)(2,1)S(1)}, bf16[1,160,128]{2,1,0:T(8,128)(2,1)S(1)}, u32[]{:S(2)}, u32[]{:S(2)}) %collective-permute-start.4) | collective-permute-done | bytes 40992 | tf_op jit(solution)/shard_map/ppermute | solution.py:438
  14.9 0.0 collective-permute-start.5
  14.9 0.0 collective-permute-done.2.refs_1_
  14.9 0.5 %collective-permute-start.3 = (bf16[1,160,128]{2,1,0:T(8,128)(2,1)S(1)}, bf16[1,160,128]{2,1,0:T(8,128)(2,1)S(1)}, u32[]{:S(2)}, u32[]{:S(2)}) collective-permute-start(bf16[1,160,128]{2,1,0:T(8,128)(2,1)S(1)} %collective-permute-done.2.refs_1_), channel_id=1, source_target_pairs={{0,2},{2,0},{1,3},{3,1},{4,6},{6,4},{5,7},{7,5},{8,10},{10,8},{9,1... | collective-permute-start | bytes 122888 | tf_op jit(solution)/shard_map/ppermute | solution.py:438
  15.4 0.0 collective-permute-done.1.refs_1_
  15.4 2.2 %shard_map.139 = (f32[3,128,128]{2,1,0:T(8,128)S(1)}, f32[128,128]{1,0:T(8,128)S(1)}, bf16[128,128]{1,0:T(8,128)(2,1)S(1)}, f32[4,8,128]{2,1,0:T(8,128)S(1)}, f3...) custom-call(bf16[1,160,128]{2,1,0:T(8,128)(2,1)S(1)} %constant_dynam, ...), custom_call_target="tpu_custom_call" | custom-call | flops 1000000000 | bytes 4000000 | tf_op jit(solution)/shard_map/pallas_call | solution.py:523
  17.6 0.0 collective-permute-done.5.refs_4_
  17.7 0.0 collective-permute-done.3.refs_2_
  17.7 0.0 copy-done
  17.7 0.0 copy-done.2
  17.7 0.0 copy-done.3
  17.7 0.0 copy-done.4
  17.7 0.0 copy-done.5
  17.7 0.0 copy-done.6
  17.7 0.0 copy-done.7
  17.7 0.0 copy-done.8
  17.7 5.1 %shard_map.140 = (bf16[512,256]{1,0:T(8,128)(2,1)S(1)}, bf16[256,512]{1,0:T(8,128)(2,1)S(1)}, f32[3,128,128]{2,1,0:T(8,128)S(1)}, bf16[128,256]{1,0:T(8,128)(2,1...) custom-call(s32[1,1,1,27]{3,2,1,0:T(1,128)S(1)} %copy-done.4, ...), custom_call_target="tpu_custom_call" | custom-call | flops 1000000000 | bytes 4000000 | tf_op jit(solution)/shard_map/pallas_call | solution.py:523
  22.9 0.8 %collective-permute-start.7 = (bf16[4,80,128]{2,1,0:T(8,128)(2,1)S(1)}, bf16[4,80,128]{2,1,0:T(8,128)(2,1)S(1)}, u32[]{:S(2)}, u32[]{:S(2)}) collective-permute-start(bf16[4,80,128]{2,1,0:T(8,128)(2,1)S(1)} %get-tuple-element.45), channel_id=1, source_target_pairs={{0,2},{2,0},{1,3},{3,1},{4,6},{6,4},{5,7},{7,5},{8,10},{10,8},{9,1... | collective-permute-start | bytes 245768 | tf_op jit(solution)/shard_map/ppermute | solution.py:438
  23.7 0.0 copy-start.1
  23.7 2.9 %shard_map.141 = (f32[1,1,1,128]{3,2,1,0:T(1,128)}, f32[128,256]{1,0:T(8,128)S(1)}, f32[2,80,128]{2,1,0:T(8,128)S(1)}, bf16[2,80,128]{2,1,0:T(8,128)(2,1)S(1)}) custom-call(s32[1,1,1,27]{3,2,1,0:T(1,128)S(1)} %copy-done.4, bf16[256,256]{1,0:T(8,128)(2,1)S(1)} %copy-done, f32[3,128,128]{2,1,0:T(8,128)S(1)} %get-tuple-element.26.refs_13_.refs_2_, ...), custom_call_target="tpu_custom_call" | custom-call | flops 1000000000 | bytes 4000000 | tf_op jit(solution)/shard_map/pallas_call | solution.py:523
  26.6 0.1 collective-permute-start.6
  26.6 0.0 collective-permute-done.7
  26.7 3.6 %collective-permute-start.8 = (bf16[2,80,128]{2,1,0:T(8,128)(2,1)S(1)}, bf16[2,80,128]{2,1,0:T(8,128)(2,1)S(1)}, u32[]{:S(2)}, u32[]{:S(2)}) collective-permute-start(bf16[2,80,128]{2,1,0:T(8,128)(2,1)S(1)} %get-tuple-element.52), channel_id=1, source_target_pairs={{0,28},{4,8},{8,4},{12,16},{16,12},{20,24},{24,20},{28,0},{1,29},{... | collective-permute-start | bytes 122888 | tf_op jit(solution)/shard_map/ppermute | solution.py:461
  30.2 0.0 collective-permute-start.9
  30.2 0.0 collective-permute-done.6
  30.2 3.3 %collective-permute-done.8 = bf16[2,80,128]{2,1,0:T(8,128)(2,1)S(1)} collective-permute-done((bf16[2,80,128]{2,1,0:T(8,128)(2,1)S(1)}, bf16[2,80,128]{2,1,0:T(8,128)(2,1)S(1)}, u32[]{:S(2)}, u32[]{:S(2)}) %collective-permute-start.8) | collective-permute-done | bytes 40992 | tf_op jit(solution)/shard_map/ppermute | solution.py:461
  33.5 0.8 %collective-permute-done.9 = bf16[2,80,128]{2,1,0:T(8,128)(2,1)S(1)} collective-permute-done((bf16[2,80,128]{2,1,0:T(8,128)(2,1)S(1)}, bf16[2,80,128]{2,1,0:T(8,128)(2,1)S(1)}, u32[]{:S(2)}, u32[]{:S(2)}) %collective-permute-start.9) | collective-permute-done | bytes 40992 | tf_op jit(solution)/shard_map/ppermute | solution.py:462
  34.3 2.5 %collective-permute-start.10 = (bf16[1,80,128]{2,1,0:T(8,128)(2,1)S(1)}, bf16[1,80,128]{2,1,0:T(8,128)(2,1)S(1)}, u32[]{:S(2)}, u32[]{:S(2)}) collective-permute-start(bf16[1,80,128]{2,1,0:T(8,128)(2,1)S(1)} %slice.24), channel_id=1, source_target_pairs={{0,1},{1,0},{2,3},{3,2},{4,5},{5,4},{6,7},{7,6},{8,9},{9,8},{10,11... | collective-permute-start | bytes 61448 | tf_op jit(solution)/shard_map/ppermute | solution.py:438
  36.8 1.8 %collective-permute-done.10.refs_1_ = bf16[1,80,128]{2,1,0:T(8,128)(2,1)S(1)} collective-permute-done((bf16[1,80,128]{2,1,0:T(8,128)(2,1)S(1)}, bf16[1,80,128]{2,1,0:T(8,128)(2,1)S(1)}, u32[]{:S(2)}, u32[]{:S(2)}) %collective-permute-start.10) | collective-permute-done | bytes 20512 | tf_op jit(solution)/shard_map/ppermute | solution.py:438
  38.6 0.0 copy-done.1
  38.6 0.8 %finish.1 = (f32[1,1,3,1,128]{4,3,2,1,0:T(1,128)}, bf16[1,1,1,128,256]{4,3,2,1,0:T(8,128)(2,1)}) custom-call(f32[1,80,128]{2,1,0:T(8,128)S(1)} %slice.21.refs_0_, bf16[1,80,128]{2,1,0:T(8,128)(2,1)S(1)} %collective-permute-done.10.refs_1_, f32[128,256]{1,0:T(8,128)S(1)} %get-tuple-element.46.refs_2_, bf16[64,256]{1,0:T(8,128)(2,1)S(1)} %bitcast.7), custom_call_target="tpu_custom_call" | custom-call | tf_op jit(solution)/shard_map/finish/pallas_call | solution.py:616
  (7 shorter events, 0.1 us)
Async XLA Ops:
  2.9 5.0 %collective-permute-start = (bf16[1,80,128]{2,1,0:T(8,128)(2,1)}, bf16[1,80,128]{2,1,0:T(8,128)(2,1)S(1)}, u32[]{:S(2)}, u32[]{:S(2)}) collective-permute-start(bf16[1,80,128]{2,1,0:T(8,128)(2,1)} %pack.1), channel_id=1, source_target_pairs={{0,1},{1,0},{2,3},{3,2},{4,5},{5,4},{6,7},{7,6},{8,9},{9,8},{10,11... | collective-permute-start | bytes 61448 | tf_op jit(solution)/shard_map/ppermute | solution.py:438
  7.9 7.0 %collective-permute-start.4 = (bf16[1,160,128]{2,1,0:T(8,128)(2,1)S(1)}, bf16[1,160,128]{2,1,0:T(8,128)(2,1)S(1)}, u32[]{:S(2)}, u32[]{:S(2)}) collective-permute-start(bf16[1,160,128]{2,1,0:T(8,128)(2,1)S(1)} %constant_dynamic-update-slice_fusion.refs_0_), channel_id=1, source_target_pairs={{0,4},{4,8},{8,12},{12,16},{16,20},{20,24},{24,28},{28,0},{1,5},{5... | collective-permute-start | bytes 122888 | tf_op jit(solution)/shard_map/ppermute | solution.py:438
  9.9 5.0 %collective-permute-start.2 = (bf16[1,160,128]{2,1,0:T(8,128)(2,1)S(1)}, bf16[1,160,128]{2,1,0:T(8,128)(2,1)S(1)}, u32[]{:S(2)}, u32[]{:S(2)}) collective-permute-start(bf16[1,160,128]{2,1,0:T(8,128)(2,1)S(1)} %constant_dynamic-update-slice_fusion.refs_0_), channel_id=1, source_target_pairs={{0,28},{4,0},{8,4},{12,8},{16,12},{20,16},{24,20},{28,24},{1,29},{... | collective-permute-start | bytes 122888 | tf_op jit(solution)/shard_map/ppermute | solution.py:438
  13.0 2.4 %collective-permute-start.1 = (bf16[1,160,128]{2,1,0:T(8,128)(2,1)S(1)}, bf16[1,160,128]{2,1,0:T(8,128)(2,1)S(1)}, u32[]{:S(2)}, u32[]{:S(2)}) collective-permute-start(bf16[1,160,128]{2,1,0:T(8,128)(2,1)S(1)} %constant_dynamic-update-slice_fusion.refs_0_), channel_id=1, source_target_pairs={{0,2},{2,0},{1,3},{3,1},{4,6},{6,4},{5,7},{7,5},{8,10},{10,8},{9,1... | collective-permute-start | bytes 122888 | tf_op jit(solution)/shard_map/ppermute | solution.py:438
  13.1 4.6 %copy-start = (bf16[256,256]{1,0:T(8,128)(2,1)S(1)}, bf16[256,256]{1,0:T(8,128)(2,1)}, u32[]{:S(2)}) copy-start(bf16[256,256]{1,0:T(8,128)(2,1)} %refs_1_.1) | copy-start | bytes 393220
  13.1 4.6 %copy-start.2 = (bf16[1,1,1,128,256]{4,3,2,1,0:T(8,128)(2,1)S(1)}, bf16[1,1,1,128,256]{4,3,2,1,0:T(8,128)(2,1)}, u32[]{:S(2)}) copy-start(bf16[1,1,1,128,256]{4,3,2,1,0:T(8,128)(2,1)} %refs_11_.1) | copy-start | bytes 196612
  13.1 4.6 %copy-start.3 = (f32[6,6]{1,0:T(8,128)S(1)}, f32[6,6]{1,0:T(8,128)}, u32[]{:S(2)}) copy-start(f32[6,6]{1,0:T(8,128)} %refs_5_.1) | copy-start | bytes 436
  13.1 4.6 %copy-start.4 = (s32[1,1,1,27]{3,2,1,0:T(1,128)S(1)}, s32[1,1,1,27]{3,2,1,0:T(1,128)}, u32[]{:S(2)}) copy-start(s32[1,1,1,27]{3,2,1,0:T(1,128)} %refs_0_.3) | copy-start | bytes 328
  13.1 4.6 %copy-start.5 = (bf16[64,256]{1,0:T(8,128)(2,1)S(1)}, bf16[64,256]{1,0:T(8,128)(2,1)}, u32[]{:S(2)}) copy-start(bf16[64,256]{1,0:T(8,128)(2,1)} %refs_7_.1) | copy-start | bytes 98308
  13.2 4.6 %copy-start.6 = (bf16[64,256]{1,0:T(8,128)(2,1)S(1)}, bf16[64,256]{1,0:T(8,128)(2,1)}, u32[]{:S(2)}) copy-start(bf16[64,256]{1,0:T(8,128)(2,1)} %refs_8_.1) | copy-start | bytes 98308
  13.2 4.6 %copy-start.7 = (f32[4,64]{1,0:T(4,128)S(1)}, f32[4,64]{1,0:T(4,128)}, u32[]{:S(2)}) copy-start(f32[4,64]{1,0:T(4,128)} %refs_6_.1) | copy-start | bytes 3076
  13.2 4.6 %copy-start.8 = (f32[256]{0:T(256)S(1)}, f32[256]{0:T(256)}, u32[]{:S(2)}) copy-start(f32[256]{0:T(256)} %param.23) | copy-start | bytes 3076
  14.9 2.7 %collective-permute-start.5 = (bf16[1,160,128]{2,1,0:T(8,128)(2,1)S(1)}, bf16[1,160,128]{2,1,0:T(8,128)(2,1)S(1)}, u32[]{:S(2)}, u32[]{:S(2)}) collective-permute-start(bf16[1,160,128]{2,1,0:T(8,128)(2,1)S(1)} %collective-permute-done.4.refs_3_), channel_id=1, source_target_pairs={{0,2},{2,0},{1,3},{3,1},{4,6},{6,4},{5,7},{7,5},{8,10},{10,8},{9,1... | collective-permute-start | bytes 122888 | tf_op jit(solution)/shard_map/ppermute | solution.py:438
  14.9 2.7 %collective-permute-start.3 = (bf16[1,160,128]{2,1,0:T(8,128)(2,1)S(1)}, bf16[1,160,128]{2,1,0:T(8,128)(2,1)S(1)}, u32[]{:S(2)}, u32[]{:S(2)}) collective-permute-start(bf16[1,160,128]{2,1,0:T(8,128)(2,1)S(1)} %collective-permute-done.2.refs_1_), channel_id=1, source_target_pairs={{0,2},{2,0},{1,3},{3,1},{4,6},{6,4},{5,7},{7,5},{8,10},{10,8},{9,1... | collective-permute-start | bytes 122888 | tf_op jit(solution)/shard_map/ppermute | solution.py:438
  22.9 3.7 %collective-permute-start.7 = (bf16[4,80,128]{2,1,0:T(8,128)(2,1)S(1)}, bf16[4,80,128]{2,1,0:T(8,128)(2,1)S(1)}, u32[]{:S(2)}, u32[]{:S(2)}) collective-permute-start(bf16[4,80,128]{2,1,0:T(8,128)(2,1)S(1)} %get-tuple-element.45), channel_id=1, source_target_pairs={{0,2},{2,0},{1,3},{3,1},{4,6},{6,4},{5,7},{7,5},{8,10},{10,8},{9,1... | collective-permute-start | bytes 245768 | tf_op jit(solution)/shard_map/ppermute | solution.py:438
  23.7 14.9 %copy-start.1 = (bf16[256,64]{0,1:T(8,128)(2,1)S(1)}, bf16[256,64]{0,1:T(8,128)(2,1)}, u32[]{:S(2)}) copy-start(bf16[256,64]{0,1:T(8,128)(2,1)} %param.17) | copy-start | bytes 98308
  26.6 3.7 %collective-permute-start.6 = (bf16[2,80,128]{2,1,0:T(8,128)(2,1)S(1)}, bf16[2,80,128]{2,1,0:T(8,128)(2,1)S(1)}, u32[]{:S(2)}, u32[]{:S(2)}) collective-permute-start(bf16[2,80,128]{2,1,0:T(8,128)(2,1)S(1)} %get-tuple-element.43), channel_id=1, source_target_pairs={{0,2},{2,0},{1,3},{3,1},{4,6},{6,4},{5,7},{7,5},{8,10},{10,8},{9,1... | collective-permute-start | bytes 122888 | tf_op jit(solution)/shard_map/ppermute | solution.py:438
  26.7 6.9 %collective-permute-start.8 = (bf16[2,80,128]{2,1,0:T(8,128)(2,1)S(1)}, bf16[2,80,128]{2,1,0:T(8,128)(2,1)S(1)}, u32[]{:S(2)}, u32[]{:S(2)}) collective-permute-start(bf16[2,80,128]{2,1,0:T(8,128)(2,1)S(1)} %get-tuple-element.52), channel_id=1, source_target_pairs={{0,28},{4,8},{8,4},{12,16},{16,12},{20,24},{24,20},{28,0},{1,29},{... | collective-permute-start | bytes 122888 | tf_op jit(solution)/shard_map/ppermute | solution.py:461
  30.2 4.0 %collective-permute-start.9 = (bf16[2,80,128]{2,1,0:T(8,128)(2,1)S(1)}, bf16[2,80,128]{2,1,0:T(8,128)(2,1)S(1)}, u32[]{:S(2)}, u32[]{:S(2)}) collective-permute-start(bf16[2,80,128]{2,1,0:T(8,128)(2,1)S(1)} %get-tuple-element.53), channel_id=1, source_target_pairs={{0,4},{4,0},{8,12},{12,8},{16,20},{20,16},{24,28},{28,24},{1,5},{5... | collective-permute-start | bytes 122888 | tf_op jit(solution)/shard_map/ppermute | solution.py:462
  34.3 4.3 %collective-permute-start.10 = (bf16[1,80,128]{2,1,0:T(8,128)(2,1)S(1)}, bf16[1,80,128]{2,1,0:T(8,128)(2,1)S(1)}, u32[]{:S(2)}, u32[]{:S(2)}) collective-permute-start(bf16[1,80,128]{2,1,0:T(8,128)(2,1)S(1)} %slice.24), channel_id=1, source_target_pairs={{0,1},{1,0},{2,3},{3,2},{4,5},{5,4},{6,7},{7,6},{8,9},{9,8},{10,11... | collective-permute-start | bytes 61448 | tf_op jit(solution)/shard_map/ppermute | solution.py:438

commit v5 on v4

--- a/solution.py
+++ b/solution.py
@@ -239,6 +239,7 @@
 
     def backward(pair, carry):
         cell_a, cell_b, _, _, rows = rows_of(pair, tables, xj)
+        settle(jnp.maximum(pair - 1, 0))
         totals = [jnp.zeros((CHUNK, LANES), F32) for _ in range(3)]
         for block in range(CHUNKS):
             at = slice(block * CHUNK, (block + 1) * CHUNK)
@@ -263,7 +264,6 @@
             total = (2.0 / KAPPA) * jnp.sum(totals[axis], axis=0, keepdims=True)
             pg[cell_a, axis : axis + 1] += total[:, :SLOTS]
             pg[cell_b, axis : axis + 1] += total[:, SLOTS:]
-        settle(jnp.maximum(pair - 1, 0))
         pbuf[...] = dot_nn(grad[...], rmat[pair + 1])
         bbuf[...] = dot_nn(gradt[...], tiles[pair])
         return carry
@@ -398,20 +398,22 @@
 
 def rest_kernel(sizes, counts, *refs):
     nyu = counts[1]
-    list_ref, w_hidden_ref, xi, xj, *saved = refs[:9]
-    grad, gradt, fi_in, pre_ref, heat_ref = refs[9:14]
-    energy_ref, direct_ref = refs[14:16]
-    out_refs = refs[16 : 16 + nyu]
-    cell_of, slot_of, shift_of, pbuf, bbuf, fi, cg, pg = refs[16 + nyu :]
+    list_ref, xi, xj, *saved = refs[:8]
+    grad, gradt, fi_in = refs[8:11]
+    out_refs = refs[11 : 11 + nyu]
+    cell_of, slot_of, shift_of, pbuf, bbuf, fi, cg, pg = refs[11 + nyu :]
     tables = (cell_of, slot_of, shift_of)
     trips = tabulate(lambda tile: list_ref[0, 0, 0, tile], tables, False, sizes, counts)
-    energy_ref[0, 0] = row_sums(heat_ref[...])
-    direct_ref[...] = dot_nt(pre_ref[...], w_hidden_ref[...])
     fi[...] = fi_in[...]
     backward_tiles(trips, tables, xi, xj, saved, grad, gradt, pbuf, bbuf, fi, cg, pg)
     for axis in range(3):
         pg[0, axis : axis + 1] -= (2.0 / KAPPA) * row_sums(fi[axis])
     write_out(out_refs, counts, cg, pg, [0])
+
+
+def direct_kernel(sizes, counts, pre_ref, heat_ref, w_hidden_ref, energy_ref, direct_ref):
+    energy_ref[0, 0] = row_sums(heat_ref[...])
+    direct_ref[...] = dot_nt(pre_ref[...], w_hidden_ref[...])
 
 
 def finish_kernel(count, *refs):
@@ -595,18 +597,25 @@
     from_far = swapped(sends, "gx")
     rest = call(
         rest_kernel,
-        [((1, 1, 1, SLOTS), F32), ((SLOTS, D), F32), ((nzu, ROWS, SLOTS), F32)]
-        + [((nzu, ROWS, SLOTS), BF16)] * (nyu - 1),
+        [((nzu, ROWS, SLOTS), F32)] + [((nzu, ROWS, SLOTS), BF16)] * (nyu - 1),
         table_scratch()
         + buffers
         + [pltpu.VMEM((3,) + square, F32)]
         + sums_scratch(near_cells),
         12,
         [SMEM],
-        pair_list, w_hidden, xi, xj, *saved, grad, gradt, force_in, pre_grad, heat,
+        pair_list, xi, xj, *saved, grad, gradt, force_in,
     )
-    energy, direct, total = rest[:3]
-    for got in returned(rest[3:], "gy"):
+    energy, direct = call(
+        direct_kernel,
+        [((1, 1, 1, SLOTS), F32), ((SLOTS, D), F32)],
+        [],
+        4,
+        [],
+        pre_grad, heat, w_hidden,
+    )
+    total = rest[0]
+    for got in returned(rest[1:], "gy"):
         total = total + got.astype(F32)
     for got in from_far:
         total = total + got.astype(F32)

time: 39.7 us -> 39.2 us (0.987)
  waiting for transfers between devices: 8.74 us -> 8.3 us
    ppermute x9, waiting for transfers between devices: 4.69 us -> 4.15 us  [shifted(): lax.ppermute(value, axis, [(i, (i + steps) % count) for i in range(count)])]
    pallas_call x3 -> x4, Pallas kernels: 10.2 us -> 10.5 us  [call(): pl.pallas_call(lambda *refs: kernel(sizes, counts, *refs), out_shape=[jax...]
  transfers between devices with their start and end apart: 11 -> 11, of which waited for: 5 -> 5; matrix products, arithmetic and copies ran while one was open for 2% -> 2% of each run, Pallas kernels for 13% -> 14%
where the time goes in v5:
time: 39.2 us; the launch traced here: 39 us
  starting transfers between devices  15.3 us (39%)
  Pallas kernels  12.9 us (33%)
  waiting for transfers between devices  8.3 us (21%)
  between operations  1.48 us (4%)
  local copies, waits for them, and re-layouts  0.84 us (2%)
    ppermute x9, starting transfers between devices, shifted(): lax.ppermute(value, axis, [(i, (i + steps) % count) for i in range(count)])  11.8 us
    pallas_call x4, Pallas kernels, call(): pl.pallas_call(lambda *refs: kernel(sizes, counts, *refs), out_shape=[jax...  10.5 us
    ppermute x9, waiting for transfers between devices, shifted(): lax.ppermute(value, axis, [(i, (i + steps) % count) for i in range(count)])  4.15 us
    ppermute x1, starting transfers between devices, swapped(): far = lax.ppermute(parts[0], axis, ring)  3.46 us
    ppermute x1, waiting for transfers between devices, swapped(): far = lax.ppermute(parts[0], axis, ring)  3.35 us
    pallas_call x1, Pallas kernels, layer(): pl.pallas_call(pack_kernel, out_shape=jax.ShapeDtypeStruct((1, ROWS, SLOT...  1.65 us
    pallas_call x1, Pallas kernels, layer(): pl.pallas_call(lambda *refs: finish_kernel(len(arrived), *refs), out_shap...  0.84 us
    ppermute x1, waiting for transfers between devices, swapped(): near = lax.ppermute(parts[1], axis, [(i, i ^ 1) for i in range(count)])  0.79 us
  transfers between devices with their start and end apart: 11, of which 5 were waited for; matrix products, arithmetic and copies ran while one was open for 2% of the time, Pallas kernels for 14%

profile of v5, /device:TPU:0, one launch (start us, length us, event | category | flops | bytes accessed | tf_op | source)
XLA Modules:
  0.0 39.0 jit_solution(10619248069335468573)
XLA Ops:
  1.3 1.6 %pack.1 = bf16[1,80,128]{2,1,0:T(8,128)(2,1)} custom-call(s32[1,1,1]{2,1,0:T(1,128)S(6)} %copy.17.counts_ref, bf16[1,1,1,128,256]{4,3,2,1,0:T(8,128)(2,1)} %refs_11_.1, f32[1,1,3,1,128]{4,3,2,1,0:T(1,128)} %bitcast.9, s32[1,1,1,128]{3,2,1,0:T(1,128)} %species_ref.1, bf16[64,256]{1,0:T(8,128)(2,1)} %bitcast.6, s32[1,1,1,27]{3,2,1,0:T(1,128)} %refs_0_.3, ...), custom_call_target="tpu_custom_call" | custom-call | tf_op jit(solution)/shard_map/pack/pallas_call | solution.py:479
  2.9 3.0 %collective-permute-start = (bf16[1,80,128]{2,1,0:T(8,128)(2,1)}, bf16[1,80,128]{2,1,0:T(8,128)(2,1)S(1)}, u32[]{:S(2)}, u32[]{:S(2)}) collective-permute-start(bf16[1,80,128]{2,1,0:T(8,128)(2,1)} %pack.1), channel_id=1, source_target_pairs={{0,1},{1,0},{2,3},{3,2},{4,5},{5,4},{6,7},{7,6},{8,9},{9,8},{10,11... | collective-permute-start | bytes 61448 | tf_op jit(solution)/shard_map/ppermute | solution.py:440
  5.9 0.8 %pad.4 = bf16[1,160,128]{2,1,0:T(8,128)(2,1)S(1)} pad(bf16[1,80,128]{2,1,0:T(8,128)(2,1)} %pack.1, bf16[]{:T(256)} %constant.50.clone.1), padding=0_0x0_80x0_0 | pad | bytes 61442 | tf_op jit(solution)/shard_map/jit(_pad)/pad | solution.py:491
  6.7 1.2 %collective-permute-done = bf16[1,80,128]{2,1,0:T(8,128)(2,1)S(1)} collective-permute-done((bf16[1,80,128]{2,1,0:T(8,128)(2,1)}, bf16[1,80,128]{2,1,0:T(8,128)(2,1)S(1)}, u32[]{:S(2)}, u32[]{:S(2)}) %collective-permute-start) | collective-permute-done | bytes 20512 | tf_op jit(solution)/shard_map/ppermute | solution.py:440
  7.9 0.0 collective-permute-start.5
  7.9 2.0 %collective-permute-start.3 = (bf16[1,160,128]{2,1,0:T(8,128)(2,1)S(1)}, bf16[1,160,128]{2,1,0:T(8,128)(2,1)S(1)}, u32[]{:S(2)}, u32[]{:S(2)}) collective-permute-start(bf16[1,160,128]{2,1,0:T(8,128)(2,1)S(1)} %constant_dynamic-update-slice_fusion.refs_0_), channel_id=1, source_target_pairs={{0,4},{4,8},{8,12},{12,16},{16,20},{20,24},{24,28},{28,0},{1,5},{5... | collective-permute-start | bytes 122888 | tf_op jit(solution)/shard_map/ppermute | solution.py:440
  9.9 3.1 %collective-permute-start.1 = (bf16[1,160,128]{2,1,0:T(8,128)(2,1)S(1)}, bf16[1,160,128]{2,1,0:T(8,128)(2,1)S(1)}, u32[]{:S(2)}, u32[]{:S(2)}) collective-permute-start(bf16[1,160,128]{2,1,0:T(8,128)(2,1)S(1)} %constant_dynamic-update-slice_fusion.refs_0_), channel_id=1, source_target_pairs={{0,28},{4,0},{8,4},{12,8},{16,12},{20,16},{24,20},{28,24},{1,29},{... | collective-permute-start | bytes 122888 | tf_op jit(solution)/shard_map/ppermute | solution.py:440
  13.1 0.1 fusion.refs_10_
  13.2 0.0 copy-start.1
  13.2 0.0 copy-start.2
  13.2 0.0 copy-start.3
  13.2 0.0 copy-start.4
  13.2 0.0 copy-start.5
  13.2 0.0 copy-start.6
  13.2 0.0 copy-start.7
  13.2 0.0 copy-start.8
  13.3 1.9 %collective-permute-done.3.refs_3_ = bf16[1,160,128]{2,1,0:T(8,128)(2,1)S(1)} collective-permute-done((bf16[1,160,128]{2,1,0:T(8,128)(2,1)S(1)}, bf16[1,160,128]{2,1,0:T(8,128)(2,1)S(1)}, u32[]{:S(2)}, u32[]{:S(2)}) %collective-permute-start.3) | collective-permute-done | bytes 40992 | tf_op jit(solution)/shard_map/ppermute | solution.py:440
  15.2 0.0 collective-permute-start.4
  15.2 0.0 collective-permute-done.1.refs_1_
  15.2 0.5 %collective-permute-start.2 = (bf16[1,160,128]{2,1,0:T(8,128)(2,1)S(1)}, bf16[1,160,128]{2,1,0:T(8,128)(2,1)S(1)}, u32[]{:S(2)}, u32[]{:S(2)}) collective-permute-start(bf16[1,160,128]{2,1,0:T(8,128)(2,1)S(1)} %collective-permute-done.1.refs_1_), channel_id=1, source_target_pairs={{0,2},{2,0},{1,3},{3,1},{4,6},{6,4},{5,7},{7,5},{8,10},{10,8},{9,1... | collective-permute-start | bytes 122888 | tf_op jit(solution)/shard_map/ppermute | solution.py:440
  15.7 0.0 collective-permute-done.5.refs_1_
  15.7 2.2 %shard_map.139 = (f32[3,128,128]{2,1,0:T(8,128)S(1)}, f32[128,128]{1,0:T(8,128)S(1)}, bf16[128,128]{1,0:T(8,128)(2,1)S(1)}, f32[4,8,128]{2,1,0:T(8,128)S(1)}, f3...) custom-call(bf16[1,160,128]{2,1,0:T(8,128)(2,1)S(1)} %constant_dynam, ...), custom_call_target="tpu_custom_call" | custom-call | flops 1000000000 | bytes 4000000 | tf_op jit(solution)/shard_map/pallas_call | solution.py:525
  17.9 0.0 collective-permute-done.4.refs_4_
  17.9 0.0 collective-permute-done.2.refs_2_
  17.9 0.0 copy-done.1
  17.9 0.0 copy-done.2
  17.9 0.0 copy-done.3
  18.0 0.0 copy-done.4
  18.0 0.0 copy-done.5
  18.0 0.0 copy-done.6
  18.0 0.0 copy-done.7
  18.0 0.0 copy-done.8
  18.0 5.0 %shard_map.140 = (bf16[512,256]{1,0:T(8,128)(2,1)S(1)}, bf16[256,512]{1,0:T(8,128)(2,1)S(1)}, f32[3,128,128]{2,1,0:T(8,128)S(1)}, bf16[128,256]{1,0:T(8,128)(2,1...) custom-call(s32[1,1,1,27]{3,2,1,0:T(1,128)S(1)} %copy-done.3, ...), custom_call_target="tpu_custom_call" | custom-call | flops 1000000000 | bytes 4000000 | tf_op jit(solution)/shard_map/pallas_call | solution.py:525
  23.0 0.7 %collective-permute-start.7 = (bf16[4,80,128]{2,1,0:T(8,128)(2,1)S(1)}, bf16[4,80,128]{2,1,0:T(8,128)(2,1)S(1)}, u32[]{:S(2)}, u32[]{:S(2)}) collective-permute-start(bf16[4,80,128]{2,1,0:T(8,128)(2,1)S(1)} %get-tuple-element.45), channel_id=1, source_target_pairs={{0,2},{2,0},{1,3},{3,1},{4,6},{6,4},{5,7},{7,5},{8,10},{10,8},{9,1... | collective-permute-start | bytes 245768 | tf_op jit(solution)/shard_map/ppermute | solution.py:440
  23.7 2.5 %shard_map.142 = (f32[2,80,128]{2,1,0:T(8,128)S(1)}, bf16[2,80,128]{2,1,0:T(8,128)(2,1)S(1)}) custom-call(s32[1,1,1,27]{3,2,1,0:T(1,128)S(1)} %copy-done.3, f32[3,128,128]{2,1,0:T(8,128)S(1)} %get-tuple-element.26.refs_13_.refs_1_, f32[4,8,128]{2,1,0:T(8,128)S(1)} %get-tuple-element.33.refs_2_, bf16[5,512,256]{2,1,0:T(8,128)(2,1)S(1)} %get-tuple-element.34.refs_3_, ...), custom_call_target="tpu_custom_call" | custom-call | flops 1000000000 | bytes 4000000 | tf_op jit(solution)/shard_map/pallas_call | solution.py:525
  26.3 0.0 collective-permute-start.6
  26.3 0.0 collective-permute-done.7
  26.3 3.5 %collective-permute-start.8 = (bf16[2,80,128]{2,1,0:T(8,128)(2,1)S(1)}, bf16[2,80,128]{2,1,0:T(8,128)(2,1)S(1)}, u32[]{:S(2)}, u32[]{:S(2)}) collective-permute-start(bf16[2,80,128]{2,1,0:T(8,128)(2,1)S(1)} %get-tuple-element.52), channel_id=1, source_target_pairs={{0,28},{4,8},{8,4},{12,16},{16,12},{20,24},{24,20},{28,0},{1,29},{... | collective-permute-start | bytes 122888 | tf_op jit(solution)/shard_map/ppermute | solution.py:463
  29.8 0.0 collective-permute-start.9
  29.8 0.0 collective-permute-done.6
  29.8 3.4 %collective-permute-done.8 = bf16[2,80,128]{2,1,0:T(8,128)(2,1)S(1)} collective-permute-done((bf16[2,80,128]{2,1,0:T(8,128)(2,1)S(1)}, bf16[2,80,128]{2,1,0:T(8,128)(2,1)S(1)}, u32[]{:S(2)}, u32[]{:S(2)}) %collective-permute-start.8) | collective-permute-done | bytes 40992 | tf_op jit(solution)/shard_map/ppermute | solution.py:463
  33.1 0.8 %collective-permute-done.9 = bf16[2,80,128]{2,1,0:T(8,128)(2,1)S(1)} collective-permute-done((bf16[2,80,128]{2,1,0:T(8,128)(2,1)S(1)}, bf16[2,80,128]{2,1,0:T(8,128)(2,1)S(1)}, u32[]{:S(2)}, u32[]{:S(2)}) %collective-permute-start.9) | collective-permute-done | bytes 40992 | tf_op jit(solution)/shard_map/ppermute | solution.py:464
  34.0 2.4 %collective-permute-start.10 = (bf16[1,80,128]{2,1,0:T(8,128)(2,1)S(1)}, bf16[1,80,128]{2,1,0:T(8,128)(2,1)S(1)}, u32[]{:S(2)}, u32[]{:S(2)}) collective-permute-start(bf16[1,80,128]{2,1,0:T(8,128)(2,1)S(1)} %slice.24), channel_id=1, source_target_pairs={{0,1},{1,0},{2,3},{3,2},{4,5},{5,4},{6,7},{7,6},{8,9},{9,8},{10,11... | collective-permute-start | bytes 61448 | tf_op jit(solution)/shard_map/ppermute | solution.py:440
  36.4 0.0 copy-start
  36.4 0.7 %shard_map.141 = (f32[1,1,1,128]{3,2,1,0:T(1,128)}, f32[128,256]{1,0:T(8,128)S(1)}) custom-call(bf16[128,256]{1,0:T(8,128)(2,1)S(1)} %get-tuple-element.30.refs_0_, f32[128,256]{1,0:T(8,128)S(1)} %get-tuple-element.31.refs_1_, bf16[256,256]{1,0:T(8,128)(2,1)S(1)} %copy-done.4), custom_call_target="tpu_custom_call" | custom-call | flops 1000000000 | bytes 4000000 | tf_op jit(solution)/shard_map/pallas_call | solution.py:525
  37.1 1.0 %collective-permute-done.10.refs_1_ = bf16[1,80,128]{2,1,0:T(8,128)(2,1)S(1)} collective-permute-done((bf16[1,80,128]{2,1,0:T(8,128)(2,1)S(1)}, bf16[1,80,128]{2,1,0:T(8,128)(2,1)S(1)}, u32[]{:S(2)}, u32[]{:S(2)}) %collective-permute-start.10) | collective-permute-done | bytes 20512 | tf_op jit(solution)/shard_map/ppermute | solution.py:440
  38.1 0.0 copy-done
  38.1 0.8 %finish.1 = (f32[1,1,3,1,128]{4,3,2,1,0:T(1,128)}, bf16[1,1,1,128,256]{4,3,2,1,0:T(8,128)(2,1)}) custom-call(f32[1,80,128]{2,1,0:T(8,128)S(1)} %slice.21.refs_0_, bf16[1,80,128]{2,1,0:T(8,128)(2,1)S(1)} %collective-permute-done.10.refs_1_, f32[128,256]{1,0:T(8,128)S(1)} %get-tuple-element.46.refs_2_, bf16[64,256]{1,0:T(8,128)(2,1)S(1)} %bitcast.7), custom_call_target="tpu_custom_call" | custom-call | tf_op jit(solution)/shard_map/finish/pallas_call | solution.py:625
  (7 shorter events, 0.1 us)
Async XLA Ops:
  2.9 5.0 %collective-permute-start = (bf16[1,80,128]{2,1,0:T(8,128)(2,1)}, bf16[1,80,128]{2,1,0:T(8,128)(2,1)S(1)}, u32[]{:S(2)}, u32[]{:S(2)}) collective-permute-start(bf16[1,80,128]{2,1,0:T(8,128)(2,1)} %pack.1), channel_id=1, source_target_pairs={{0,1},{1,0},{2,3},{3,2},{4,5},{5,4},{6,7},{7,6},{8,9},{9,8},{10,11... | collective-permute-start | bytes 61448 | tf_op jit(solution)/shard_map/ppermute | solution.py:440
  7.9 7.8 %collective-permute-start.5 = (bf16[1,160,128]{2,1,0:T(8,128)(2,1)S(1)}, bf16[1,160,128]{2,1,0:T(8,128)(2,1)S(1)}, u32[]{:S(2)}, u32[]{:S(2)}) collective-permute-start(bf16[1,160,128]{2,1,0:T(8,128)(2,1)S(1)} %constant_dynamic-update-slice_fusion.refs_0_), channel_id=1, source_target_pairs={{0,2},{2,0},{1,3},{3,1},{4,6},{6,4},{5,7},{7,5},{8,10},{10,8},{9,1... | collective-permute-start | bytes 122888 | tf_op jit(solution)/shard_map/ppermute | solution.py:440
  7.9 7.3 %collective-permute-start.3 = (bf16[1,160,128]{2,1,0:T(8,128)(2,1)S(1)}, bf16[1,160,128]{2,1,0:T(8,128)(2,1)S(1)}, u32[]{:S(2)}, u32[]{:S(2)}) collective-permute-start(bf16[1,160,128]{2,1,0:T(8,128)(2,1)S(1)} %constant_dynamic-update-slice_fusion.refs_0_), channel_id=1, source_target_pairs={{0,4},{4,8},{8,12},{12,16},{16,20},{20,24},{24,28},{28,0},{1,5},{5... | collective-permute-start | bytes 122888 | tf_op jit(solution)/shard_map/ppermute | solution.py:440
  9.9 5.2 %collective-permute-start.1 = (bf16[1,160,128]{2,1,0:T(8,128)(2,1)S(1)}, bf16[1,160,128]{2,1,0:T(8,128)(2,1)S(1)}, u32[]{:S(2)}, u32[]{:S(2)}) collective-permute-start(bf16[1,160,128]{2,1,0:T(8,128)(2,1)S(1)} %constant_dynamic-update-slice_fusion.refs_0_), channel_id=1, source_target_pairs={{0,28},{4,0},{8,4},{12,8},{16,12},{20,16},{24,20},{28,24},{1,29},{... | collective-permute-start | bytes 122888 | tf_op jit(solution)/shard_map/ppermute | solution.py:440
  13.2 4.8 %copy-start.1 = (bf16[1,1,1,128,256]{4,3,2,1,0:T(8,128)(2,1)S(1)}, bf16[1,1,1,128,256]{4,3,2,1,0:T(8,128)(2,1)}, u32[]{:S(2)}) copy-start(bf16[1,1,1,128,256]{4,3,2,1,0:T(8,128)(2,1)} %refs_11_.1) | copy-start | bytes 196612
  13.2 4.8 %copy-start.2 = (f32[6,6]{1,0:T(8,128)S(1)}, f32[6,6]{1,0:T(8,128)}, u32[]{:S(2)}) copy-start(f32[6,6]{1,0:T(8,128)} %refs_5_.1) | copy-start | bytes 436
  13.2 4.8 %copy-start.3 = (s32[1,1,1,27]{3,2,1,0:T(1,128)S(1)}, s32[1,1,1,27]{3,2,1,0:T(1,128)}, u32[]{:S(2)}) copy-start(s32[1,1,1,27]{3,2,1,0:T(1,128)} %refs_0_.3) | copy-start | bytes 328
  13.2 4.8 %copy-start.4 = (bf16[256,256]{1,0:T(8,128)(2,1)S(1)}, bf16[256,256]{1,0:T(8,128)(2,1)}, u32[]{:S(2)}) copy-start(bf16[256,256]{1,0:T(8,128)(2,1)} %refs_2_.1) | copy-start | bytes 393220
  13.2 4.8 %copy-start.5 = (bf16[64,256]{1,0:T(8,128)(2,1)S(1)}, bf16[64,256]{1,0:T(8,128)(2,1)}, u32[]{:S(2)}) copy-start(bf16[64,256]{1,0:T(8,128)(2,1)} %refs_7_.1) | copy-start | bytes 98308
  13.2 4.8 %copy-start.6 = (bf16[64,256]{1,0:T(8,128)(2,1)S(1)}, bf16[64,256]{1,0:T(8,128)(2,1)}, u32[]{:S(2)}) copy-start(bf16[64,256]{1,0:T(8,128)(2,1)} %refs_8_.1) | copy-start | bytes 98308
  13.2 4.8 %copy-start.7 = (f32[4,64]{1,0:T(4,128)S(1)}, f32[4,64]{1,0:T(4,128)}, u32[]{:S(2)}) copy-start(f32[4,64]{1,0:T(4,128)} %refs_6_.1) | copy-start | bytes 3076
  13.2 4.8 %copy-start.8 = (f32[256]{0:T(256)S(1)}, f32[256]{0:T(256)}, u32[]{:S(2)}) copy-start(f32[256]{0:T(256)} %param.23) | copy-start | bytes 3076
  15.2 2.7 %collective-permute-start.4 = (bf16[1,160,128]{2,1,0:T(8,128)(2,1)S(1)}, bf16[1,160,128]{2,1,0:T(8,128)(2,1)S(1)}, u32[]{:S(2)}, u32[]{:S(2)}) collective-permute-start(bf16[1,160,128]{2,1,0:T(8,128)(2,1)S(1)} %collective-permute-done.3.refs_3_), channel_id=1, source_target_pairs={{0,2},{2,0},{1,3},{3,1},{4,6},{6,4},{5,7},{7,5},{8,10},{10,8},{9,1... | collective-permute-start | bytes 122888 | tf_op jit(solution)/shard_map/ppermute | solution.py:440
  15.2 2.7 %collective-permute-start.2 = (bf16[1,160,128]{2,1,0:T(8,128)(2,1)S(1)}, bf16[1,160,128]{2,1,0:T(8,128)(2,1)S(1)}, u32[]{:S(2)}, u32[]{:S(2)}) collective-permute-start(bf16[1,160,128]{2,1,0:T(8,128)(2,1)S(1)} %collective-permute-done.1.refs_1_), channel_id=1, source_target_pairs={{0,2},{2,0},{1,3},{3,1},{4,6},{6,4},{5,7},{7,5},{8,10},{10,8},{9,1... | collective-permute-start | bytes 122888 | tf_op jit(solution)/shard_map/ppermute | solution.py:440
  23.0 3.3 %collective-permute-start.7 = (bf16[4,80,128]{2,1,0:T(8,128)(2,1)S(1)}, bf16[4,80,128]{2,1,0:T(8,128)(2,1)S(1)}, u32[]{:S(2)}, u32[]{:S(2)}) collective-permute-start(bf16[4,80,128]{2,1,0:T(8,128)(2,1)S(1)} %get-tuple-element.45), channel_id=1, source_target_pairs={{0,2},{2,0},{1,3},{3,1},{4,6},{6,4},{5,7},{7,5},{8,10},{10,8},{9,1... | collective-permute-start | bytes 245768 | tf_op jit(solution)/shard_map/ppermute | solution.py:440
  26.3 3.5 %collective-permute-start.6 = (bf16[2,80,128]{2,1,0:T(8,128)(2,1)S(1)}, bf16[2,80,128]{2,1,0:T(8,128)(2,1)S(1)}, u32[]{:S(2)}, u32[]{:S(2)}) collective-permute-start(bf16[2,80,128]{2,1,0:T(8,128)(2,1)S(1)} %get-tuple-element.43), channel_id=1, source_target_pairs={{0,2},{2,0},{1,3},{3,1},{4,6},{6,4},{5,7},{7,5},{8,10},{10,8},{9,1... | collective-permute-start | bytes 122888 | tf_op jit(solution)/shard_map/ppermute | solution.py:440
  26.3 6.8 %collective-permute-start.8 = (bf16[2,80,128]{2,1,0:T(8,128)(2,1)S(1)}, bf16[2,80,128]{2,1,0:T(8,128)(2,1)S(1)}, u32[]{:S(2)}, u32[]{:S(2)}) collective-permute-start(bf16[2,80,128]{2,1,0:T(8,128)(2,1)S(1)} %get-tuple-element.52), channel_id=1, source_target_pairs={{0,28},{4,8},{8,4},{12,16},{16,12},{20,24},{24,20},{28,0},{1,29},{... | collective-permute-start | bytes 122888 | tf_op jit(solution)/shard_map/ppermute | solution.py:463
  29.8 4.2 %collective-permute-start.9 = (bf16[2,80,128]{2,1,0:T(8,128)(2,1)S(1)}, bf16[2,80,128]{2,1,0:T(8,128)(2,1)S(1)}, u32[]{:S(2)}, u32[]{:S(2)}) collective-permute-start(bf16[2,80,128]{2,1,0:T(8,128)(2,1)S(1)} %get-tuple-element.53), channel_id=1, source_target_pairs={{0,4},{4,0},{8,12},{12,8},{16,20},{20,16},{24,28},{28,24},{1,5},{5... | collective-permute-start | bytes 122888 | tf_op jit(solution)/shard_map/ppermute | solution.py:464
  34.0 4.1 %collective-permute-start.10 = (bf16[1,80,128]{2,1,0:T(8,128)(2,1)S(1)}, bf16[1,80,128]{2,1,0:T(8,128)(2,1)S(1)}, u32[]{:S(2)}, u32[]{:S(2)}) collective-permute-start(bf16[1,80,128]{2,1,0:T(8,128)(2,1)S(1)} %slice.24), channel_id=1, source_target_pairs={{0,1},{1,0},{2,3},{3,2},{4,5},{5,4},{6,7},{7,6},{8,9},{9,8},{10,11... | collective-permute-start | bytes 61448 | tf_op jit(solution)/shard_map/ppermute | solution.py:440
  36.4 1.8 %copy-start = (bf16[256,64]{0,1:T(8,128)(2,1)S(1)}, bf16[256,64]{0,1:T(8,128)(2,1)}, u32[]{:S(2)}) copy-start(bf16[256,64]{0,1:T(8,128)(2,1)} %param.17) | copy-start | bytes 98308

commit v6 on v5

--- a/solution.py
+++ b/solution.py
@@ -168,14 +168,18 @@
     return out
 
 
-def forward_tiles(trips, tables, xi, xj, chan, weight, saved, acc, tile_now, rmat_now):
+def forward_tiles(trips, tables, xi, xj, chan, weight, saved, acc):
     tiles, rmat, s_all, r_all, wb_all = saved
-    tile_now[...] = jnp.zeros_like(tile_now)
-    rmat_now[...] = jnp.zeros_like(rmat_now)
 
     def forward(pair, carry):
-        acc[...] += dot_nt(tile_now[...], rmat_now[...])
         cell_a, cell_b, weight_a, weight_b, rows = rows_of(pair, tables, xj)
+        values = jnp.concatenate([chan[cell_a], chan[cell_b]], axis=1)
+        rmat[pair, :CHANNELS] = values
+        wide = values.astype(F32)
+        for axis in range(3):
+            base = (axis + 1) * CHANNELS
+            scaled = (wide * rows[axis]).astype(BF16)
+            rmat[pair, base : base + CHANNELS] = scaled
         for block in range(CHUNKS):
             at = slice(block * CHUNK, (block + 1) * CHUNK)
             dx, dy, dz = relative(rows, xi, block)
@@ -193,22 +197,12 @@
                 base = block * 4 * CHUNK + k * CHUNK
                 rounded = tile.astype(BF16)
                 tiles[pair, base : base + CHUNK] = rounded
-                tile_now[base : base + CHUNK] = rounded
                 if k + 1 < NBASIS:
                     tile = tile * ratio
-        values = jnp.concatenate([chan[cell_a], chan[cell_b]], axis=1)
-        rmat[pair, :CHANNELS] = values
-        rmat_now[:CHANNELS] = values
-        wide = values.astype(F32)
-        for axis in range(3):
-            base = (axis + 1) * CHANNELS
-            scaled = (wide * rows[axis]).astype(BF16)
-            rmat[pair, base : base + CHANNELS] = scaled
-            rmat_now[base : base + CHANNELS] = scaled
+        acc[...] += dot_nt(tiles[pair], rmat[pair])
         return carry
 
     lax.fori_loop(0, trips, forward, 0)
-    acc[...] += dot_nt(tile_now[...], rmat_now[...])
 
 
 def backward_tiles(trips, tables, xi, xj, saved, grad, gradt, pbuf, bbuf, fi, cg, pg):
@@ -240,6 +234,7 @@
     def backward(pair, carry):
         cell_a, cell_b, _, _, rows = rows_of(pair, tables, xj)
         settle(jnp.maximum(pair - 1, 0))
+        bbuf[...] = dot_nn(gradt[...], tiles[pair])
         totals = [jnp.zeros((CHUNK, LANES), F32) for _ in range(3)]
         for block in range(CHUNKS):
             at = slice(block * CHUNK, (block + 1) * CHUNK)
@@ -265,7 +260,6 @@
             pg[cell_a, axis : axis + 1] += total[:, :SLOTS]
             pg[cell_b, axis : axis + 1] += total[:, SLOTS:]
         pbuf[...] = dot_nn(grad[...], rmat[pair + 1])
-        bbuf[...] = dot_nn(gradt[...], tiles[pair])
         return carry
 
     lax.fori_loop(0, trips, backward, 0)
@@ -289,9 +283,7 @@
     _, nyu, _ = counts
     msg_refs = refs[:nyu]
     xi, code_ref, onehot_ref, xj, acc, *saved = refs[nyu : 10 + nyu]
-    (
-        cell_of, slot_of, shift_of, weight, chan, tile_now, rmat_now, list_row, list_ref, sem,
-    ) = refs[10 + nyu :]
+    (cell_of, slot_of, shift_of, weight, chan, _, _, list_row, list_ref, sem) = refs[10 + nyu :]
     tables = (cell_of, slot_of, shift_of)
     tail = msg_refs[0][0, CHANNELS:ROWS].astype(F32)
     extra = tail[EXTRA_ROW - CHANNELS : EXTRA_ROW - CHANNELS + NSPEC]
@@ -314,7 +306,7 @@
     trips = tabulate(lambda tile: list_ref[0, LIST_LANE + tile], tables, False, sizes, counts)
     weight[0] = jnp.where(lane == sub, 0.0, weight[0])
     acc[...] = jnp.zeros_like(acc)
-    forward_tiles(trips, tables, xi, xj, chan, weight, saved, acc, tile_now, rmat_now)
+    forward_tiles(trips, tables, xi, xj, chan, weight, saved, acc)
 
 
 def outer_kernel(sizes, counts, *refs):
@@ -328,7 +320,7 @@
     out_refs = refs[17 : 17 + nyu]
     (
         cell_of, slot_of, shift_of, weight, xj, chan, tiles, rmat, s_all, r_all, wb_all,
-        acc, pbuf, bbuf, tile_now, rmat_now, cg, pg, hbuf,
+        acc, pbuf, bbuf, _, _, cg, pg, hbuf,
     ) = refs[17 + nyu :]
     tables = (cell_of, slot_of, shift_of)
     saved = (tiles, rmat, s_all, r_all, wb_all)
@@ -337,7 +329,7 @@
     strengths(codes, onehot_ref[...], scale_ref[...], weight)
     acc[...] = acc_in[...]
     hbuf[...] = dot_nn(feats_ref[0, 0, 0], w_hidden_ref[...])
-    forward_tiles(trips, tables, xi, xj, chan, weight, saved, acc, tile_now, rmat_now)
+    forward_tiles(trips, tables, xi, xj, chan, weight, saved, acc)
 
     radial = radial_ref[...]
     weights_k = []

time: 39.2 us -> 38.9 us (level)
  transfers between devices with their start and end apart: 11 -> 11, of which waited for: 5 -> 5; matrix products, arithmetic and copies ran while one was open for 2% -> 2% of each run, Pallas kernels for 14% -> 13%
where the time goes in v6:
time: 38.9 us; the launch traced here: 38.7 us
  starting transfers between devices  15.2 us (39%)
  Pallas kernels  12.6 us (32%)
  waiting for transfers between devices  8.34 us (21%)
  between operations  1.48 us (4%)
  local copies, waits for them, and re-layouts  0.84 us (2%)
    ppermute x9, starting transfers between devices, shifted(): lax.ppermute(value, axis, [(i, (i + steps) % count) for i in range(count)])  11.8 us
    pallas_call x4, Pallas kernels, call(): pl.pallas_call(lambda *refs: kernel(sizes, counts, *refs), out_shape=[jax...  10.2 us
    ppermute x9, waiting for transfers between devices, shifted(): lax.ppermute(value, axis, [(i, (i + steps) % count) for i in range(count)])  4.16 us
    ppermute x1, starting transfers between devices, swapped(): far = lax.ppermute(parts[0], axis, ring)  3.41 us
    ppermute x1, waiting for transfers between devices, swapped(): far = lax.ppermute(parts[0], axis, ring)  3.39 us
    pallas_call x1, Pallas kernels, layer(): pl.pallas_call(pack_kernel, out_shape=jax.ShapeDtypeStruct((1, ROWS, SLOT...  1.65 us
    pallas_call x1, Pallas kernels, layer(): pl.pallas_call(lambda *refs: finish_kernel(len(arrived), *refs), out_shap...  0.84 us
    ppermute x1, waiting for transfers between devices, swapped(): near = lax.ppermute(parts[1], axis, [(i, i ^ 1) for i in range(count)])  0.79 us
  transfers between devices with their start and end apart: 11, of which 5 were waited for; matrix products, arithmetic and copies ran while one was open for 2% of the time, Pallas kernels for 13%

profile of v6, /device:TPU:0, one launch (start us, length us, event | category | flops | bytes accessed | tf_op | source)
XLA Modules:
  0.0 38.7 jit_solution(5035788664223330235)
XLA Ops:
  1.3 1.6 %pack.1 = bf16[1,80,128]{2,1,0:T(8,128)(2,1)} custom-call(s32[1,1,1]{2,1,0:T(1,128)S(6)} %copy.17.counts_ref, bf16[1,1,1,128,256]{4,3,2,1,0:T(8,128)(2,1)} %refs_11_.1, f32[1,1,3,1,128]{4,3,2,1,0:T(1,128)} %bitcast.9, s32[1,1,1,128]{3,2,1,0:T(1,128)} %species_ref.1, bf16[64,256]{1,0:T(8,128)(2,1)} %bitcast.6, s32[1,1,1,27]{3,2,1,0:T(1,128)} %refs_0_.3, ...), custom_call_target="tpu_custom_call" | custom-call | tf_op jit(solution)/shard_map/pack/pallas_call | solution.py:471
  2.9 3.0 %collective-permute-start = (bf16[1,80,128]{2,1,0:T(8,128)(2,1)}, bf16[1,80,128]{2,1,0:T(8,128)(2,1)S(1)}, u32[]{:S(2)}, u32[]{:S(2)}) collective-permute-start(bf16[1,80,128]{2,1,0:T(8,128)(2,1)} %pack.1), channel_id=1, source_target_pairs={{0,1},{1,0},{2,3},{3,2},{4,5},{5,4},{6,7},{7,6},{8,9},{9,8},{10,11... | collective-permute-start | bytes 61448 | tf_op jit(solution)/shard_map/ppermute | solution.py:432
  5.9 0.8 %pad.4 = bf16[1,160,128]{2,1,0:T(8,128)(2,1)S(1)} pad(bf16[1,80,128]{2,1,0:T(8,128)(2,1)} %pack.1, bf16[]{:T(256)} %constant.50.clone.1), padding=0_0x0_80x0_0 | pad | bytes 61442 | tf_op jit(solution)/shard_map/jit(_pad)/pad | solution.py:483
  6.7 1.2 %collective-permute-done = bf16[1,80,128]{2,1,0:T(8,128)(2,1)S(1)} collective-permute-done((bf16[1,80,128]{2,1,0:T(8,128)(2,1)}, bf16[1,80,128]{2,1,0:T(8,128)(2,1)S(1)}, u32[]{:S(2)}, u32[]{:S(2)}) %collective-permute-start) | collective-permute-done | bytes 20512 | tf_op jit(solution)/shard_map/ppermute | solution.py:432
  7.9 0.0 collective-permute-start.5
  7.9 2.0 %collective-permute-start.3 = (bf16[1,160,128]{2,1,0:T(8,128)(2,1)S(1)}, bf16[1,160,128]{2,1,0:T(8,128)(2,1)S(1)}, u32[]{:S(2)}, u32[]{:S(2)}) collective-permute-start(bf16[1,160,128]{2,1,0:T(8,128)(2,1)S(1)} %constant_dynamic-update-slice_fusion.refs_0_), channel_id=1, source_target_pairs={{0,4},{4,8},{8,12},{12,16},{16,20},{20,24},{24,28},{28,0},{1,5},{5... | collective-permute-start | bytes 122888 | tf_op jit(solution)/shard_map/ppermute | solution.py:432
  9.9 3.1 %collective-permute-start.1 = (bf16[1,160,128]{2,1,0:T(8,128)(2,1)S(1)}, bf16[1,160,128]{2,1,0:T(8,128)(2,1)S(1)}, u32[]{:S(2)}, u32[]{:S(2)}) collective-permute-start(bf16[1,160,128]{2,1,0:T(8,128)(2,1)S(1)} %constant_dynamic-update-slice_fusion.refs_0_), channel_id=1, source_target_pairs={{0,28},{4,0},{8,4},{12,8},{16,12},{20,16},{24,20},{28,24},{1,29},{... | collective-permute-start | bytes 122888 | tf_op jit(solution)/shard_map/ppermute | solution.py:432
  13.1 0.1 fusion.refs_10_
  13.2 0.0 copy-start.1
  13.2 0.0 copy-start.2
  13.2 0.0 copy-start.3
  13.2 0.0 copy-start.4
  13.2 0.0 copy-start.5
  13.2 0.0 copy-start.6
  13.2 0.0 copy-start.7
  13.2 0.0 copy-start.8
  13.3 1.9 %collective-permute-done.3.refs_3_ = bf16[1,160,128]{2,1,0:T(8,128)(2,1)S(1)} collective-permute-done((bf16[1,160,128]{2,1,0:T(8,128)(2,1)S(1)}, bf16[1,160,128]{2,1,0:T(8,128)(2,1)S(1)}, u32[]{:S(2)}, u32[]{:S(2)}) %collective-permute-start.3) | collective-permute-done | bytes 40992 | tf_op jit(solution)/shard_map/ppermute | solution.py:432
  15.2 0.0 collective-permute-start.4
  15.2 0.0 collective-permute-done.1.refs_1_
  15.2 0.5 %collective-permute-start.2 = (bf16[1,160,128]{2,1,0:T(8,128)(2,1)S(1)}, bf16[1,160,128]{2,1,0:T(8,128)(2,1)S(1)}, u32[]{:S(2)}, u32[]{:S(2)}) collective-permute-start(bf16[1,160,128]{2,1,0:T(8,128)(2,1)S(1)} %collective-permute-done.1.refs_1_), channel_id=1, source_target_pairs={{0,2},{2,0},{1,3},{3,1},{4,6},{6,4},{5,7},{7,5},{8,10},{10,8},{9,1... | collective-permute-start | bytes 122888 | tf_op jit(solution)/shard_map/ppermute | solution.py:432
  15.7 0.0 collective-permute-done.5.refs_1_
  15.7 2.0 %shard_map.139 = (f32[3,128,128]{2,1,0:T(8,128)S(1)}, f32[128,128]{1,0:T(8,128)S(1)}, bf16[128,128]{1,0:T(8,128)(2,1)S(1)}, f32[4,8,128]{2,1,0:T(8,128)S(1)}, f3...) custom-call(bf16[1,160,128]{2,1,0:T(8,128)(2,1)S(1)} %constant_dynam, ...), custom_call_target="tpu_custom_call" | custom-call | flops 1000000000 | bytes 4000000 | tf_op jit(solution)/shard_map/pallas_call | solution.py:517
  17.7 0.0 collective-permute-done.4.refs_4_
  17.7 0.0 collective-permute-done.2.refs_2_
  17.7 0.0 copy-done.1
  17.7 0.0 copy-done.2
  17.7 0.0 copy-done.3
  17.7 0.0 copy-done.4
  17.8 0.0 copy-done.5
  17.8 0.0 copy-done.6
  17.8 0.0 copy-done.7
  17.8 0.0 copy-done.8
  17.8 4.9 %shard_map.140 = (bf16[512,256]{1,0:T(8,128)(2,1)S(1)}, bf16[256,512]{1,0:T(8,128)(2,1)S(1)}, f32[3,128,128]{2,1,0:T(8,128)S(1)}, bf16[128,256]{1,0:T(8,128)(2,1...) custom-call(s32[1,1,1,27]{3,2,1,0:T(1,128)S(1)} %copy-done.3, ...), custom_call_target="tpu_custom_call" | custom-call | flops 1000000000 | bytes 4000000 | tf_op jit(solution)/shard_map/pallas_call | solution.py:517
  22.7 0.8 %collective-permute-start.7 = (bf16[4,80,128]{2,1,0:T(8,128)(2,1)S(1)}, bf16[4,80,128]{2,1,0:T(8,128)(2,1)S(1)}, u32[]{:S(2)}, u32[]{:S(2)}) collective-permute-start(bf16[4,80,128]{2,1,0:T(8,128)(2,1)S(1)} %get-tuple-element.45), channel_id=1, source_target_pairs={{0,2},{2,0},{1,3},{3,1},{4,6},{6,4},{5,7},{7,5},{8,10},{10,8},{9,1... | collective-permute-start | bytes 245768 | tf_op jit(solution)/shard_map/ppermute | solution.py:432
  23.5 2.5 %shard_map.142 = (f32[2,80,128]{2,1,0:T(8,128)S(1)}, bf16[2,80,128]{2,1,0:T(8,128)(2,1)S(1)}) custom-call(s32[1,1,1,27]{3,2,1,0:T(1,128)S(1)} %copy-done.3, f32[3,128,128]{2,1,0:T(8,128)S(1)} %get-tuple-element.26.refs_13_.refs_1_, f32[4,8,128]{2,1,0:T(8,128)S(1)} %get-tuple-element.33.refs_2_, bf16[5,512,256]{2,1,0:T(8,128)(2,1)S(1)} %get-tuple-element.34.refs_3_, ...), custom_call_target="tpu_custom_call" | custom-call | flops 1000000000 | bytes 4000000 | tf_op jit(solution)/shard_map/pallas_call | solution.py:517
  26.0 0.0 collective-permute-start.6
  26.0 0.0 collective-permute-done.7
  26.1 3.4 %collective-permute-start.8 = (bf16[2,80,128]{2,1,0:T(8,128)(2,1)S(1)}, bf16[2,80,128]{2,1,0:T(8,128)(2,1)S(1)}, u32[]{:S(2)}, u32[]{:S(2)}) collective-permute-start(bf16[2,80,128]{2,1,0:T(8,128)(2,1)S(1)} %get-tuple-element.52), channel_id=1, source_target_pairs={{0,28},{4,8},{8,4},{12,16},{16,12},{20,24},{24,20},{28,0},{1,29},{... | collective-permute-start | bytes 122888 | tf_op jit(solution)/shard_map/ppermute | solution.py:455
  29.5 0.0 collective-permute-start.9
  29.5 0.0 collective-permute-done.6
  29.5 3.4 %collective-permute-done.8 = bf16[2,80,128]{2,1,0:T(8,128)(2,1)S(1)} collective-permute-done((bf16[2,80,128]{2,1,0:T(8,128)(2,1)S(1)}, bf16[2,80,128]{2,1,0:T(8,128)(2,1)S(1)}, u32[]{:S(2)}, u32[]{:S(2)}) %collective-permute-start.8) | collective-permute-done | bytes 40992 | tf_op jit(solution)/shard_map/ppermute | solution.py:455
  32.9 0.8 %collective-permute-done.9 = bf16[2,80,128]{2,1,0:T(8,128)(2,1)S(1)} collective-permute-done((bf16[2,80,128]{2,1,0:T(8,128)(2,1)S(1)}, bf16[2,80,128]{2,1,0:T(8,128)(2,1)S(1)}, u32[]{:S(2)}, u32[]{:S(2)}) %collective-permute-start.9) | collective-permute-done | bytes 40992 | tf_op jit(solution)/shard_map/ppermute | solution.py:456
  33.7 2.4 %collective-permute-start.10 = (bf16[1,80,128]{2,1,0:T(8,128)(2,1)S(1)}, bf16[1,80,128]{2,1,0:T(8,128)(2,1)S(1)}, u32[]{:S(2)}, u32[]{:S(2)}) collective-permute-start(bf16[1,80,128]{2,1,0:T(8,128)(2,1)S(1)} %slice.24), channel_id=1, source_target_pairs={{0,1},{1,0},{2,3},{3,2},{4,5},{5,4},{6,7},{7,6},{8,9},{9,8},{10,11... | collective-permute-start | bytes 61448 | tf_op jit(solution)/shard_map/ppermute | solution.py:432
  36.1 0.0 copy-start
  36.1 0.7 %shard_map.141 = (f32[1,1,1,128]{3,2,1,0:T(1,128)}, f32[128,256]{1,0:T(8,128)S(1)}) custom-call(bf16[128,256]{1,0:T(8,128)(2,1)S(1)} %get-tuple-element.30.refs_0_, f32[128,256]{1,0:T(8,128)S(1)} %get-tuple-element.31.refs_1_, bf16[256,256]{1,0:T(8,128)(2,1)S(1)} %copy-done.4), custom_call_target="tpu_custom_call" | custom-call | flops 1000000000 | bytes 4000000 | tf_op jit(solution)/shard_map/pallas_call | solution.py:517
  36.8 1.0 %collective-permute-done.10.refs_1_ = bf16[1,80,128]{2,1,0:T(8,128)(2,1)S(1)} collective-permute-done((bf16[1,80,128]{2,1,0:T(8,128)(2,1)S(1)}, bf16[1,80,128]{2,1,0:T(8,128)(2,1)S(1)}, u32[]{:S(2)}, u32[]{:S(2)}) %collective-permute-start.10) | collective-permute-done | bytes 20512 | tf_op jit(solution)/shard_map/ppermute | solution.py:432
  37.9 0.0 copy-done
  37.9 0.8 %finish.1 = (f32[1,1,3,1,128]{4,3,2,1,0:T(1,128)}, bf16[1,1,1,128,256]{4,3,2,1,0:T(8,128)(2,1)}) custom-call(f32[1,80,128]{2,1,0:T(8,128)S(1)} %slice.21.refs_0_, bf16[1,80,128]{2,1,0:T(8,128)(2,1)S(1)} %collective-permute-done.10.refs_1_, f32[128,256]{1,0:T(8,128)S(1)} %get-tuple-element.46.refs_2_, bf16[64,256]{1,0:T(8,128)(2,1)S(1)} %bitcast.7), custom_call_target="tpu_custom_call" | custom-call | tf_op jit(solution)/shard_map/finish/pallas_call | solution.py:617
  (7 shorter events, 0.1 us)
Async XLA Ops:
  2.9 5.0 %collective-permute-start = (bf16[1,80,128]{2,1,0:T(8,128)(2,1)}, bf16[1,80,128]{2,1,0:T(8,128)(2,1)S(1)}, u32[]{:S(2)}, u32[]{:S(2)}) collective-permute-start(bf16[1,80,128]{2,1,0:T(8,128)(2,1)} %pack.1), channel_id=1, source_target_pairs={{0,1},{1,0},{2,3},{3,2},{4,5},{5,4},{6,7},{7,6},{8,9},{9,8},{10,11... | collective-permute-start | bytes 61448 | tf_op jit(solution)/shard_map/ppermute | solution.py:432
  7.9 7.8 %collective-permute-start.5 = (bf16[1,160,128]{2,1,0:T(8,128)(2,1)S(1)}, bf16[1,160,128]{2,1,0:T(8,128)(2,1)S(1)}, u32[]{:S(2)}, u32[]{:S(2)}) collective-permute-start(bf16[1,160,128]{2,1,0:T(8,128)(2,1)S(1)} %constant_dynamic-update-slice_fusion.refs_0_), channel_id=1, source_target_pairs={{0,2},{2,0},{1,3},{3,1},{4,6},{6,4},{5,7},{7,5},{8,10},{10,8},{9,1... | collective-permute-start | bytes 122888 | tf_op jit(solution)/shard_map/ppermute | solution.py:432
  7.9 7.3 %collective-permute-start.3 = (bf16[1,160,128]{2,1,0:T(8,128)(2,1)S(1)}, bf16[1,160,128]{2,1,0:T(8,128)(2,1)S(1)}, u32[]{:S(2)}, u32[]{:S(2)}) collective-permute-start(bf16[1,160,128]{2,1,0:T(8,128)(2,1)S(1)} %constant_dynamic-update-slice_fusion.refs_0_), channel_id=1, source_target_pairs={{0,4},{4,8},{8,12},{12,16},{16,20},{20,24},{24,28},{28,0},{1,5},{5... | collective-permute-start | bytes 122888 | tf_op jit(solution)/shard_map/ppermute | solution.py:432
  9.9 5.2 %collective-permute-start.1 = (bf16[1,160,128]{2,1,0:T(8,128)(2,1)S(1)}, bf16[1,160,128]{2,1,0:T(8,128)(2,1)S(1)}, u32[]{:S(2)}, u32[]{:S(2)}) collective-permute-start(bf16[1,160,128]{2,1,0:T(8,128)(2,1)S(1)} %constant_dynamic-update-slice_fusion.refs_0_), channel_id=1, source_target_pairs={{0,28},{4,0},{8,4},{12,8},{16,12},{20,16},{24,20},{28,24},{1,29},{... | collective-permute-start | bytes 122888 | tf_op jit(solution)/shard_map/ppermute | solution.py:432
  13.2 4.6 %copy-start.1 = (bf16[1,1,1,128,256]{4,3,2,1,0:T(8,128)(2,1)S(1)}, bf16[1,1,1,128,256]{4,3,2,1,0:T(8,128)(2,1)}, u32[]{:S(2)}) copy-start(bf16[1,1,1,128,256]{4,3,2,1,0:T(8,128)(2,1)} %refs_11_.1) | copy-start | bytes 196612
  13.2 4.6 %copy-start.2 = (f32[6,6]{1,0:T(8,128)S(1)}, f32[6,6]{1,0:T(8,128)}, u32[]{:S(2)}) copy-start(f32[6,6]{1,0:T(8,128)} %refs_5_.1) | copy-start | bytes 436
  13.2 4.5 %copy-start.3 = (s32[1,1,1,27]{3,2,1,0:T(1,128)S(1)}, s32[1,1,1,27]{3,2,1,0:T(1,128)}, u32[]{:S(2)}) copy-start(s32[1,1,1,27]{3,2,1,0:T(1,128)} %refs_0_.3) | copy-start | bytes 328
  13.2 4.5 %copy-start.4 = (bf16[256,256]{1,0:T(8,128)(2,1)S(1)}, bf16[256,256]{1,0:T(8,128)(2,1)}, u32[]{:S(2)}) copy-start(bf16[256,256]{1,0:T(8,128)(2,1)} %refs_2_.1) | copy-start | bytes 393220
  13.2 4.5 %copy-start.5 = (bf16[64,256]{1,0:T(8,128)(2,1)S(1)}, bf16[64,256]{1,0:T(8,128)(2,1)}, u32[]{:S(2)}) copy-start(bf16[64,256]{1,0:T(8,128)(2,1)} %refs_7_.1) | copy-start | bytes 98308
  13.2 4.5 %copy-start.6 = (bf16[64,256]{1,0:T(8,128)(2,1)S(1)}, bf16[64,256]{1,0:T(8,128)(2,1)}, u32[]{:S(2)}) copy-start(bf16[64,256]{1,0:T(8,128)(2,1)} %refs_8_.1) | copy-start | bytes 98308
  13.2 4.5 %copy-start.7 = (f32[4,64]{1,0:T(4,128)S(1)}, f32[4,64]{1,0:T(4,128)}, u32[]{:S(2)}) copy-start(f32[4,64]{1,0:T(4,128)} %refs_6_.1) | copy-start | bytes 3076
  13.2 4.5 %copy-start.8 = (f32[256]{0:T(256)S(1)}, f32[256]{0:T(256)}, u32[]{:S(2)}) copy-start(f32[256]{0:T(256)} %param.23) | copy-start | bytes 3076
  15.2 2.5 %collective-permute-start.4 = (bf16[1,160,128]{2,1,0:T(8,128)(2,1)S(1)}, bf16[1,160,128]{2,1,0:T(8,128)(2,1)S(1)}, u32[]{:S(2)}, u32[]{:S(2)}) collective-permute-start(bf16[1,160,128]{2,1,0:T(8,128)(2,1)S(1)} %collective-permute-done.3.refs_3_), channel_id=1, source_target_pairs={{0,2},{2,0},{1,3},{3,1},{4,6},{6,4},{5,7},{7,5},{8,10},{10,8},{9,1... | collective-permute-start | bytes 122888 | tf_op jit(solution)/shard_map/ppermute | solution.py:432
  15.2 2.5 %collective-permute-start.2 = (bf16[1,160,128]{2,1,0:T(8,128)(2,1)S(1)}, bf16[1,160,128]{2,1,0:T(8,128)(2,1)S(1)}, u32[]{:S(2)}, u32[]{:S(2)}) collective-permute-start(bf16[1,160,128]{2,1,0:T(8,128)(2,1)S(1)} %collective-permute-done.1.refs_1_), channel_id=1, source_target_pairs={{0,2},{2,0},{1,3},{3,1},{4,6},{6,4},{5,7},{7,5},{8,10},{10,8},{9,1... | collective-permute-start | bytes 122888 | tf_op jit(solution)/shard_map/ppermute | solution.py:432
  22.7 3.3 %collective-permute-start.7 = (bf16[4,80,128]{2,1,0:T(8,128)(2,1)S(1)}, bf16[4,80,128]{2,1,0:T(8,128)(2,1)S(1)}, u32[]{:S(2)}, u32[]{:S(2)}) collective-permute-start(bf16[4,80,128]{2,1,0:T(8,128)(2,1)S(1)} %get-tuple-element.45), channel_id=1, source_target_pairs={{0,2},{2,0},{1,3},{3,1},{4,6},{6,4},{5,7},{7,5},{8,10},{10,8},{9,1... | collective-permute-start | bytes 245768 | tf_op jit(solution)/shard_map/ppermute | solution.py:432
  26.0 3.5 %collective-permute-start.6 = (bf16[2,80,128]{2,1,0:T(8,128)(2,1)S(1)}, bf16[2,80,128]{2,1,0:T(8,128)(2,1)S(1)}, u32[]{:S(2)}, u32[]{:S(2)}) collective-permute-start(bf16[2,80,128]{2,1,0:T(8,128)(2,1)S(1)} %get-tuple-element.43), channel_id=1, source_target_pairs={{0,2},{2,0},{1,3},{3,1},{4,6},{6,4},{5,7},{7,5},{8,10},{10,8},{9,1... | collective-permute-start | bytes 122888 | tf_op jit(solution)/shard_map/ppermute | solution.py:432
  26.1 6.8 %collective-permute-start.8 = (bf16[2,80,128]{2,1,0:T(8,128)(2,1)S(1)}, bf16[2,80,128]{2,1,0:T(8,128)(2,1)S(1)}, u32[]{:S(2)}, u32[]{:S(2)}) collective-permute-start(bf16[2,80,128]{2,1,0:T(8,128)(2,1)S(1)} %get-tuple-element.52), channel_id=1, source_target_pairs={{0,28},{4,8},{8,4},{12,16},{16,12},{20,24},{24,20},{28,0},{1,29},{... | collective-permute-start | bytes 122888 | tf_op jit(solution)/shard_map/ppermute | solution.py:455
  29.5 4.2 %collective-permute-start.9 = (bf16[2,80,128]{2,1,0:T(8,128)(2,1)S(1)}, bf16[2,80,128]{2,1,0:T(8,128)(2,1)S(1)}, u32[]{:S(2)}, u32[]{:S(2)}) collective-permute-start(bf16[2,80,128]{2,1,0:T(8,128)(2,1)S(1)} %get-tuple-element.53), channel_id=1, source_target_pairs={{0,4},{4,0},{8,12},{12,8},{16,20},{20,16},{24,28},{28,24},{1,5},{5... | collective-permute-start | bytes 122888 | tf_op jit(solution)/shard_map/ppermute | solution.py:456
  33.7 4.1 %collective-permute-start.10 = (bf16[1,80,128]{2,1,0:T(8,128)(2,1)S(1)}, bf16[1,80,128]{2,1,0:T(8,128)(2,1)S(1)}, u32[]{:S(2)}, u32[]{:S(2)}) collective-permute-start(bf16[1,80,128]{2,1,0:T(8,128)(2,1)S(1)} %slice.24), channel_id=1, source_target_pairs={{0,1},{1,0},{2,3},{3,2},{4,5},{5,4},{6,7},{7,6},{8,9},{9,8},{10,11... | collective-permute-start | bytes 61448 | tf_op jit(solution)/shard_map/ppermute | solution.py:432
  36.1 1.8 %copy-start = (bf16[256,64]{0,1:T(8,128)(2,1)S(1)}, bf16[256,64]{0,1:T(8,128)(2,1)}, u32[]{:S(2)}) copy-start(bf16[256,64]{0,1:T(8,128)(2,1)} %param.17) | copy-start | bytes 98308
